TPU v7x, 512 devices: a whole 4x8x8 slice. The times are simulated.
512 devices in a mesh: gx: 4 (over x), gy: 8 (over y), gz: 16 (over z, core).
Axes of the slice: x: 4, y: 8, z: 8, core: 2. Of those that a mesh axis runs over, the one named last changes fastest.
Arguments:
- source: float32 [32, 128, 2048], P('gx', 'gy', 'gz'), may hold values from -6 to 6
- state: float32 [32, 128, 2048], P('gx', 'gy', 'gz'), may hold values from -6 to 6
- log_coef: float32 [32, 128, 2048], P('gx', 'gy', 'gz'), may hold values from -1 to 1
- lateral: float32 [32, 128], P('gx', 'gy'), may hold values from -0.5 to 0.5
- owners: int32 [4, 8, 16], P('gx', 'gy'), may hold values from 0 to 15, as said below
Outputs:
- adjoint_field: float32 [32, 128, 2048], P('gx', 'gy', 'gz')
- lateral_gradient: float32 [32, 128], P('gx', ('gy', 'gz'))
Inputs may be any that keep to these rules, and one draw needn't show every extreme that they name: Along each line, the devices with equal owners entries form a contiguous run of at most 4 devices, and every line has a run of exactly 4; the entry names the device that solves that run's level-2 system, which need not belong to the run; different runs of a line name different devices.
All inputs are finite; a program needn't handle non-finite values.
Results may differ from a plain program's by a relative error of at most 0.0003.
Values sent between devices are 32-bit elements; how exact they have to be, the bound alone decides.
No kernel may reach another device: no remote copies, remote signals or barrier semaphores. Data moves between devices by JAX's collectives and lax.ppermute only.
A program may use at most 64 MiB of HBM per device.

v0:
```python
import math

import jax
import jax.numpy as jnp
from jax import lax
from jax.sharding import PartitionSpec as P

SWEEPS = 3
ANISO = 200


omega_relax = 0.8
neighbour_offsets = ((2, 1, 1), (0, 1, 1), (1, 2, 1), (1, 0, 1), (1, 1, 2), (1, 1, 0))


def padded_2(value, sides, width):
    for axis, dim in sides:
        count, length = (lax.axis_size(axis), value.shape[dim])
        up = [(i, (i + 1) % count) for i in range(count - 1)]
        down = [(j, i) for i, j in up]
        last = lax.slice_in_dim(value, length - width, length, axis=dim)
        first = lax.slice_in_dim(value, 0, width, axis=dim)
        before = lax.ppermute(last, axis, up)
        after = lax.ppermute(first, axis, down)
        value = jnp.concatenate([before, value, after], axis=dim)
    return value


def neighbour(padded, offset, shape):
    return padded[
        offset[0] : offset[0] + shape[0],
        offset[1] : offset[1] + shape[1],
        offset[2] : offset[2] + shape[2],
    ]


def face_scale(scale, order_index):
    if order_index >= 4:
        return scale * ANISO
    return scale


def halo_fine(field):
    return padded_2(field, (("gx", 0), ("gy", 1), ("gz", 2)), 1)


def halo_mid(field):
    return padded_2(field, (("gx", 0), ("gy", 1), ("gz", 2)), 1)


def level_weights(padded, coef, scale):
    weights = []
    for order_index, offset in enumerate(neighbour_offsets):
        raw = neighbour(padded, offset, coef.shape)
        fixed = jnp.where(raw == 0.0, coef, raw)
        weights.append(face_scale(scale, order_index) * (0.5 * (coef + fixed)))
    total = weights[0]
    for extra in weights[1:]:
        total = total + extra
    return (weights, total)


def operate(padded, field, weights, total):
    result = total * field
    for order_index, offset in enumerate(neighbour_offsets):
        result = result - weights[order_index] * neighbour(padded, offset, field.shape)
    return result


def smooth(field, rhs, weights, total, halo_step, from_zero):
    remaining = SWEEPS
    if from_zero:
        field = omega_relax * rhs / total
        remaining = SWEEPS - 1
    for repeat in range(remaining):
        padded = halo_step(field)
        field = field + omega_relax * (rhs - operate(padded, field, weights, total)) / total
    return field


def restrict(field):
    shape = field.shape
    return field.reshape(shape[0] // 2, 2, shape[1] // 2, 2, shape[2] // 2, 2).mean(axis=(1, 3, 5))


def prolong(field):
    shape = field.shape
    spread = jnp.broadcast_to(
        field[:, None, :, None, :, None], (shape[0], 2, shape[1], 2, shape[2], 2)
    )
    return spread.reshape(2 * shape[0], 2 * shape[1], 2 * shape[2])


def line_solve(rhs, total, lower):
    upper = jnp.concatenate([lower[..., 1:], jnp.zeros_like(lower[..., :1])], axis=-1)
    solved = lax.linalg.tridiagonal_solve(-lower, total, -upper, rhs[..., None])
    return solved[..., 0]


def per_device(source, state, log_coef, lateral, owners):
    coef = jnp.exp(log_coef + lateral[:, :, None])
    mid_coef = restrict(coef)
    low_coef = restrict(mid_coef)
    low_pad = padded_2(low_coef, (("gx", 0), ("gy", 1), ("gz", 2)), 1)
    low_weights, low_total = level_weights(low_pad, low_coef, 0.0625)
    coef_pad = halo_fine(coef)
    fine_weights, fine_total = level_weights(coef_pad, coef, 1.0)
    mid_weights, mid_total = level_weights(halo_mid(mid_coef), mid_coef, 0.25)
    adjoint = smooth(jnp.zeros_like(source), source, fine_weights, fine_total, halo_fine, True)
    mid_rhs = restrict(source - operate(halo_fine(adjoint), adjoint, fine_weights, fine_total))
    mid_field = smooth(jnp.zeros_like(mid_rhs), mid_rhs, mid_weights, mid_total, halo_mid, True)
    low_rhs = restrict(mid_rhs - operate(halo_mid(mid_field), mid_field, mid_weights, mid_total))
    position = lax.axis_index("gz")
    count = lax.axis_size("gz")
    depth_len = low_coef.shape[2]
    line = owners[0, 0]
    own_group = line[position]
    prev_group = line[jnp.maximum(position - 1, 0)]
    cut_first = (position == 0) | (own_group != prev_group)
    depth_first = (jnp.arange(depth_len) == 0)[None, None, :]
    lower = jnp.where(cut_first & depth_first, jnp.zeros_like(low_weights[5]), low_weights[5])
    slots = jnp.arange(count)
    target = (slots == own_group).astype(jnp.float32)
    member = (line == position).astype(jnp.float32)
    piece = jnp.stack([low_rhs, low_total, lower])
    outgoing = piece[:, :, :, None, :] * target[None, None, None, :, None]
    received = lax.all_to_all(outgoing, "gz", split_axis=3, concat_axis=3, tiled=True)
    flat = (received.shape[1], received.shape[2], count * received.shape[4])
    diag_flat = (received[1] + (1.0 - member)[None, None, :, None]).reshape(flat)
    solution = line_solve(received[0].reshape(flat), diag_flat, received[2].reshape(flat))
    returned = lax.all_to_all(
        solution.reshape(received.shape[1:]), "gz", split_axis=2, concat_axis=2, tiled=True
    )
    correction = jnp.sum(returned, axis=2)
    mid_field = smooth(
        mid_field + prolong(correction), mid_rhs, mid_weights, mid_total, halo_mid, False
    )
    adjoint = smooth(
        adjoint + prolong(mid_field), source, fine_weights, fine_total, halo_fine, False
    )
    paired = padded_2(jnp.stack([adjoint, state]), (("gx", 1), ("gy", 2), ("gz", 3)), 1)
    adjoint_pad, state_pad = (paired[0], paired[1])
    grad_terms = jnp.zeros_like(adjoint)
    for offset in neighbour_offsets:
        raw = neighbour(coef_pad, offset, coef.shape)
        factor = jnp.where(raw == 0.0, 1.0, 0.5)
        grad_terms = grad_terms + factor * (
            adjoint - neighbour(adjoint_pad, offset, adjoint.shape)
        ) * (state - neighbour(state_pad, offset, state.shape))
    partial_sums = jnp.sum(coef * grad_terms, axis=2)
    summed = lax.psum_scatter(partial_sums, "gz", scatter_dimension=1, tiled=True)
    return (adjoint, summed * (-1.0 / math.sqrt(source.shape[2] * count)))


def solution(mesh):
    placed = (
        P("gx", "gy", "gz"),
        P("gx", "gy", "gz"),
        P("gx", "gy", "gz"),
        P("gx", "gy"),
        P("gx", "gy", None),
    )
    return jax.shard_map(
        per_device,
        mesh=mesh,
        in_specs=placed,
        out_specs=(P("gx", "gy", "gz"), P("gx", ("gy", "gz"))),
        check_vma=False,
    )
```

profile of v0, /device:TPU:286, one launch (start us, length us, event | category | flops | bytes accessed | tf_op | source)
XLA Modules:
  0.0 1755.5 jit_solution(12068976091215473077)
XLA Ops:
  1.6 2.7 collective-permute-start
  5.7 4.2 collective-permute-done.1
  12.2 4.7 collective-permute-start.3
  22.7 5.0 collective-permute-done.5
  32.6 4.2 collective-permute-done.7
  38.7 5.4 collective-permute-start.9
  47.5 2.5 collective-permute-start.11
  50.0 5.5 reshape.511
  55.5 2.5 reduce_sum.55
  62.1 4.2 collective-permute-done.13
  68.3 5.4 collective-permute-start.15
  77.7 2.7 collective-permute-start.16
  82.8 5.0 collective-permute-done.17
  88.0 4.3 collective-permute-start.18
  95.5 5.1 collective-permute-start.27
  102.6 5.1 collective-permute-start.21
  113.6 4.4 collective-permute-start.28
  120.1 5.5 reshape.510
  125.6 2.5 reduce_sum.54
  128.3 4.5 collective-permute-start.30
  134.2 4.5 collective-permute-start.48
  142.6 5.4 collective-permute-start.33
  150.1 3.7 collective-permute-start.34
  155.8 4.7 collective-permute-done.35
  160.5 4.3 collective-permute-start.36
  166.2 4.2 collective-permute-done.37
  172.2 5.1 collective-permute-start.39
  177.4 2.6 collective-permute-start.51
  180.0 3.2 collective-permute-start.50
  187.8 4.2 collective-permute-done.41
  202.0 5.1 collective-permute-start.45
  208.5 3.2 collective-permute-start.46
  213.7 4.7 collective-permute-done.47
  220.0 7.2 all-to-all-start
  227.4 2.6 all-to-all-done
  237.6 1216.4 %while.32 = (s32[]{:T(128)}, f32[2,4]{1,0:T(2,128)S(1)}, f32[2,4,1]{1,0,2:T(2,128)}, f32[15,32,2,4]{1,0,3,2:T(8,128)}, f32[15,32,2,4,1]{1,0,3,2,4:T(8,128)}, /*i...) while((s32[]{:T(128)}, f32[2,4]{1,0:T(2,128)S(1)}, ...), condition=%wide.region_5.6_spmd, body=%wide.region_4.5_spmd.sunk | while | flops 1585 | bytes 19841 | solution.py:96
  1466.0 53.7 %while.33 = (s32[]{:T(128)}, f32[2,4,1]{1,0,2:T(2,128)S(1)}, f32[15,32,2,4,1]{1,0,3,2,4:T(8,128)S(1)}, f32[15,32,2,4,1]{3,2,4,1,0:T(2,128)S(1)}, f32[15,32,2,4]{...) while((s32[]{:T(128)}, f32[2,4,1]{1,0,2:T(2,128)S(1)}, ...), condition=%wide.region_7.8_spmd, body=%wide.region_6.7_spmd.sunk | while | flops 546 | bytes 10161 | solution.py:96
  1523.7 9.9 all_to_all.10
  1534.9 4.5 collective-permute-start.54
  1540.7 4.2 collective-permute-done.55
  1546.8 5.1 collective-permute-start.57
  1557.7 4.2 collective-permute-done.59
  1565.6 4.2 collective-permute-done.61
  1571.7 5.4 collective-permute-start.63
  1582.8 4.2 collective-permute-done.65
  1590.4 4.2 collective-permute-done.67
  1596.6 5.4 collective-permute-start.69
  1605.3 2.6 collective-permute-start.71
  1607.9 4.0 collective-permute-done.71
  1614.5 4.0 reshape.523
  1621.9 4.2 collective-permute-done.73
  1628.1 5.5 collective-permute-start.75
  1639.4 5.0 collective-permute-done.77
  1647.8 4.2 collective-permute-done.79
  1654.0 5.4 collective-permute-start.81
  1665.2 5.0 collective-permute-done.83
  1673.6 4.2 collective-permute-done.85
  1679.7 5.4 collective-permute-start.87
  1690.9 5.0 collective-permute-done.89
  1697.4 4.5 collective-permute-start.91
  1703.4 5.4 collective-permute-start.92
  1710.8 4.8 collective-permute-done.93
  1717.7 4.9 collective-permute-start.95
  1727.1 27.2 %all-reduce.1 = f32[8,16]{0,1:T(8,128)S(1)} all-reduce(f32[8,16]{0,1:T(8,128)S(1)} %copy.1047), channel_id=2, replica_groups=mesh['gx'=4,'gy'=8,'gz'=16] {'gz'}, use_global_device_ids=true, to_apply=%region_10.11.clone | all-reduce | flops 128 | bytes 1024
  (2087 shorter events, 1447.2 us)
Async XLA Ops:
  9.9 7.1 collective-permute-start.2
  12.2 6.0 collective-permute-start.3
  20.3 7.4 collective-permute-start.5
  36.8 7.3 collective-permute-start.8
  38.7 6.7 collective-permute-start.9
  45.6 12.6 collective-permute-start.10
  47.5 10.6 collective-permute-start.11
  66.3 11.2 collective-permute-start.14
  68.3 9.3 collective-permute-start.15
  73.7 19.9 %collective-permute-start.24 = (f32[1,8,64]{2,1,0:T(8,128)S(1)}, f32[1,8,64]{2,1,0:T(8,128)S(1)}, u32[]{:S(2)}, u32[]{:S(2)}) collective-permute-start(f32[1,8,64]{2,1,0:T(8,128)S(1)} %get-tuple-element.608), channel_id=1, source_target_pairs={{128,0},{256,128},{384,256},{129,1},{257,129},{385,257},{130,2},{2... | collective-permute-start | bytes 6152 | tf_op jit(solution)/shard_map/ppermute | solution.py:24
  75.6 18.0 %collective-permute-start.25 = (f32[1,8,64]{2,1,0:T(8,128)S(1)}, f32[1,8,64]{2,1,0:T(8,128)S(1)}, u32[]{:S(2)}, u32[]{:S(2)}) collective-permute-start(f32[1,8,64]{2,1,0:T(8,128)S(1)} %get-tuple-element.607), channel_id=1, source_target_pairs={{0,128},{128,256},{256,384},{1,129},{129,257},{257,385},{2,130},{1... | collective-permute-start | bytes 6152 | tf_op jit(solution)/shard_map/ppermute | solution.py:23
  80.4 7.4 collective-permute-start.17
  88.0 12.7 collective-permute-start.18
  92.2 8.4 collective-permute-start.19
  93.6 14.2 collective-permute-start.26
  95.5 12.3 collective-permute-start.27
  100.7 7.1 collective-permute-start.20
  102.6 6.5 collective-permute-start.21
  109.2 10.7 collective-permute-start.22
  111.1 8.8 collective-permute-start.23
  113.6 14.5 collective-permute-start.28
  118.0 10.2 collective-permute-start.29
  128.3 12.3 collective-permute-start.30
  132.9 7.8 collective-permute-start.31
  134.2 31.9 %collective-permute-start.48 = (f32[1,4,32]{2,1,0:T(4,128)S(1)}, f32[1,4,32]{2,1,0:T(4,128)S(1)}, u32[]{:S(2)}, u32[]{:S(2)}) collective-permute-start(f32[1,4,32]{2,1,0:T(4,128)S(1)} %get-tuple-element.618), channel_id=1, source_target_pairs={{128,0},{256,128},{384,256},{129,1},{257,129},{385,257},{130,2},{2... | collective-permute-start | bytes 1544 | tf_op jit(solution)/shard_map/ppermute | solution.py:24
  138.7 27.4 %collective-permute-start.49 = (f32[1,4,32]{2,1,0:T(4,128)S(1)}, f32[1,4,32]{2,1,0:T(4,128)S(1)}, u32[]{:S(2)}, u32[]{:S(2)}) collective-permute-start(f32[1,4,32]{2,1,0:T(4,128)S(1)} %get-tuple-element.617), channel_id=1, source_target_pairs={{0,128},{128,256},{256,384},{1,129},{129,257},{257,385},{2,130},{1... | collective-permute-start | bytes 1544 | tf_op jit(solution)/shard_map/ppermute | solution.py:23
  140.6 9.3 collective-permute-start.32
  142.6 7.4 collective-permute-start.33
  153.8 6.6 collective-permute-start.35
  170.3 13.0 collective-permute-start.38
  172.2 11.0 collective-permute-start.39
  177.4 10.3 collective-permute-start.51
  180.0 7.7 collective-permute-start.50
  185.3 6.6 collective-permute-start.41
  192.1 7.9 collective-permute-start.42
  195.7 11.4 collective-permute-start.52
  197.6 9.5 collective-permute-start.53
  200.0 7.2 collective-permute-start.44
  202.0 6.4 collective-permute-start.45
  211.7 6.6 collective-permute-start.47
  220.0 10.0 all-to-all-start
  1544.9 7.1 collective-permute-start.56
  1546.8 6.4 collective-permute-start.57
  1555.3 6.6 collective-permute-start.59
  1569.8 7.3 collective-permute-start.62
  1571.7 6.7 collective-permute-start.63
  1580.4 6.6 collective-permute-start.65
  1594.6 7.3 collective-permute-start.68
  1596.6 6.7 collective-permute-start.69
  1605.3 6.6 collective-permute-start.71
  1626.1 7.5 collective-permute-start.74
  1628.1 6.9 collective-permute-start.75
  1637.0 7.4 collective-permute-start.77
  1652.0 7.3 collective-permute-start.80
  1654.0 6.7 collective-permute-start.81
  1662.7 7.4 collective-permute-start.83
  1677.8 7.3 collective-permute-start.86
  1679.7 6.7 collective-permute-start.87
  1688.5 7.4 collective-permute-start.89
  1697.4 6.0 collective-permute-start.91
  1703.4 7.3 collective-permute-start.92
  1708.8 6.8 collective-permute-start.93
  1715.8 8.7 collective-permute-start.94
  1717.7 8.6 collective-permute-start.95
  (75 other events, 1106.8 us)
where the time goes:
time: 1780 us; the launch traced here: 1760 us
  local copies, waits for them, and re-layouts  1270 us (71%)
  starting transfers between devices  267 us (15%)
  waiting for transfers between devices  118 us (7%)
  other arithmetic  56.5 us (3%)
  blocking collectives  37.1 us (2%)
    broadcast_in_dim x1534, local copies, waits for them, and re-layouts, line_solve(): solved = lax.linalg.tridiagonal_solve(-lower, total, -upper, rhs[..., None])  1140 us
    ppermute x48, starting transfers between devices, padded_2(): before = lax.ppermute(last, axis, up)  139 us
    ppermute x48, starting transfers between devices, padded_2(): after = lax.ppermute(first, axis, down)  121 us
    ppermute x48, waiting for transfers between devices, padded_2(): before = lax.ppermute(last, axis, up)  106 us
    concatenate x48, local copies, waits for them, and re-layouts, line_solve(): solved = lax.linalg.tridiagonal_solve(-lower, total, -upper, rhs[..., None])  48.7 us
    dynamic_update_slice x45, local copies, waits for them, and re-layouts, line_solve(): solved = lax.linalg.tridiagonal_solve(-lower, total, -upper, rhs[..., None])  42.2 us
    div x32, other arithmetic, line_solve(): solved = lax.linalg.tridiagonal_solve(-lower, total, -upper, rhs[..., None])  38.4 us
  transfers between devices with their start and end apart: 97, of which 37 were waited for; matrix products, arithmetic and copies ran while one was open for 1% of the time, Pallas kernels for 0%

commit v1 on v0

v1 whole, which is shorter than its diff:
```python
import math

import jax
import jax.numpy as jnp
from jax import lax
from jax.experimental import pallas as pl
from jax.experimental.pallas import tpu as pltpu
from jax.sharding import PartitionSpec as P

CX, CY, CZ = 8, 16, 128
ANISO = 200.0
OMEGA = 0.8
HY = 12
HZ = 18
YE = CY + 2 * HY
ZE = 2 * CZ
YM = 24
ZM = CZ
XW = CX + 8
YW = CY + 8
HIGHEST = lax.Precision.HIGHEST


def iota(shape, dim):
    return lax.broadcasted_iota(jnp.int32, shape, dim)


def mm(a, b):
    return jnp.dot(a, b, precision=HIGHEST, preferred_element_type=jnp.float32)


def nxt(v, axis):
    return pltpu.roll(v, v.shape[axis] - 1, axis)


def prv(v, axis):
    return pltpu.roll(v, 1, axis)


def face(a, b):
    both = a + b
    return jnp.where(jnp.minimum(a, b) == 0.0, both, 0.5 * both)


def make_weights(c, wx, wy, wz, inv, planes, scale):
    wx[0] = scale * face(c[0], c[1])

    def step(x, carry):
        here = c[x + 1]
        fx = scale * face(here, c[x + 2])
        fy = scale * face(here, nxt(here, 0))
        fz = (scale * ANISO) * face(here, nxt(here, 1))
        wx[x + 1] = fx
        wy[x] = fy
        wz[x] = fz
        total = fx + wx[x] + fy + prv(fy, 0) + fz + prv(fz, 1)
        inv[x] = jnp.where(here > 0.0, OMEGA / total, 0.0)
        return carry

    lax.fori_loop(0, planes, step, 0)


def residual(v, b, wx, wy, wz, x, before):
    here = v[x + 1]
    fx = wx[x + 1] * (here - v[x + 2])
    fy = wy[x] * (here - nxt(here, 0))
    fz = wz[x] * (here - nxt(here, 1))
    flow = (fx - before) + (fy - prv(fy, 0)) + (fz - prv(fz, 1))
    return here, b[x] - flow, fx


def sweep(v, out, b, wx, wy, wz, inv, planes):
    def step(x, before):
        here, rest, fx = residual(v, b, wx, wy, wz, x, before)
        out[x + 1] = here + inv[x] * rest
        return fx

    lax.fori_loop(0, planes, step, wx[0] * (0.0 - v[1]))


def pack_z_kernel(line, src, c, state, down, up):
    gz = lax.axis_index("gz")
    cut = (line[gz] != line[jnp.minimum(gz + 1, 15)]).astype(jnp.float32)
    lane = iota((CX, CY, CZ), 2)
    s, k = src[...], pltpu.roll(c[...], 64, 2)
    t = pltpu.roll(state[...], 32, 2)
    zero = jnp.zeros_like(s)
    far = CZ - HZ
    coef = jnp.where((lane >= 64) & (lane < 64 + HZ), k, zero)
    down[...] = jnp.where(lane < HZ, s, jnp.where(lane == 32, t, coef))
    coef = jnp.where((lane >= far - 64) & (lane < 64), k, zero)
    coef = jnp.where(lane == 20, cut, coef)
    up[...] = jnp.where(lane >= far, s, jnp.where(lane == 31, t, coef))


def pack_y_kernel(g, state, up, down):
    row = iota((24, CZ), 0)

    def put(at, one, two):
        zero = jnp.zeros((8, CZ), jnp.float32)
        one = jnp.concatenate([one, zero], 0)
        two = jnp.concatenate([two, zero], 0)
        up[at] = jnp.where(row < HY, pltpu.roll(one, 20, 0), pltpu.roll(two, 8, 0))
        down[at] = jnp.where(row < HY, one, pltpu.roll(two, 12, 0))

    for s in range(4):
        for k in range(12):
            put(12 * s + k, g[s, 2 * k], g[s, 2 * k + 1])
    for k in range(4):
        put(48 + k, state[2 * k], state[2 * k + 1])


def rows_of(yp, own, yn, odd):
    row = iota((YE, CZ), 0)
    zero16 = jnp.zeros((16, CZ), jnp.float32)
    zero24 = jnp.zeros((24, CZ), jnp.float32)
    low = jnp.concatenate([yp, zero16], 0)
    high = jnp.concatenate([yn, zero16], 0)
    mid = pltpu.roll(jnp.concatenate([own, zero24], 0), HY, 0)
    if odd:
        low = pltpu.roll(low, YE - HY, 0)
        high = pltpu.roll(high, HY + CY - HY, 0)
    else:
        high = pltpu.roll(high, HY + CY, 0)
    return jnp.where(row < HY, low, jnp.where(row < HY + CY, mid, high))


def first_kernel(
    g, yp, yn, state,
    src_w, pre_w, c_w, se, mid_pre_o, mid_rhs_o, mid_c_o, low_o,
    c, wx, wy, wz, inv, b, va, vb, t, mc, mwx, mwy, mwz, minv, mb, mva, mvb, lc,
):
    gx, gz = lax.axis_index("gx"), lax.axis_index("gz")
    zero = jnp.zeros((YE, ZE), jnp.float32)
    nx = 4 * CX
    for ref in (c, va, vb):
        ref[0] = zero
        ref[nx + 1] = zero
    lane = iota((YE, CZ), 1)
    edge = (lane < HZ) | (lane >= CZ - HZ)

    for s in range(4):
        for i in range(0, CX, 2):
            for odd in (0, 1):
                x = CX * s + i + odd
                near = [
                    rows_of(yp[12 * s + (a * CX + i) // 2], g[s, a * CX + i + odd],
                            yn[12 * s + (a * CX + i) // 2], odd)
                    for a in range(3)
                ]
                halo = near[2]
                b[x] = jnp.concatenate([near[0], jnp.where(edge, halo, 0.0)], 1)
                other = pltpu.roll(halo, 64, 1)
                c[x + 1] = jnp.concatenate([near[1], jnp.where(edge, other, 0.0)], 1)

    make_weights(c, wx, wy, wz, inv, nx, 1.0)

    def start(x, carry):
        va[x + 1] = inv[x] * b[x]
        return carry

    lax.fori_loop(0, nx, start, 0)
    sweep(va, vb, b, wx, wy, wz, inv, nx)
    sweep(vb, va, b, wx, wy, wz, inv, nx)

    fold_y = (iota((YM, YE), 1) // 2 + 2 == iota((YM, YE), 0)).astype(jnp.float32)
    fold_z = (iota((ZE, ZM), 0) // 2 == iota((ZE, ZM), 1)).astype(jnp.float32) * 0.125

    def coarse(m, before):
        x = 2 * m
        _, one, fx = residual(va, b, wx, wy, wz, x, before)
        _, two, fx = residual(va, b, wx, wy, wz, x + 1, fx)
        t[m] = mm(fold_y, one + two)
        t[m + 16] = mm(fold_y, c[x + 1] + c[x + 2])
        return fx

    lax.fori_loop(0, 16, coarse, wx[0] * (0.0 - va[1]))
    both = mm(t[...].reshape(32 * YM, ZE), fold_z).reshape(32, YM, ZM)
    mb[...] = both[:16]
    mid_rhs_o[...] = both[:16]
    mid_zero = jnp.zeros((YM, ZM), jnp.float32)
    for ref in (mc, mva, mvb):
        ref[0] = mid_zero
        ref[17] = mid_zero
    mc[1:17] = both[16:]
    mid_c_o[...] = both[16:]

    def keep(w, carry):
        x = CX * gx - 4 + w
        inside = (x >= 0) & (x < nx)
        x = jnp.clip(x, 0, nx - 1)
        src_w[w] = jnp.where(inside, b[x, 8:32], 0.0)
        pre_w[w] = jnp.where(inside, va[x + 1, 8:32], 0.0)
        c_w[w] = jnp.where(inside, c[x + 1, 8:32], 0.0)
        return carry

    lax.fori_loop(0, XW, keep, 0)

    zero8 = jnp.zeros((8, CZ), jnp.float32)
    wide = jnp.zeros((YW, CZ), jnp.float32)
    row = iota((YW, CZ), 0)
    lane = iota((YW, CZ), 1)
    left = g[jnp.maximum(gx - 1, 0), 25]
    right = g[jnp.minimum(gx + 1, 3), 24]
    left = jnp.where(gx > 0, left, 0.0)
    right = jnp.where(gx < 3, right, 0.0)
    for at, plane in ((0, left), (9, right)):
        mid = pltpu.roll(jnp.concatenate([plane, zero8], 0), 4, 0)
        se[at] = jnp.concatenate([mid, wide], 1)
    for i in range(CX):
        mid = pltpu.roll(jnp.concatenate([state[i], zero8], 0), 4, 0)
        low, high = yp[48 + i // 2], yn[48 + i // 2]
        low = pltpu.roll(low, (3 - 11 - 12 * (i % 2)) % 24, 0)
        high = pltpu.roll(high, (20 - 12 * (i % 2)) % 24, 0)
        mid = jnp.where(row == 3, low, jnp.where(row == 20, high, mid))
        halo = pltpu.roll(jnp.concatenate([g[gx, 16 + i], zero8], 0), 4, 0)
        halo = pltpu.roll(halo, CZ - 32, 1)
        halo = jnp.where((lane == 0) | (lane == CZ - 1), halo, 0.0)
        se[i + 1] = jnp.concatenate([mid, halo], 1)

    make_weights(mc, mwx, mwy, mwz, minv, 16, 0.25)
    mva[1:17] = minv[...] * mb[...]
    sweep(mva, mvb, mb, mwx, mwy, mwz, minv, 16)
    sweep(mvb, mva, mb, mwx, mwy, mwz, minv, 16)

    def rest(x, before):
        _, r, fx = residual(mva, mb, mwx, mwy, mwz, x, before)
        mvb[x + 1] = r
        mid_pre_o[x] = mva[x + 1, 8:16]
        return fx

    lax.fori_loop(0, 16, rest, mwx[0] * (0.0 - mva[1]))

    shape = (64, 16 * YM)
    to, frm = iota(shape, 0), iota(shape, 1)
    m, r = frm // YM, frm % YM
    fold = ((m // 2 == to // 8) & (r // 2 - 2 == to % 8)).astype(jnp.float32) * 0.125
    m, l = iota((ZM, CZ), 0), iota((ZM, CZ), 1)
    m = jnp.where(m < 96, m, m - 128)
    squeeze = ((m + 8) // 2 == l).astype(jnp.float32)
    rhs = mm(mm(fold, mvb[1:17].reshape(16 * YM, ZM)), squeeze).reshape(8, 8, CZ)
    low_c = mm(mm(fold, mc[1:17].reshape(16 * YM, ZM)), squeeze).reshape(8, 8, CZ)
    lc[0] = jnp.zeros((8, CZ), jnp.float32)
    lc[9] = jnp.zeros((8, CZ), jnp.float32)
    lc[1:9] = low_c
    scale = 0.0625
    fx0 = scale * face(lc[0:8], low_c)
    fx1 = scale * face(low_c, lc[2:10])
    fy = scale * face(low_c, nxt(low_c, 1))
    fz = (scale * ANISO) * face(low_c, nxt(low_c, 2))
    lower = prv(fz, 2)
    total = fx1 + fx0 + fy + prv(fy, 1) + fz + lower
    flags = [pltpu.roll(g[s, 16, 0:8], CZ - 16, 1) for s in range(4)]
    flags = jnp.stack([flags[x // 2] for x in range(8)])
    lane = iota((8, 8, CZ), 2)
    lower = jnp.where((lane == 4) & ((flags > 0.0) | (gz == 0)), 0.0, lower)
    packed = jnp.where(
        lane < 32, pltpu.roll(rhs, CZ - 4, 2),
        jnp.where(lane < 64, pltpu.roll(total, 28, 2), pltpu.roll(lower, 60, 2)),
    )
    packed = jnp.where(lane < 96, packed, 0.0).reshape(64, CZ)
    to, frm = iota((32, 64), 0), iota((32, 64), 1)
    pick = ((to // 4 == frm // 8) & (to % 4 + 2 == frm % 8)).astype(jnp.float32)
    packed = mm(pick, packed)
    for p in range(16):
        low_o[p] = packed


def solve_kernel(rec, mid_pre, out):
    gz = lax.axis_index("gz")
    lane = iota((32, CZ), 1)
    parts = [[], [], []]
    for tile in range(4):
        pieces = [jnp.zeros((32, CZ), jnp.float32)] * 3
        for j in range(4):
            block = rec[4 * tile + j]
            here = (lane >= 32 * j) & (lane < 32 * j + 32)
            for a in range(3):
                shift = (32 * (j - a)) % CZ
                moved = pltpu.roll(block, shift, 1) if shift else block
                pieces[a] = jnp.where(here, moved, pieces[a])
        for a in range(3):
            parts[a].append(pieces[a])
    r, d, e = [jnp.concatenate(p, 1) for p in parts]
    for k in range(7):
        s = 1 << k
        back = 4 * CZ - s
        inv = 1.0 / d
        t = e * inv
        alpha = e * pltpu.roll(inv, s, 1)
        d = d - alpha * e - pltpu.roll(t * e, back, 1)
        r = r + alpha * pltpu.roll(r, s, 1) + pltpu.roll(t * r, back, 1)
        e = alpha * pltpu.roll(e, s, 1)
    x = r / d
    k, m = iota((4 * CZ, ZM), 0), iota((4 * CZ, ZM), 1)
    m = jnp.where(m < 96, m, m - 128)
    spread_z = (k == 32 * gz + ((m + 64) // 2 - 32)).astype(jnp.float32)
    to, frm = iota((128, 32), 0), iota((128, 32), 1)
    spread = ((to // 16 == frm // 4) & ((to % 8) // 2 == frm % 4)).astype(jnp.float32)
    out[...] = mid_pre[...] + mm(spread, mm(x, spread_z)).reshape(16, 8, ZM)


def second_kernel(
    mid, mid_p, mid_n, mid_rhs, mid_c, src_w, pre_w, c_w, se,
    adj, grad,
    mc, mwx, mwy, mwz, minv, mva, mvb, sp, c, wx, wy, wz, inv, va, vb,
):
    gx = lax.axis_index("gx")
    mid_zero = jnp.zeros((YM, ZM), jnp.float32)
    mc[0] = mid_zero
    mc[17] = mid_zero
    mc[1:17] = mid_c[...]
    make_weights(mc, mwx, mwy, mwz, minv, 16, 0.25)
    for ref in (mva, mvb):
        for at in (0, 1, 18, 19):
            ref[at] = mid_zero
    for x in range(16):
        mva[x + 2] = jnp.concatenate([mid_p[x], mid[x], mid_n[x]], 0)
    a, o = mva.at[1:19], mvb.at[1:19]
    sweep(a, o, mid_rhs, mwx, mwy, mwz, minv, 16)
    sweep(o, a, mid_rhs, mwx, mwy, mwz, minv, 16)
    sweep(a, o, mid_rhs, mwx, mwy, mwz, minv, 16)

    zero = jnp.zeros((YW, ZE), jnp.float32)
    for ref in (c, va, vb):
        ref[0] = zero
        ref[XW + 1] = zero
    c[1 : XW + 1] = c_w[...]
    make_weights(c, wx, wy, wz, inv, XW, 1.0)
    spread_z = (iota((ZM, ZE), 1) // 2 == iota((ZM, ZE), 0)).astype(jnp.float32)
    spread_y = ((iota((YW, YM), 0) + 12) // 2 == iota((YW, YM), 1)).astype(jnp.float32)
    near = mvb[pl.ds(4 * gx, 8)]
    sp[...] = mm(near.reshape(8 * YM, ZM), spread_z).reshape(8, YM, ZE)
    for m in range(8):
        more = mm(spread_y, sp[m])
        for x in (2 * m, 2 * m + 1):
            va[x + 1] = pre_w[x] + more
    sweep(va, vb, src_w, wx, wy, wz, inv, XW)
    sweep(vb, va, src_w, wx, wy, wz, inv, XW)
    sweep(va, vb, src_w, wx, wy, wz, inv, XW)

    def product(f, one, two, sone, stwo):
        return f * (one - two) * (sone - stwo)

    def half(one, two):
        return jnp.where(jnp.minimum(one, two) == 0.0, 1.0, 0.5)

    lane = iota((YW, CZ), 1)

    def terms(i, carry):
        before, acc = carry
        v, k, s = vb[i + 5], c[i + 5], se[i + 1]
        px = product(half(k, c[i + 6]), v, vb[i + 6], s, se[i + 2])
        py = product(half(k, nxt(k, 0)), v, nxt(v, 0), s, nxt(s, 0))
        pz = product(half(k, nxt(k, 1)), v, nxt(v, 1), s, nxt(s, 1))
        both = k * (px + before + py + prv(py, 0) + pz + prv(pz, 1))
        part = jnp.sum(both[:, :CZ], axis=1, keepdims=True)
        acc = jnp.where(lane == i, part, acc)
        adj[i] = pltpu.roll(v, YW - 4, 0)[:CY, :CZ]
        return px, acc

    first = product(half(c[4], c[5]), vb[4], vb[5], se[0], se[1])
    _, acc = lax.fori_loop(0, CX, terms, (first, jnp.zeros((YW, CZ), jnp.float32)))
    grad[...] = pltpu.roll(acc, YW - 4, 0)[:CY]


def f32(*shape):
    return jax.ShapeDtypeStruct(shape, jnp.float32)


def vm(*shape):
    return pltpu.VMEM(shape, jnp.float32)


def params():
    return pltpu.CompilerParams(vmem_limit_bytes=48 << 20)


def both_ways(up, down, axis):
    count = lax.axis_size(axis)
    higher = [(i, i + 1) for i in range(count - 1)]
    lower = [(j, i) for i, j in higher]
    return lax.ppermute(up, axis, higher), lax.ppermute(down, axis, lower)


def per_device(source, state, log_coef, lateral, owners):
    coef = jnp.exp(log_coef + lateral[:, :, None])
    block = f32(CX, CY, CZ)
    smem = pl.BlockSpec(memory_space=pltpu.SMEM)
    vmem = pl.BlockSpec(memory_space=pltpu.VMEM)
    down, up = pl.pallas_call(
        pack_z_kernel,
        out_shape=(block, block),
        in_specs=[smem, vmem, vmem, vmem],
        name="pack_z",
    )(owners[0, 0], source, coef, state)
    before, after = both_ways(up, down, "gz")
    mine = jnp.concatenate([source, coef, before + after, state[:1], state[CX - 1 :]], 0)
    g = lax.all_gather(mine, "gx")
    pair = f32(52, 24, CZ)
    up, down = pl.pallas_call(
        pack_y_kernel, out_shape=(pair, pair), compiler_params=params(), name="pack_y"
    )(g, state)
    yp, yn = both_ways(up, down, "gy")

    fine, fine1, fine2 = (32, YE, ZE), (33, YE, ZE), (34, YE, ZE)
    mid, mid1, mid2 = (16, YM, ZM), (17, YM, ZM), (18, YM, ZM)
    win, win1, win2 = (XW, YW, ZE), (XW + 1, YW, ZE), (XW + 2, YW, ZE)
    src_w, pre_w, c_w, se, mid_pre, mid_rhs, mid_c, low = pl.pallas_call(
        first_kernel,
        out_shape=(
            f32(*win), f32(*win), f32(*win), f32(CX + 2, YW, ZE),
            f32(16, 8, ZM), f32(*mid), f32(*mid), f32(16, 32, CZ),
        ),
        scratch_shapes=[
            vm(*fine2), vm(*fine1), vm(*fine), vm(*fine), vm(*fine), vm(*fine),
            vm(*fine2), vm(*fine2), vm(32, YM, ZE),
            vm(*mid2), vm(*mid1), vm(*mid), vm(*mid), vm(*mid), vm(*mid),
            vm(*mid2), vm(*mid2), vm(10, 8, CZ),
        ],
        compiler_params=params(),
        name="first",
    )(g, yp, yn, state)

    rec = lax.all_to_all(low, "gz", 0, 0, tiled=True)
    mid_init = pl.pallas_call(
        solve_kernel, out_shape=f32(16, 8, ZM), compiler_params=params(), name="solve"
    )(rec, mid_pre)
    mid_p, mid_n = both_ways(mid_init, mid_init, "gy")

    adj, grad = pl.pallas_call(
        second_kernel,
        out_shape=(block, f32(CY, CZ)),
        scratch_shapes=[
            vm(*mid2), vm(*mid1), vm(*mid), vm(*mid), vm(*mid),
            vm(20, YM, ZM), vm(20, YM, ZM), vm(8, YM, ZE),
            vm(*win2), vm(*win1), vm(*win), vm(*win), vm(*win), vm(*win2), vm(*win2),
        ],
        compiler_params=params(),
        name="second",
    )(mid_init, mid_p, mid_n, mid_rhs, mid_c, src_w, pre_w, c_w, se)
    sums = lax.all_to_all(grad, "gz", 0, 0, tiled=True)
    total = jnp.sum(sums[:, :CX], axis=0)[:, None]
    return adj, total * (-1.0 / math.sqrt(source.shape[2] * lax.axis_size("gz")))


def solution(mesh):
    placed = (
        P("gx", "gy", "gz"),
        P("gx", "gy", "gz"),
        P("gx", "gy", "gz"),
        P("gx", "gy"),
        P("gx", "gy", None),
    )
    return jax.shard_map(
        per_device,
        mesh=mesh,
        in_specs=placed,
        out_specs=(P("gx", "gy", "gz"), P("gx", ("gy", "gz"))),
        check_vma=False,
    )
```

time: 1780 us -> 152 us (0.09)
  the two profiles are of different devices: /device:TPU:286 before, /device:TPU:33 now
where the time goes in v1:
time: 152 us
  Pallas kernels  59.9 us (39%)
  blocking collectives  46.1 us (30%)
  waiting for transfers between devices  21.9 us (14%)
  starting transfers between devices  20.2 us (13%)
  local copies, waits for them, and re-layouts  1.72 us (1%)
    pallas_call x1, Pallas kernels, per_device(): pl.pallas_call(first_kernel, out_shape=(f32(*win), f32(*win), f32(*win),...  34 us
    all_to_all x1, blocking collectives, per_device(): rec = lax.all_to_all(low, 'gz', 0, 0, tiled=True)  23.4 us
    pallas_call x1, Pallas kernels, per_device(): pl.pallas_call(second_kernel, out_shape=(block, f32(CY, CZ)), scratch_sha...  22.8 us
    ppermute x6, waiting for transfers between devices, both_ways(): return (lax.ppermute(up, axis, higher), lax.ppermute(down, axis, lower))  21.9 us
    ppermute x6, starting transfers between devices, both_ways(): return (lax.ppermute(up, axis, higher), lax.ppermute(down, axis, lower))  20.2 us
    all_gather x1, blocking collectives, per_device(): g = lax.all_gather(mine, 'gx')  12.3 us
    all_to_all x1, blocking collectives, per_device(): sums = lax.all_to_all(grad, 'gz', 0, 0, tiled=True)  10.4 us
  transfers between devices with their start and end apart: 6, of which 4 were waited for; matrix products, arithmetic and copies ran while one was open for 0% of the time, Pallas kernels for 0%

profile of v1, /device:TPU:33, one launch (start us, length us, event | category | flops | bytes accessed | tf_op | source)
XLA Modules:
  0.0 151.8 jit_solution(8688242334512017404)
XLA Ops:
  0.6 0.0 copy-start.2
  0.6 0.0 copy-start.1
  0.6 0.9 constant_dynamic-update-slice_fusion.3
  1.5 0.0 copy-done.2
  1.5 0.0 copy-done.1
  1.5 0.7 constant_dynamic-update-slice_fusion.2
  2.3 1.6 %pack_z.1 = (f32[8,16,128]{2,1,0:T(8,128)}, f32[8,16,128]{2,1,0:T(8,128)}) custom-call(s32[16]{0:T(128)} %bitcast.12, f32[8,16,128]{2,1,0:T(8,128)} %src.1, f32[8,16,128]{2,1,0:T(8,128)} %get-tuple-element.31.c, f32[8,16,128]{2,1,0:T(8,128)} %state.5), custom_call_target="tpu_custom_call" | custom-call | tf_op jit(solution)/shard_map/pack_z/pallas_call | solution.py:391
  3.9 4.5 %collective-permute-start = (f32[8,16,128]{2,1,0:T(8,128)}, f32[8,16,128]{2,1,0:T(8,128)S(1)}, u32[]{:S(2)}, u32[]{:S(2)}) collective-permute-start(f32[8,16,128]{2,1,0:T(8,128)} %get-tuple-element.16), channel_id=1, source_target_pairs={{0,1},{1,2},{2,3},{3,4},{4,5},{5,6},{6,7},{7,8},{8,9},{9,10},{10,1... | collective-permute-start | bytes 196616 | tf_op jit(solution)/shard_map/ppermute | solution.py:383
  8.5 1.9 %collective-permute-start.1 = (f32[8,16,128]{2,1,0:T(8,128)}, f32[8,16,128]{2,1,0:T(8,128)S(1)}, u32[]{:S(2)}, u32[]{:S(2)}) collective-permute-start(f32[8,16,128]{2,1,0:T(8,128)} %get-tuple-element.17), channel_id=1, source_target_pairs={{1,0},{2,1},{3,2},{4,3},{5,4},{6,5},{7,6},{8,7},{9,8},{10,9},{11,1... | collective-permute-start | bytes 196616 | tf_op jit(solution)/shard_map/ppermute | solution.py:383
  10.4 0.0 collective-permute-done
  10.4 3.9 %collective-permute-done.1 = f32[8,16,128]{2,1,0:T(8,128)S(1)} collective-permute-done((f32[8,16,128]{2,1,0:T(8,128)}, f32[8,16,128]{2,1,0:T(8,128)S(1)}, u32[]{:S(2)}, u32[]{:S(2)}) %collective-permute-start.1) | collective-permute-done | bytes 65568 | tf_op jit(solution)/shard_map/ppermute | solution.py:383
  14.3 0.0 copy-start
  14.3 0.8 copy-done
  15.1 12.3 %all-gather = f32[104,16,128]{2,1,0:T(8,128)S(1)} all-gather(f32[26,16,128]{2,1,0:T(8,128)S(1)} %constant_dynamic-update-slice_fusion), channel_id=2, replica_groups=mesh['gx'=4,'gy'=8,'gz'=16] {'gx'}, dimensions={0}, use_global_device_ids=true | all-gather | bytes 1064960 | tf_op jit(solution)/shard_map/all_gather | solution.py:399
  27.4 0.1 pack_y.1
  27.5 2.3 %collective-permute-start.2 = (f32[52,24,128]{2,1,0:T(8,128)S(1)}, f32[52,24,128]{2,1,0:T(8,128)S(1)}, u32[]{:S(2)}, u32[]{:S(2)}) collective-permute-start(f32[52,24,128]{2,1,0:T(8,128)S(1)} %get-tuple-element.18), channel_id=1, source_target_pairs={{0,16},{16,32},{32,48},{48,64},{64,80},{80,96},{96,112},{1,17},{17... | collective-permute-start | bytes 1916936 | tf_op jit(solution)/shard_map/ppermute | solution.py:383
  29.8 4.2 %collective-permute-start.3 = (f32[52,24,128]{2,1,0:T(8,128)S(1)}, f32[52,24,128]{2,1,0:T(8,128)S(1)}, u32[]{:S(2)}, u32[]{:S(2)}) collective-permute-start(f32[52,24,128]{2,1,0:T(8,128)S(1)} %get-tuple-element.19), channel_id=1, source_target_pairs={{16,0},{32,16},{48,32},{64,48},{80,64},{96,80},{112,96},{17,1},{33... | collective-permute-start | bytes 1916936 | tf_op jit(solution)/shard_map/ppermute | solution.py:383
  34.0 12.2 %collective-permute-done.2.yp = f32[52,24,128]{2,1,0:T(8,128)S(1)} collective-permute-done((f32[52,24,128]{2,1,0:T(8,128)S(1)}, f32[52,24,128]{2,1,0:T(8,128)S(1)}, u32[]{:S(2)}, u32[]{:S(2)}) %collective-permute-start.2) | collective-permute-done | bytes 639008 | tf_op jit(solution)/shard_map/ppermute | solution.py:383
  46.2 0.9 collective-permute-done.3.yn
  47.1 34.0 %first.1 = (f32[16,24,256]{2,1,0:T(8,128)S(1)}, f32[16,24,256]{2,1,0:T(8,128)S(1)}, f32[16,24,256]{2,1,0:T(8,128)S(1)}, f32[10,24,256]{2,1,0:T(8,128)S(1)}, f32[...) custom-call(f32[4,26,16,128]{3,2,1,0:T(8,128)S(1)} %bitcast.9, ...), custom_call_target="tpu_custom_call" | custom-call | tf_op jit(solution)/shard_map/first/pallas_call | solution.py:409
  81.0 23.4 %all_to_all.17.rec = f32[16,32,128]{2,1,0:T(8,128)S(1)} all-to-all(f32[16,32,128]{2,1,0:T(8,128)S(1)} %get-tuple-element.20), channel_id=1, replica_groups=mesh['gx'=4,'gy'=8,'gz'=16] {'gz'}, dimensions={0} | all-to-all | bytes 524288 | tf_op jit(solution)/shard_map/all_to_all | solution.py:425
  104.4 1.4 solve.1.mid
  105.8 5.3 %collective-permute-start.5 = (f32[16,8,128]{2,1,0:T(8,128)S(1)}, f32[16,8,128]{2,1,0:T(8,128)S(1)}, u32[]{:S(2)}, u32[]{:S(2)}) collective-permute-start(f32[16,8,128]{2,1,0:T(8,128)S(1)} %solve.1.mid), channel_id=1, source_target_pairs={{16,0},{32,16},{48,32},{64,48},{80,64},{96,80},{112,96},{17,1},{33... | collective-permute-start | bytes 196616 | tf_op jit(solution)/shard_map/ppermute | solution.py:383
  111.1 1.9 %collective-permute-start.4 = (f32[16,8,128]{2,1,0:T(8,128)S(1)}, f32[16,8,128]{2,1,0:T(8,128)S(1)}, u32[]{:S(2)}, u32[]{:S(2)}) collective-permute-start(f32[16,8,128]{2,1,0:T(8,128)S(1)} %solve.1.mid), channel_id=1, source_target_pairs={{0,16},{16,32},{32,48},{48,64},{64,80},{80,96},{96,112},{1,17},{17... | collective-permute-start | bytes 196616 | tf_op jit(solution)/shard_map/ppermute | solution.py:383
  113.0 0.0 collective-permute-done.5.mid_n
  113.0 5.0 %collective-permute-done.4.mid_p = f32[16,8,128]{2,1,0:T(8,128)S(1)} collective-permute-done((f32[16,8,128]{2,1,0:T(8,128)S(1)}, f32[16,8,128]{2,1,0:T(8,128)S(1)}, u32[]{:S(2)}, u32[]{:S(2)}) %collective-permute-start.4) | collective-permute-done | bytes 65568 | tf_op jit(solution)/shard_map/ppermute | solution.py:383
  118.0 22.8 %second.1 = (f32[8,16,128]{2,1,0:T(8,128)}, f32[16,128]{1,0:T(8,128)S(1)}) custom-call(f32[16,8,128]{2,1,0:T(8,128)S(1)} %solve.1.mid, f32[16,8,128]{2,1,0:T(8,128)S(1)} %collective-permute-done.4.mid_p, f32[16,8,128]{2,1,0:T(8,128)S(1)} %collective-permute-done.5.mid_n, f32[16,24,128]{2,1,0:T(8,128)S(1)} %get-tuple-element.22.mid_rhs, ...), custom_call_target="tpu_custom_call" | custom-call | tf_op jit(solution)/shard_map/second/pallas_call | solution.py:431
  140.8 10.4 %all_to_all.18 = f32[16,1,128]{2,1,0:T(1,128)S(1)} all-to-all(f32[16,1,128]{2,1,0:T(1,128)S(1)} %bitcast.10), channel_id=1, replica_groups=mesh['gx'=4,'gy'=8,'gz'=16] {'gz'}, dimensions={0} | all-to-all | bytes 16384 | tf_op jit(solution)/shard_map/all_to_all | solution.py:442
  151.3 0.5 multiply_bitcast_fusion
  (4 shorter events, 0.0 us)
Async XLA Ops:
  0.6 0.9 copy-start.2
  0.6 0.9 copy-start.1
  3.9 6.5 %collective-permute-start = (f32[8,16,128]{2,1,0:T(8,128)}, f32[8,16,128]{2,1,0:T(8,128)S(1)}, u32[]{:S(2)}, u32[]{:S(2)}) collective-permute-start(f32[8,16,128]{2,1,0:T(8,128)} %get-tuple-element.16), channel_id=1, source_target_pairs={{0,1},{1,2},{2,3},{3,4},{4,5},{5,6},{6,7},{7,8},{8,9},{9,10},{10,1... | collective-permute-start | bytes 196616 | tf_op jit(solution)/shard_map/ppermute | solution.py:383
  8.5 5.8 %collective-permute-start.1 = (f32[8,16,128]{2,1,0:T(8,128)}, f32[8,16,128]{2,1,0:T(8,128)S(1)}, u32[]{:S(2)}, u32[]{:S(2)}) collective-permute-start(f32[8,16,128]{2,1,0:T(8,128)} %get-tuple-element.17), channel_id=1, source_target_pairs={{1,0},{2,1},{3,2},{4,3},{5,4},{6,5},{7,6},{8,7},{9,8},{10,9},{11,1... | collective-permute-start | bytes 196616 | tf_op jit(solution)/shard_map/ppermute | solution.py:383
  14.3 0.8 copy-start
  27.5 18.7 %collective-permute-start.2 = (f32[52,24,128]{2,1,0:T(8,128)S(1)}, f32[52,24,128]{2,1,0:T(8,128)S(1)}, u32[]{:S(2)}, u32[]{:S(2)}) collective-permute-start(f32[52,24,128]{2,1,0:T(8,128)S(1)} %get-tuple-element.18), channel_id=1, source_target_pairs={{0,16},{16,32},{32,48},{48,64},{64,80},{80,96},{96,112},{1,17},{17... | collective-permute-start | bytes 1916936 | tf_op jit(solution)/shard_map/ppermute | solution.py:383
  29.8 17.3 %collective-permute-start.3 = (f32[52,24,128]{2,1,0:T(8,128)S(1)}, f32[52,24,128]{2,1,0:T(8,128)S(1)}, u32[]{:S(2)}, u32[]{:S(2)}) collective-permute-start(f32[52,24,128]{2,1,0:T(8,128)S(1)} %get-tuple-element.19), channel_id=1, source_target_pairs={{16,0},{32,16},{48,32},{64,48},{80,64},{96,80},{112,96},{17,1},{33... | collective-permute-start | bytes 1916936 | tf_op jit(solution)/shard_map/ppermute | solution.py:383
  105.8 7.3 %collective-permute-start.5 = (f32[16,8,128]{2,1,0:T(8,128)S(1)}, f32[16,8,128]{2,1,0:T(8,128)S(1)}, u32[]{:S(2)}, u32[]{:S(2)}) collective-permute-start(f32[16,8,128]{2,1,0:T(8,128)S(1)} %solve.1.mid), channel_id=1, source_target_pairs={{16,0},{32,16},{48,32},{64,48},{80,64},{96,80},{112,96},{17,1},{33... | collective-permute-start | bytes 196616 | tf_op jit(solution)/shard_map/ppermute | solution.py:383
  111.1 6.9 %collective-permute-start.4 = (f32[16,8,128]{2,1,0:T(8,128)S(1)}, f32[16,8,128]{2,1,0:T(8,128)S(1)}, u32[]{:S(2)}, u32[]{:S(2)}) collective-permute-start(f32[16,8,128]{2,1,0:T(8,128)S(1)} %solve.1.mid), channel_id=1, source_target_pairs={{0,16},{16,32},{32,48},{48,64},{64,80},{80,96},{96,112},{1,17},{17... | collective-permute-start | bytes 196616 | tf_op jit(solution)/shard_map/ppermute | solution.py:383

commit v2 on v1

--- a/solution.py
+++ b/solution.py
@@ -42,6 +42,10 @@
     return jnp.where(jnp.minimum(a, b) == 0.0, both, 0.5 * both)
 
 
+def unroll(planes):
+    return 16 if planes == 16 else 8
+
+
 def make_weights(c, wx, wy, wz, inv, planes, scale):
     wx[0] = scale * face(c[0], c[1])
 
@@ -57,7 +61,7 @@
         inv[x] = jnp.where(here > 0.0, OMEGA / total, 0.0)
         return carry
 
-    lax.fori_loop(0, planes, step, 0)
+    lax.fori_loop(0, planes, step, 0, unroll=unroll(planes))
 
 
 def residual(v, b, wx, wy, wz, x, before):
@@ -75,14 +79,25 @@
         out[x + 1] = here + inv[x] * rest
         return fx
 
-    lax.fori_loop(0, planes, step, wx[0] * (0.0 - v[1]))
-
-
-def pack_z_kernel(line, src, c, state, down, up):
+    lax.fori_loop(0, planes, step, wx[0] * (0.0 - v[1]), unroll=unroll(planes))
+
+
+def pack_z_kernel(line, src, log_coef, lateral, state, mine, down, up):
     gz = lax.axis_index("gz")
     cut = (line[gz] != line[jnp.minimum(gz + 1, 15)]).astype(jnp.float32)
+    pick = (iota((CX * CY, CX), 0) // CY == iota((CX * CY, CX), 1)).astype(jnp.float32)
+    rows = mm(pick, lateral[...])
+    own = iota((CX * CY, CY), 0) % CY == iota((CX * CY, CY), 1)
+    rows = jnp.sum(jnp.where(own, rows, 0.0), axis=1, keepdims=True)
+    rows = jnp.broadcast_to(rows, (CX * CY, CZ)).reshape(CX, CY, CZ)
+    c = jnp.exp(log_coef[...] + rows)
+    s = src[...]
+    mine[0:CX] = s
+    mine[CX : 2 * CX] = c
+    mine[3 * CX] = state[0]
+    mine[3 * CX + 1] = state[CX - 1]
     lane = iota((CX, CY, CZ), 2)
-    s, k = src[...], pltpu.roll(c[...], 64, 2)
+    k = pltpu.roll(c, 64, 2)
     t = pltpu.roll(state[...], 32, 2)
     zero = jnp.zeros_like(s)
     far = CZ - HZ
@@ -159,7 +174,7 @@
         va[x + 1] = inv[x] * b[x]
         return carry
 
-    lax.fori_loop(0, nx, start, 0)
+    lax.fori_loop(0, nx, start, 0, unroll=4)
     sweep(va, vb, b, wx, wy, wz, inv, nx)
     sweep(vb, va, b, wx, wy, wz, inv, nx)
 
@@ -174,7 +189,7 @@
         t[m + 16] = mm(fold_y, c[x + 1] + c[x + 2])
         return fx
 
-    lax.fori_loop(0, 16, coarse, wx[0] * (0.0 - va[1]))
+    lax.fori_loop(0, 16, coarse, wx[0] * (0.0 - va[1]), unroll=8)
     both = mm(t[...].reshape(32 * YM, ZE), fold_z).reshape(32, YM, ZM)
     mb[...] = both[:16]
     mid_rhs_o[...] = both[:16]
@@ -194,7 +209,7 @@
         c_w[w] = jnp.where(inside, c[x + 1, 8:32], 0.0)
         return carry
 
-    lax.fori_loop(0, XW, keep, 0)
+    lax.fori_loop(0, XW, keep, 0, unroll=4)
 
     zero8 = jnp.zeros((8, CZ), jnp.float32)
     wide = jnp.zeros((YW, CZ), jnp.float32)
@@ -229,7 +244,7 @@
         mid_pre_o[x] = mva[x + 1, 8:16]
         return fx
 
-    lax.fori_loop(0, 16, rest, mwx[0] * (0.0 - mva[1]))
+    lax.fori_loop(0, 16, rest, mwx[0] * (0.0 - mva[1]), unroll=16)
 
     shape = (64, 16 * YM)
     to, frm = iota(shape, 0), iota(shape, 1)
@@ -360,7 +375,9 @@
         return px, acc
 
     first = product(half(c[4], c[5]), vb[4], vb[5], se[0], se[1])
-    _, acc = lax.fori_loop(0, CX, terms, (first, jnp.zeros((YW, CZ), jnp.float32)))
+    _, acc = lax.fori_loop(
+        0, CX, terms, (first, jnp.zeros((YW, CZ), jnp.float32)), unroll=8
+    )
     grad[...] = pltpu.roll(acc, YW - 4, 0)[:CY]
 
 
@@ -384,18 +401,20 @@
 
 
 def per_device(source, state, log_coef, lateral, owners):
-    coef = jnp.exp(log_coef + lateral[:, :, None])
     block = f32(CX, CY, CZ)
     smem = pl.BlockSpec(memory_space=pltpu.SMEM)
     vmem = pl.BlockSpec(memory_space=pltpu.VMEM)
-    down, up = pl.pallas_call(
+    mine, down, up = pl.pallas_call(
         pack_z_kernel,
-        out_shape=(block, block),
-        in_specs=[smem, vmem, vmem, vmem],
+        out_shape=(f32(3 * CX + 2, CY, CZ), block, block),
+        in_specs=[smem, vmem, vmem, vmem, vmem],
         name="pack_z",
-    )(owners[0, 0], source, coef, state)
-    before, after = both_ways(up, down, "gz")
-    mine = jnp.concatenate([source, coef, before + after, state[:1], state[CX - 1 :]], 0)
+    )(owners[0, 0], source, log_coef, lateral, state)
+    gz, count = lax.axis_index("gz"), lax.axis_size("gz")
+    before = lax.ppermute(up, "gz", [(i, (i + 1) % count) for i in range(count)])
+    after = lax.ppermute(down, "gz", [(i, (i - 1) % count) for i in range(count)])
+    halo = jnp.where(gz > 0, before, 0.0) + jnp.where(gz < count - 1, after, 0.0)
+    mine = lax.dynamic_update_slice(mine, halo, (2 * CX, 0, 0))
     g = lax.all_gather(mine, "gx")
     pair = f32(52, 24, CZ)
     up, down = pl.pallas_call(

time: 152 us -> 104 us (0.68)
  Pallas kernels: 59.9 us -> 17.2 us
  blocking collectives: 46.1 us -> 52.2 us
  waiting for transfers between devices: 21.9 us -> 16.2 us
  starting transfers between devices: 20.2 us -> 16.4 us
  local copies, waits for them, and re-layouts: 1.72 us -> 0.01 us
    pallas_call x1, Pallas kernels: 34 us -> 10.2 us  [per_device(): pl.pallas_call(first_kernel, out_shape=(f32(*win), f32(*win), f32(*win),...]
    pallas_call x1, Pallas kernels: 22.8 us -> 3.57 us  [per_device(): pl.pallas_call(second_kernel, out_shape=(block, f32(CY, CZ)), scratch_sha...]
    ppermute x6 -> x4, waiting for transfers between devices: 21.9 us -> 12.3 us  [both_ways(): return (lax.ppermute(up, axis, higher), lax.ppermute(down, axis, lower))]
    ppermute x6 -> x4, starting transfers between devices: 20.2 us -> 13.7 us  [both_ways(): return (lax.ppermute(up, axis, higher), lax.ppermute(down, axis, lower))]
    all_to_all x1, blocking collectives: 23.4 us -> 29.2 us  [per_device(): rec = lax.all_to_all(low, 'gz', 0, 0, tiled=True)]
    ppermute x0 -> x2, waiting for transfers between devices: none -> 3.9 us  [the longest x1 2.25 us: per_device(): lax.ppermute(down, 'gz', [(i, (i - 1) % count) for i in range(count)])]
    ppermute x0 -> x2, starting transfers between devices: none -> 2.65 us  [the longest x1 2.65 us: per_device(): lax.ppermute(up, 'gz', [(i, (i + 1) % count) for i in range(count)])]
    unnamed x8 -> x2, local copies, waits for them, and re-layouts: 1.72 us -> 0.01 us
  transfers between devices with their start and end apart: 6 -> 6, of which waited for: 4 -> 5; matrix products, arithmetic and copies ran while one was open for 0% -> 0% of each run, Pallas kernels for 0% -> 0%
where the time goes in v2:
time: 104 us
  blocking collectives  52.2 us (50%)
  Pallas kernels  17.2 us (17%)
  starting transfers between devices  16.4 us (16%)
  waiting for transfers between devices  16.2 us (16%)
  other arithmetic  1.17 us (1%)
    all_to_all x1, blocking collectives, per_device(): rec = lax.all_to_all(low, 'gz', 0, 0, tiled=True)  29.2 us
    ppermute x4, starting transfers between devices, both_ways(): return (lax.ppermute(up, axis, higher), lax.ppermute(down, axis, lower))  13.7 us
    all_gather x1, blocking collectives, per_device(): g = lax.all_gather(mine, 'gx')  12.5 us
    ppermute x4, waiting for transfers between devices, both_ways(): return (lax.ppermute(up, axis, higher), lax.ppermute(down, axis, lower))  12.3 us
    all_to_all x1, blocking collectives, per_device(): sums = lax.all_to_all(grad, 'gz', 0, 0, tiled=True)  10.4 us
    pallas_call x1, Pallas kernels, per_device(): pl.pallas_call(first_kernel, out_shape=(f32(*win), f32(*win), f32(*win),...  10.2 us
    pallas_call x1, Pallas kernels, per_device(): pl.pallas_call(second_kernel, out_shape=(block, f32(CY, CZ)), scratch_sha...  3.57 us
    ppermute x1, starting transfers between devices, per_device(): lax.ppermute(up, 'gz', [(i, (i + 1) % count) for i in range(count)])  2.65 us
  transfers between devices with their start and end apart: 6, of which 5 were waited for; matrix products, arithmetic and copies ran while one was open for 0% of the time, Pallas kernels for 0%

profile of v2, /device:TPU:33, one launch (start us, length us, event | category | flops | bytes accessed | tf_op | source)
XLA Modules:
  0.0 103.8 jit_solution(12918902582433576784)
XLA Ops:
  0.6 1.9 %pack_z.1 = (f32[26,16,128]{2,1,0:T(8,128)}, f32[8,16,128]{2,1,0:T(8,128)}, f32[8,16,128]{2,1,0:T(8,128)}) custom-call(s32[16]{0:T(128)} %bitcast.13, f32[8,16,128]{2,1,0:T(8,128)} %src.1, f32[8,16,128]{2,1,0:T(8,128)} %log_coef.1, f32[8,16]{1,0:T(8,128)} %lateral.1, f32[8,16,128]{2,1,0:T(8,128)} %state.5), custom_call_target="tpu_custom_call" | custom-call | tf_op jit(solution)/shard_map/pack_z/pallas_call | solution.py:407
  2.6 2.7 %collective-permute-start = (f32[8,16,128]{2,1,0:T(8,128)}, f32[8,16,128]{2,1,0:T(8,128)S(1)}, u32[]{:S(2)}, u32[]{:S(2)}) collective-permute-start(f32[8,16,128]{2,1,0:T(8,128)} %get-tuple-element.18), channel_id=1, source_target_pairs={{0,1},{1,2},{2,3},{3,4},{4,5},{5,6},{6,7},{7,8},{8,9},{9,10},{10,1... | collective-permute-start | bytes 196616 | tf_op jit(solution)/shard_map/ppermute | solution.py:414
  5.2 0.0 collective-permute-start.1
  5.2 1.6 %collective-permute-done = f32[8,16,128]{2,1,0:T(8,128)S(1)} collective-permute-done((f32[8,16,128]{2,1,0:T(8,128)}, f32[8,16,128]{2,1,0:T(8,128)S(1)}, u32[]{:S(2)}, u32[]{:S(2)}) %collective-permute-start) | collective-permute-done | bytes 65568 | tf_op jit(solution)/shard_map/ppermute | solution.py:414
  6.9 2.3 %collective-permute-done.1 = f32[8,16,128]{2,1,0:T(8,128)S(1)} collective-permute-done((f32[8,16,128]{2,1,0:T(8,128)}, f32[8,16,128]{2,1,0:T(8,128)S(1)}, u32[]{:S(2)}, u32[]{:S(2)}) %collective-permute-start.1) | collective-permute-done | bytes 65568 | tf_op jit(solution)/shard_map/ppermute | solution.py:415
  9.1 0.6 bitcast_dynamic-update-slice_fusion
  9.7 0.0 copy-start
  9.7 12.5 %all_gather.10.g = f32[4,26,16,128]{3,2,1,0:T(8,128)S(1)} all-gather(f32[1,26,16,128]{3,2,1,0:T(8,128)} %bitcast_dynamic-update-slice_fusion), channel_id=1, replica_groups=mesh['gx'=4,'gy'=8,'gz'=16] {'gx'}, dimensions={0}, use_global_device_ids=true | all-gather | bytes 1064960 | tf_op jit(solution)/shard_map/all_gather | solution.py:418
  22.3 0.0 copy-done
  22.3 0.1 pack_y.1
  22.4 2.3 %collective-permute-start.2 = (f32[52,24,128]{2,1,0:T(8,128)S(1)}, f32[52,24,128]{2,1,0:T(8,128)S(1)}, u32[]{:S(2)}, u32[]{:S(2)}) collective-permute-start(f32[52,24,128]{2,1,0:T(8,128)S(1)} %get-tuple-element.20), channel_id=1, source_target_pairs={{0,16},{16,32},{32,48},{48,64},{64,80},{80,96},{96,112},{1,17},{17... | collective-permute-start | bytes 1916936 | tf_op jit(solution)/shard_map/ppermute | solution.py:400
  24.7 4.2 %collective-permute-start.3 = (f32[52,24,128]{2,1,0:T(8,128)S(1)}, f32[52,24,128]{2,1,0:T(8,128)S(1)}, u32[]{:S(2)}, u32[]{:S(2)}) collective-permute-start(f32[52,24,128]{2,1,0:T(8,128)S(1)} %get-tuple-element.21), channel_id=1, source_target_pairs={{16,0},{32,16},{48,32},{64,48},{80,64},{96,80},{112,96},{17,1},{33... | collective-permute-start | bytes 1916936 | tf_op jit(solution)/shard_map/ppermute | solution.py:400
  28.9 5.9 %collective-permute-done.2.yp = f32[52,24,128]{2,1,0:T(8,128)S(1)} collective-permute-done((f32[52,24,128]{2,1,0:T(8,128)S(1)}, f32[52,24,128]{2,1,0:T(8,128)S(1)}, u32[]{:S(2)}, u32[]{:S(2)}) %collective-permute-start.2) | collective-permute-done | bytes 639008 | tf_op jit(solution)/shard_map/ppermute | solution.py:400
  34.7 1.5 %collective-permute-done.3.yn = f32[52,24,128]{2,1,0:T(8,128)S(1)} collective-permute-done((f32[52,24,128]{2,1,0:T(8,128)S(1)}, f32[52,24,128]{2,1,0:T(8,128)S(1)}, u32[]{:S(2)}, u32[]{:S(2)}) %collective-permute-start.3) | collective-permute-done | bytes 639008 | tf_op jit(solution)/shard_map/ppermute | solution.py:400
  36.2 10.2 %first.1 = (f32[16,24,256]{2,1,0:T(8,128)S(1)}, f32[16,24,256]{2,1,0:T(8,128)S(1)}, f32[16,24,256]{2,1,0:T(8,128)S(1)}, f32[10,24,256]{2,1,0:T(8,128)S(1)}, f32[...) custom-call(f32[4,26,16,128]{3,2,1,0:T(8,128)S(1)} %all_gather.10.g,, ...), custom_call_target="tpu_custom_call" | custom-call | tf_op jit(solution)/shard_map/first/pallas_call | solution.py:428
  46.5 29.2 %all_to_all.17.rec = f32[16,32,128]{2,1,0:T(8,128)S(1)} all-to-all(f32[16,32,128]{2,1,0:T(8,128)S(1)} %get-tuple-element.22), channel_id=1, replica_groups=mesh['gx'=4,'gy'=8,'gz'=16] {'gz'}, dimensions={0} | all-to-all | bytes 524288 | tf_op jit(solution)/shard_map/all_to_all | solution.py:444
  75.7 1.4 %solve.1.mid = f32[16,8,128]{2,1,0:T(8,128)S(1)} custom-call(f32[16,32,128]{2,1,0:T(8,128)S(1)} %all_to_all.17.rec, f32[16,8,128]{2,1,0:T(8,128)S(1)} %get-tuple-element.23.mid_pre), custom_call_target="tpu_custom_call" | custom-call | tf_op jit(solution)/shard_map/solve/pallas_call | solution.py:445
  77.0 5.3 %collective-permute-start.5 = (f32[16,8,128]{2,1,0:T(8,128)S(1)}, f32[16,8,128]{2,1,0:T(8,128)S(1)}, u32[]{:S(2)}, u32[]{:S(2)}) collective-permute-start(f32[16,8,128]{2,1,0:T(8,128)S(1)} %solve.1.mid), channel_id=1, source_target_pairs={{16,0},{32,16},{48,32},{64,48},{80,64},{96,80},{112,96},{17,1},{33... | collective-permute-start | bytes 196616 | tf_op jit(solution)/shard_map/ppermute | solution.py:400
  82.3 1.9 %collective-permute-start.4 = (f32[16,8,128]{2,1,0:T(8,128)S(1)}, f32[16,8,128]{2,1,0:T(8,128)S(1)}, u32[]{:S(2)}, u32[]{:S(2)}) collective-permute-start(f32[16,8,128]{2,1,0:T(8,128)S(1)} %solve.1.mid), channel_id=1, source_target_pairs={{0,16},{16,32},{32,48},{48,64},{64,80},{80,96},{96,112},{1,17},{17... | collective-permute-start | bytes 196616 | tf_op jit(solution)/shard_map/ppermute | solution.py:400
  84.3 0.0 collective-permute-done.5.mid_n
  84.3 5.0 %collective-permute-done.4.mid_p = f32[16,8,128]{2,1,0:T(8,128)S(1)} collective-permute-done((f32[16,8,128]{2,1,0:T(8,128)S(1)}, f32[16,8,128]{2,1,0:T(8,128)S(1)}, u32[]{:S(2)}, u32[]{:S(2)}) %collective-permute-start.4) | collective-permute-done | bytes 65568 | tf_op jit(solution)/shard_map/ppermute | solution.py:400
  89.3 3.6 %second.1 = (f32[8,16,128]{2,1,0:T(8,128)}, f32[16,128]{1,0:T(8,128)S(1)}) custom-call(f32[16,8,128]{2,1,0:T(8,128)S(1)} %solve.1.mid, f32[16,8,128]{2,1,0:T(8,128)S(1)} %collective-permute-done.4.mid_p, f32[16,8,128]{2,1,0:T(8,128)S(1)} %collective-permute-done.5.mid_n, f32[16,24,128]{2,1,0:T(8,128)S(1)} %get-tuple-element.24.mid_rhs, ...), custom_call_target="tpu_custom_call" | custom-call | tf_op jit(solution)/shard_map/second/pallas_call | solution.py:450
  92.8 10.4 %all_to_all.18 = f32[16,1,128]{2,1,0:T(1,128)S(1)} all-to-all(f32[16,1,128]{2,1,0:T(1,128)S(1)} %bitcast.10), channel_id=1, replica_groups=mesh['gx'=4,'gy'=8,'gz'=16] {'gz'}, dimensions={0} | all-to-all | bytes 16384 | tf_op jit(solution)/shard_map/all_to_all | solution.py:461
  103.3 0.5 multiply_bitcast_fusion
  (1 shorter events, 0.0 us)
Async XLA Ops:
  2.6 4.3 %collective-permute-start = (f32[8,16,128]{2,1,0:T(8,128)}, f32[8,16,128]{2,1,0:T(8,128)S(1)}, u32[]{:S(2)}, u32[]{:S(2)}) collective-permute-start(f32[8,16,128]{2,1,0:T(8,128)} %get-tuple-element.18), channel_id=1, source_target_pairs={{0,1},{1,2},{2,3},{3,4},{4,5},{5,6},{6,7},{7,8},{8,9},{9,10},{10,1... | collective-permute-start | bytes 196616 | tf_op jit(solution)/shard_map/ppermute | solution.py:414
  5.2 3.9 %collective-permute-start.1 = (f32[8,16,128]{2,1,0:T(8,128)}, f32[8,16,128]{2,1,0:T(8,128)S(1)}, u32[]{:S(2)}, u32[]{:S(2)}) collective-permute-start(f32[8,16,128]{2,1,0:T(8,128)} %get-tuple-element.19), channel_id=1, source_target_pairs={{0,15},{1,0},{2,1},{3,2},{4,3},{5,4},{6,5},{7,6},{8,7},{9,8},{10,9... | collective-permute-start | bytes 196616 | tf_op jit(solution)/shard_map/ppermute | solution.py:415
  9.7 12.5 %copy-start = (f32[8,16,128]{2,1,0:T(8,128)S(1)}, f32[8,16,128]{2,1,0:T(8,128)}, u32[]{:S(2)}) copy-start(f32[8,16,128]{2,1,0:T(8,128)} %state.5) | copy-start | bytes 196612
  22.4 12.4 %collective-permute-start.2 = (f32[52,24,128]{2,1,0:T(8,128)S(1)}, f32[52,24,128]{2,1,0:T(8,128)S(1)}, u32[]{:S(2)}, u32[]{:S(2)}) collective-permute-start(f32[52,24,128]{2,1,0:T(8,128)S(1)} %get-tuple-element.20), channel_id=1, source_target_pairs={{0,16},{16,32},{32,48},{48,64},{64,80},{80,96},{96,112},{1,17},{17... | collective-permute-start | bytes 1916936 | tf_op jit(solution)/shard_map/ppermute | solution.py:400
  24.7 11.5 %collective-permute-start.3 = (f32[52,24,128]{2,1,0:T(8,128)S(1)}, f32[52,24,128]{2,1,0:T(8,128)S(1)}, u32[]{:S(2)}, u32[]{:S(2)}) collective-permute-start(f32[52,24,128]{2,1,0:T(8,128)S(1)} %get-tuple-element.21), channel_id=1, source_target_pairs={{16,0},{32,16},{48,32},{64,48},{80,64},{96,80},{112,96},{17,1},{33... | collective-permute-start | bytes 1916936 | tf_op jit(solution)/shard_map/ppermute | solution.py:400
  77.0 7.3 %collective-permute-start.5 = (f32[16,8,128]{2,1,0:T(8,128)S(1)}, f32[16,8,128]{2,1,0:T(8,128)S(1)}, u32[]{:S(2)}, u32[]{:S(2)}) collective-permute-start(f32[16,8,128]{2,1,0:T(8,128)S(1)} %solve.1.mid), channel_id=1, source_target_pairs={{16,0},{32,16},{48,32},{64,48},{80,64},{96,80},{112,96},{17,1},{33... | collective-permute-start | bytes 196616 | tf_op jit(solution)/shard_map/ppermute | solution.py:400
  82.3 6.9 %collective-permute-start.4 = (f32[16,8,128]{2,1,0:T(8,128)S(1)}, f32[16,8,128]{2,1,0:T(8,128)S(1)}, u32[]{:S(2)}, u32[]{:S(2)}) collective-permute-start(f32[16,8,128]{2,1,0:T(8,128)S(1)} %solve.1.mid), channel_id=1, source_target_pairs={{0,16},{16,32},{32,48},{48,64},{64,80},{80,96},{96,112},{1,17},{17... | collective-permute-start | bytes 196616 | tf_op jit(solution)/shard_map/ppermute | solution.py:400

commit v3 on v2

--- a/solution.py
+++ b/solution.py
@@ -142,8 +142,8 @@
 
 def first_kernel(
     g, yp, yn, state,
-    src_w, pre_w, c_w, se, mid_pre_o, mid_rhs_o, mid_c_o, low_o,
-    c, wx, wy, wz, inv, b, va, vb, t, mc, mwx, mwy, mwz, minv, mb, mva, mvb, lc,
+    src_w, pre_w, c_w, se, mid_pre_o, mid_rhs_o, mid_c_o, low_o, block_o,
+    c, wx, wy, wz, inv, b, va, vb, t, mc, mwx, mwy, mwz, minv, mb, mva, mvb,
 ):
     gx, gz = lax.axis_index("gx"), lax.axis_index("gz")
     zero = jnp.zeros((YE, ZE), jnp.float32)
@@ -246,73 +246,148 @@
 
     lax.fori_loop(0, 16, rest, mwx[0] * (0.0 - mva[1]), unroll=16)
 
-    shape = (64, 16 * YM)
+    shape = (48, 16 * YM)
     to, frm = iota(shape, 0), iota(shape, 1)
     m, r = frm // YM, frm % YM
-    fold = ((m // 2 == to // 8) & (r // 2 - 2 == to % 8)).astype(jnp.float32) * 0.125
+    fold = ((m // 2 == to % 8) & (r // 2 - 3 == to // 8)).astype(jnp.float32) * 0.125
     m, l = iota((ZM, CZ), 0), iota((ZM, CZ), 1)
     m = jnp.where(m < 96, m, m - 128)
     squeeze = ((m + 8) // 2 == l).astype(jnp.float32)
-    rhs = mm(mm(fold, mvb[1:17].reshape(16 * YM, ZM)), squeeze).reshape(8, 8, CZ)
-    low_c = mm(mm(fold, mc[1:17].reshape(16 * YM, ZM)), squeeze).reshape(8, 8, CZ)
-    lc[0] = jnp.zeros((8, CZ), jnp.float32)
-    lc[9] = jnp.zeros((8, CZ), jnp.float32)
-    lc[1:9] = low_c
+    rhs = mm(mm(fold[8:40], mvb[1:17].reshape(16 * YM, ZM)), squeeze).reshape(4, 8, CZ)
+    low_c = mm(mm(fold, mc[1:17].reshape(16 * YM, ZM)), squeeze).reshape(6, 8, CZ)
+    here = low_c[1:5]
+    row = iota((4, 8, CZ), 1)
     scale = 0.0625
-    fx0 = scale * face(lc[0:8], low_c)
-    fx1 = scale * face(low_c, lc[2:10])
-    fy = scale * face(low_c, nxt(low_c, 1))
-    fz = (scale * ANISO) * face(low_c, nxt(low_c, 2))
+    fx1 = scale * face(here, jnp.where(row < 7, nxt(here, 1), 0.0))
+    fx0 = scale * face(here, jnp.where(row > 0, prv(here, 1), 0.0))
+    fy1 = scale * face(here, low_c[2:6])
+    fy0 = scale * face(here, low_c[0:4])
+    fz = (scale * ANISO) * face(here, nxt(here, 2))
     lower = prv(fz, 2)
-    total = fx1 + fx0 + fy + prv(fy, 1) + fz + lower
-    flags = [pltpu.roll(g[s, 16, 0:8], CZ - 16, 1) for s in range(4)]
-    flags = jnp.stack([flags[x // 2] for x in range(8)])
-    lane = iota((8, 8, CZ), 2)
-    lower = jnp.where((lane == 4) & ((flags > 0.0) | (gz == 0)), 0.0, lower)
-    packed = jnp.where(
-        lane < 32, pltpu.roll(rhs, CZ - 4, 2),
-        jnp.where(lane < 64, pltpu.roll(total, 28, 2), pltpu.roll(lower, 60, 2)),
-    )
-    packed = jnp.where(lane < 96, packed, 0.0).reshape(64, CZ)
-    to, frm = iota((32, 64), 0), iota((32, 64), 1)
-    pick = ((to // 4 == frm // 8) & (to % 4 + 2 == frm % 8)).astype(jnp.float32)
-    packed = mm(pick, packed)
-    for p in range(16):
-        low_o[p] = packed
-
-
-def solve_kernel(rec, mid_pre, out):
-    gz = lax.axis_index("gz")
-    lane = iota((32, CZ), 1)
-    parts = [[], [], []]
-    for tile in range(4):
-        pieces = [jnp.zeros((32, CZ), jnp.float32)] * 3
-        for j in range(4):
-            block = rec[4 * tile + j]
-            here = (lane >= 32 * j) & (lane < 32 * j + 32)
-            for a in range(3):
-                shift = (32 * (j - a)) % CZ
-                moved = pltpu.roll(block, shift, 1) if shift else block
-                pieces[a] = jnp.where(here, moved, pieces[a])
-        for a in range(3):
-            parts[a].append(pieces[a])
-    r, d, e = [jnp.concatenate(p, 1) for p in parts]
-    for k in range(7):
+    total = fx1 + fx0 + fy1 + fy0 + fz + lower
+
+    lane = iota((8, CZ), 1)
+    depth = lane % 32
+
+    def gather(v):
+        out = pltpu.roll(v[0], CZ - 4, 1)
+        for y in range(1, 4):
+            out = jnp.where(lane >= 32 * y, pltpu.roll(v[y], 32 * y - 4, 1), out)
+        return out
+
+    flag = pltpu.roll(g[3, 16, 0:8], CZ - 20, 1)
+    row = iota((8, CZ), 0)
+    for s in range(2, -1, -1):
+        flag = jnp.where(row < 2 * s + 2, pltpu.roll(g[s, 16, 0:8], CZ - 20, 1), flag)
+    flag = jnp.broadcast_to(flag[:, 0:1], (8, CZ))
+    r, d, e = gather(rhs), gather(total), gather(lower)
+    top = depth == 0
+    edge = jnp.where(top & (flag == 0.0) & (gz > 0), e, 0.0)
+    e = jnp.where(top, 0.0, e)
+    v = jnp.where(top, 1.0, 0.0)
+    w = jnp.where(depth == 31, 1.0, 0.0)
+    for k in range(5):
         s = 1 << k
-        back = 4 * CZ - s
+        back = CZ - s
         inv = 1.0 / d
         t = e * inv
         alpha = e * pltpu.roll(inv, s, 1)
+        r, v, w = [
+            q + alpha * pltpu.roll(q, s, 1) + pltpu.roll(t * q, back, 1) for q in (r, v, w)
+        ]
         d = d - alpha * e - pltpu.roll(t * e, back, 1)
-        r = r + alpha * pltpu.roll(r, s, 1) + pltpu.roll(t * r, back, 1)
         e = alpha * pltpu.roll(e, s, 1)
-    x = r / d
-    k, m = iota((4 * CZ, ZM), 0), iota((4 * CZ, ZM), 1)
-    m = jnp.where(m < 96, m, m - 128)
-    spread_z = (k == 32 * gz + ((m + 64) // 2 - 32)).astype(jnp.float32)
+    inv = 1.0 / d
+    r, v, w = r * inv, v * inv, w * inv
+    block_o[0] = r
+    block_o[1] = v
+    block_o[2] = w
+    packed = jnp.where((depth < 3) | (depth >= 29), r, 0.0)
+    packed = jnp.where((depth >= 3) & (depth < 6), pltpu.roll(v, 3, 1), packed)
+    packed = jnp.where((depth >= 26) & (depth < 29), pltpu.roll(v, CZ - 3, 1), packed)
+    packed = jnp.where((depth >= 6) & (depth < 9), pltpu.roll(w, 6, 1), packed)
+    packed = jnp.where((depth >= 23) & (depth < 26), pltpu.roll(w, CZ - 6, 1), packed)
+    packed = jnp.where(depth == 9, pltpu.roll(edge, 9, 1), packed)
+    for p in range(16):
+        low_o[p] = packed
+
+
+def solve_kernel(rec, block, mid_pre, out):
+    gz = lax.axis_index("gz")
+    lane = iota((8, CZ), 1)
+    depth = lane % 32
+
+    def take(v, at):
+        return pltpu.roll(v, (CZ - at) % CZ, 1) if at else v
+
+    def parts(offset):
+        p = gz + offset
+        v = rec[jnp.clip(p, 0, 15)]
+        low = take(v, 0), take(v, 3), take(v, 6)
+        high = take(v, 31), take(v, 28), take(v, 25)
+        return v, low, high, jnp.where((p >= 0) & (p <= 15), take(v, 9), 0.0)
+
+    every = {k: parts(k) for k in range(-4, 5)}
+    zero = jnp.zeros((8, CZ), jnp.float32)
+
+    a, b = {-5: zero}, {-5: zero}
+    f, g = {}, {}
+    for k in range(-4, 1):
+        _, (y0, v0, w0), (y1, v1, w1), e = every[k]
+        left, more = e * a[k - 1], e * e * b[k - 1]
+        den = 1.0 / (1.0 - v0 * more)
+        f[k] = (y0 + v0 * left) * den
+        g[k] = w0 * den
+        a[k] = y1 + v1 * (left + more * f[k])
+        b[k] = w1 + v1 * (more * g[k])
+    ra, rb = {5: zero}, {5: zero}
+    rf, rg = {}, {}
+    e_next = zero
+    for k in range(4, 0, -1):
+        _, (y0, v0, w0), (y1, v1, w1), e = every[k]
+        right, more = e_next * ra[k + 1], e_next * e_next * rb[k + 1]
+        den = 1.0 / (1.0 - w1 * more)
+        rf[k] = (y1 + w1 * right) * den
+        rg[k] = v1 * den
+        ra[k] = y0 + w0 * (right + more * rf[k])
+        rb[k] = v0 + w0 * (more * rg[k])
+        e_next = e
+    e0, e1 = every[0][3], every[1][3]
+    last = (a[0] + b[0] * e1 * ra[1]) / (1.0 - b[0] * e1 * e1 * rb[1])
+    right = e1 * (ra[1] + rb[1] * (e1 * last))
+    first = f[0] + g[0] * right
+    left = e0 * (a[-1] + b[-1] * (e0 * first))
+    before = f[-1] + g[-1] * (e0 * first)
+    em = every[-1][3]
+    left_m, right_m = em * (a[-2] + b[-2] * (em * before)), e0 * first
+    after = rf[1] + rg[1] * (e1 * last)
+    ep = every[2][3]
+    left_p, right_p = e1 * last, ep * (ra[2] + rb[2] * (ep * after))
+
+    ends = jnp.concatenate([left, right, left_m, right_m, left_p, right_p], 0)
+    ends = jnp.where(iota((48, CZ), 1) % 32 == 0, ends, 0.0)
+    copy = (iota((CZ, CZ), 1) // 32 * 32 == iota((CZ, CZ), 0)).astype(jnp.float32)
+    ends = mm(ends, copy).reshape(6, 8, CZ)
+    own = block[0] + block[1] * ends[0] + block[2] * ends[1]
+    v = every[-1][0]
+    low = v + pltpu.roll(v, 3, 1) * ends[2] + pltpu.roll(v, 6, 1) * ends[3]
+    low = jnp.where((depth >= 29) & (gz > 0), low, 0.0)
+    v = every[1][0]
+    high = v + pltpu.roll(v, CZ - 3, 1) * ends[4] + pltpu.roll(v, CZ - 6, 1) * ends[5]
+    high = jnp.where((depth < 3) & (gz < 15), high, 0.0)
+
+    rows = []
+    for y in range(4):
+        part = jnp.where(lane < 32, take(own, 32 * y), 0.0)
+        part = jnp.where((lane >= 32) & (lane < 64), take(high, (32 * y - 32) % CZ), part)
+        part = jnp.where(lane >= 96, take(low, (32 * y + 32) % CZ), part)
+        rows.append(part)
+    rows = jnp.concatenate(rows, 0)
+    k, m = iota((CZ, ZM), 0), iota((CZ, ZM), 1)
+    spread_z = (k == jnp.where(m < 96, m // 2, m // 2 + 64)).astype(jnp.float32)
     to, frm = iota((128, 32), 0), iota((128, 32), 1)
-    spread = ((to // 16 == frm // 4) & ((to % 8) // 2 == frm % 4)).astype(jnp.float32)
-    out[...] = mid_pre[...] + mm(spread, mm(x, spread_z)).reshape(16, 8, ZM)
+    spread = ((to // 16 == frm % 8) & ((to % 8) // 2 == frm // 8)).astype(jnp.float32)
+    out[...] = mid_pre[...] + mm(spread, mm(rows, spread_z)).reshape(16, 8, ZM)
 
 
 def second_kernel(
@@ -425,17 +500,17 @@
     fine, fine1, fine2 = (32, YE, ZE), (33, YE, ZE), (34, YE, ZE)
     mid, mid1, mid2 = (16, YM, ZM), (17, YM, ZM), (18, YM, ZM)
     win, win1, win2 = (XW, YW, ZE), (XW + 1, YW, ZE), (XW + 2, YW, ZE)
-    src_w, pre_w, c_w, se, mid_pre, mid_rhs, mid_c, low = pl.pallas_call(
+    src_w, pre_w, c_w, se, mid_pre, mid_rhs, mid_c, low, block_s = pl.pallas_call(
         first_kernel,
         out_shape=(
             f32(*win), f32(*win), f32(*win), f32(CX + 2, YW, ZE),
-            f32(16, 8, ZM), f32(*mid), f32(*mid), f32(16, 32, CZ),
+            f32(16, 8, ZM), f32(*mid), f32(*mid), f32(16, 8, CZ), f32(3, 8, CZ),
         ),
         scratch_shapes=[
             vm(*fine2), vm(*fine1), vm(*fine), vm(*fine), vm(*fine), vm(*fine),
             vm(*fine2), vm(*fine2), vm(32, YM, ZE),
             vm(*mid2), vm(*mid1), vm(*mid), vm(*mid), vm(*mid), vm(*mid),
-            vm(*mid2), vm(*mid2), vm(10, 8, CZ),
+            vm(*mid2), vm(*mid2),
         ],
         compiler_params=params(),
         name="first",
@@ -444,7 +519,7 @@
     rec = lax.all_to_all(low, "gz", 0, 0, tiled=True)
     mid_init = pl.pallas_call(
         solve_kernel, out_shape=f32(16, 8, ZM), compiler_params=params(), name="solve"
-    )(rec, mid_pre)
+    )(rec, block_s, mid_pre)
     mid_p, mid_n = both_ways(mid_init, mid_init, "gy")
 
     adj, grad = pl.pallas_call(

time: 104 us -> 99.9 us (0.961)
  blocking collectives: 52.2 us -> 48.9 us
    all_to_all x1, blocking collectives: 29.2 us -> 25.3 us  [per_device(): rec = lax.all_to_all(low, 'gz', 0, 0, tiled=True)]
where the time goes in v3:
time: 99.9 us; the launch traced here: 99.6 us
  blocking collectives  48.9 us (49%)
  Pallas kernels  16.9 us (17%)
  starting transfers between devices  16.4 us (16%)
  waiting for transfers between devices  15.5 us (16%)
  other arithmetic  1.17 us (1%)
    all_to_all x1, blocking collectives, per_device(): rec = lax.all_to_all(low, 'gz', 0, 0, tiled=True)  25.3 us
    ppermute x4, starting transfers between devices, both_ways(): return (lax.ppermute(up, axis, higher), lax.ppermute(down, axis, lower))  13.7 us
    all_gather x1, blocking collectives, per_device(): g = lax.all_gather(mine, 'gx')  12.5 us
    ppermute x4, waiting for transfers between devices, both_ways(): return (lax.ppermute(up, axis, higher), lax.ppermute(down, axis, lower))  11.6 us
    all_to_all x1, blocking collectives, per_device(): sums = lax.all_to_all(grad, 'gz', 0, 0, tiled=True)  11 us
    pallas_call x1, Pallas kernels, per_device(): pl.pallas_call(first_kernel, out_shape=(f32(*win), f32(*win), f32(*win),...  10.5 us
    pallas_call x1, Pallas kernels, per_device(): pl.pallas_call(second_kernel, out_shape=(block, f32(CY, CZ)), scratch_sha...  3.57 us
    ppermute x1, starting transfers between devices, per_device(): lax.ppermute(up, 'gz', [(i, (i + 1) % count) for i in range(count)])  2.65 us
  transfers between devices with their start and end apart: 6, of which 5 were waited for; matrix products, arithmetic and copies ran while one was open for 0% of the time, Pallas kernels for 0%

profile of v3, /device:TPU:33, one launch (start us, length us, event | category | flops | bytes accessed | tf_op | source)
XLA Modules:
  0.0 99.6 jit_solution(4614557995346235148)
XLA Ops:
  0.6 1.9 %pack_z.1 = (f32[26,16,128]{2,1,0:T(8,128)}, f32[8,16,128]{2,1,0:T(8,128)}, f32[8,16,128]{2,1,0:T(8,128)}) custom-call(s32[16]{0:T(128)} %bitcast.13, f32[8,16,128]{2,1,0:T(8,128)} %src.1, f32[8,16,128]{2,1,0:T(8,128)} %log_coef.1, f32[8,16]{1,0:T(8,128)} %lateral.1, f32[8,16,128]{2,1,0:T(8,128)} %state.5), custom_call_target="tpu_custom_call" | custom-call | tf_op jit(solution)/shard_map/pack_z/pallas_call | solution.py:482
  2.6 2.7 %collective-permute-start = (f32[8,16,128]{2,1,0:T(8,128)}, f32[8,16,128]{2,1,0:T(8,128)S(1)}, u32[]{:S(2)}, u32[]{:S(2)}) collective-permute-start(f32[8,16,128]{2,1,0:T(8,128)} %get-tuple-element.19), channel_id=1, source_target_pairs={{0,1},{1,2},{2,3},{3,4},{4,5},{5,6},{6,7},{7,8},{8,9},{9,10},{10,1... | collective-permute-start | bytes 196616 | tf_op jit(solution)/shard_map/ppermute | solution.py:489
  5.2 0.0 collective-permute-start.1
  5.2 1.6 %collective-permute-done = f32[8,16,128]{2,1,0:T(8,128)S(1)} collective-permute-done((f32[8,16,128]{2,1,0:T(8,128)}, f32[8,16,128]{2,1,0:T(8,128)S(1)}, u32[]{:S(2)}, u32[]{:S(2)}) %collective-permute-start) | collective-permute-done | bytes 65568 | tf_op jit(solution)/shard_map/ppermute | solution.py:489
  6.9 2.3 %collective-permute-done.1 = f32[8,16,128]{2,1,0:T(8,128)S(1)} collective-permute-done((f32[8,16,128]{2,1,0:T(8,128)}, f32[8,16,128]{2,1,0:T(8,128)S(1)}, u32[]{:S(2)}, u32[]{:S(2)}) %collective-permute-start.1) | collective-permute-done | bytes 65568 | tf_op jit(solution)/shard_map/ppermute | solution.py:490
  9.1 0.6 bitcast_dynamic-update-slice_fusion
  9.7 0.0 copy-start
  9.7 12.5 %all_gather.10.g = f32[4,26,16,128]{3,2,1,0:T(8,128)S(1)} all-gather(f32[1,26,16,128]{3,2,1,0:T(8,128)} %bitcast_dynamic-update-slice_fusion), channel_id=1, replica_groups=mesh['gx'=4,'gy'=8,'gz'=16] {'gx'}, dimensions={0}, use_global_device_ids=true | all-gather | bytes 1064960 | tf_op jit(solution)/shard_map/all_gather | solution.py:493
  22.3 0.0 copy-done
  22.3 0.1 pack_y.1
  22.4 2.3 %collective-permute-start.2 = (f32[52,24,128]{2,1,0:T(8,128)S(1)}, f32[52,24,128]{2,1,0:T(8,128)S(1)}, u32[]{:S(2)}, u32[]{:S(2)}) collective-permute-start(f32[52,24,128]{2,1,0:T(8,128)S(1)} %get-tuple-element.21), channel_id=1, source_target_pairs={{0,16},{16,32},{32,48},{48,64},{64,80},{80,96},{96,112},{1,17},{17... | collective-permute-start | bytes 1916936 | tf_op jit(solution)/shard_map/ppermute | solution.py:475
  24.7 4.2 %collective-permute-start.3 = (f32[52,24,128]{2,1,0:T(8,128)S(1)}, f32[52,24,128]{2,1,0:T(8,128)S(1)}, u32[]{:S(2)}, u32[]{:S(2)}) collective-permute-start(f32[52,24,128]{2,1,0:T(8,128)S(1)} %get-tuple-element.22), channel_id=1, source_target_pairs={{16,0},{32,16},{48,32},{64,48},{80,64},{96,80},{112,96},{17,1},{33... | collective-permute-start | bytes 1916936 | tf_op jit(solution)/shard_map/ppermute | solution.py:475
  28.9 5.9 %collective-permute-done.2.yp = f32[52,24,128]{2,1,0:T(8,128)S(1)} collective-permute-done((f32[52,24,128]{2,1,0:T(8,128)S(1)}, f32[52,24,128]{2,1,0:T(8,128)S(1)}, u32[]{:S(2)}, u32[]{:S(2)}) %collective-permute-start.2) | collective-permute-done | bytes 639008 | tf_op jit(solution)/shard_map/ppermute | solution.py:475
  34.7 1.5 %collective-permute-done.3.yn = f32[52,24,128]{2,1,0:T(8,128)S(1)} collective-permute-done((f32[52,24,128]{2,1,0:T(8,128)S(1)}, f32[52,24,128]{2,1,0:T(8,128)S(1)}, u32[]{:S(2)}, u32[]{:S(2)}) %collective-permute-start.3) | collective-permute-done | bytes 639008 | tf_op jit(solution)/shard_map/ppermute | solution.py:475
  36.2 10.5 %first.1 = (f32[16,24,256]{2,1,0:T(8,128)S(1)}, f32[16,24,256]{2,1,0:T(8,128)S(1)}, f32[16,24,256]{2,1,0:T(8,128)S(1)}, f32[10,24,256]{2,1,0:T(8,128)S(1)}, f32[...) custom-call(f32[4,26,16,128]{3,2,1,0:T(8,128)S(1)} %all_gather.10.g,, ...), custom_call_target="tpu_custom_call" | custom-call | tf_op jit(solution)/shard_map/first/pallas_call | solution.py:503
  46.7 25.3 %all_to_all.17.rec = f32[16,8,128]{2,1,0:T(8,128)S(1)} all-to-all(f32[16,8,128]{2,1,0:T(8,128)S(1)} %get-tuple-element.23), channel_id=1, replica_groups=mesh['gx'=4,'gy'=8,'gz'=16] {'gz'}, dimensions={0} | all-to-all | bytes 131072 | tf_op jit(solution)/shard_map/all_to_all | solution.py:519
  72.0 0.8 solve.1.mid
  72.9 5.3 %collective-permute-start.5 = (f32[16,8,128]{2,1,0:T(8,128)S(1)}, f32[16,8,128]{2,1,0:T(8,128)S(1)}, u32[]{:S(2)}, u32[]{:S(2)}) collective-permute-start(f32[16,8,128]{2,1,0:T(8,128)S(1)} %solve.1.mid), channel_id=1, source_target_pairs={{16,0},{32,16},{48,32},{64,48},{80,64},{96,80},{112,96},{17,1},{33... | collective-permute-start | bytes 196616 | tf_op jit(solution)/shard_map/ppermute | solution.py:475
  78.2 1.9 %collective-permute-start.4 = (f32[16,8,128]{2,1,0:T(8,128)S(1)}, f32[16,8,128]{2,1,0:T(8,128)S(1)}, u32[]{:S(2)}, u32[]{:S(2)}) collective-permute-start(f32[16,8,128]{2,1,0:T(8,128)S(1)} %solve.1.mid), channel_id=1, source_target_pairs={{0,16},{16,32},{32,48},{48,64},{64,80},{80,96},{96,112},{1,17},{17... | collective-permute-start | bytes 196616 | tf_op jit(solution)/shard_map/ppermute | solution.py:475
  80.1 0.0 collective-permute-done.5.mid_n
  80.1 4.3 %collective-permute-done.4.mid_p = f32[16,8,128]{2,1,0:T(8,128)S(1)} collective-permute-done((f32[16,8,128]{2,1,0:T(8,128)S(1)}, f32[16,8,128]{2,1,0:T(8,128)S(1)}, u32[]{:S(2)}, u32[]{:S(2)}) %collective-permute-start.4) | collective-permute-done | bytes 65568 | tf_op jit(solution)/shard_map/ppermute | solution.py:475
  84.4 3.6 %second.1 = (f32[8,16,128]{2,1,0:T(8,128)}, f32[16,128]{1,0:T(8,128)S(1)}) custom-call(f32[16,8,128]{2,1,0:T(8,128)S(1)} %solve.1.mid, f32[16,8,128]{2,1,0:T(8,128)S(1)} %collective-permute-done.4.mid_p, f32[16,8,128]{2,1,0:T(8,128)S(1)} %collective-permute-done.5.mid_n, f32[16,24,128]{2,1,0:T(8,128)S(1)} %get-tuple-element.26.mid_rhs, ...), custom_call_target="tpu_custom_call" | custom-call | tf_op jit(solution)/shard_map/second/pallas_call | solution.py:525
  88.0 11.0 %all_to_all.18 = f32[16,1,128]{2,1,0:T(1,128)S(1)} all-to-all(f32[16,1,128]{2,1,0:T(1,128)S(1)} %bitcast.10), channel_id=1, replica_groups=mesh['gx'=4,'gy'=8,'gz'=16] {'gz'}, dimensions={0} | all-to-all | bytes 16384 | tf_op jit(solution)/shard_map/all_to_all | solution.py:536
  99.0 0.5 multiply_bitcast_fusion
  (1 shorter events, 0.0 us)
Async XLA Ops:
  2.6 4.3 %collective-permute-start = (f32[8,16,128]{2,1,0:T(8,128)}, f32[8,16,128]{2,1,0:T(8,128)S(1)}, u32[]{:S(2)}, u32[]{:S(2)}) collective-permute-start(f32[8,16,128]{2,1,0:T(8,128)} %get-tuple-element.19), channel_id=1, source_target_pairs={{0,1},{1,2},{2,3},{3,4},{4,5},{5,6},{6,7},{7,8},{8,9},{9,10},{10,1... | collective-permute-start | bytes 196616 | tf_op jit(solution)/shard_map/ppermute | solution.py:489
  5.2 3.9 %collective-permute-start.1 = (f32[8,16,128]{2,1,0:T(8,128)}, f32[8,16,128]{2,1,0:T(8,128)S(1)}, u32[]{:S(2)}, u32[]{:S(2)}) collective-permute-start(f32[8,16,128]{2,1,0:T(8,128)} %get-tuple-element.20), channel_id=1, source_target_pairs={{0,15},{1,0},{2,1},{3,2},{4,3},{5,4},{6,5},{7,6},{8,7},{9,8},{10,9... | collective-permute-start | bytes 196616 | tf_op jit(solution)/shard_map/ppermute | solution.py:490
  9.7 12.5 %copy-start = (f32[8,16,128]{2,1,0:T(8,128)S(1)}, f32[8,16,128]{2,1,0:T(8,128)}, u32[]{:S(2)}) copy-start(f32[8,16,128]{2,1,0:T(8,128)} %state.5) | copy-start | bytes 196612
  22.4 12.4 %collective-permute-start.2 = (f32[52,24,128]{2,1,0:T(8,128)S(1)}, f32[52,24,128]{2,1,0:T(8,128)S(1)}, u32[]{:S(2)}, u32[]{:S(2)}) collective-permute-start(f32[52,24,128]{2,1,0:T(8,128)S(1)} %get-tuple-element.21), channel_id=1, source_target_pairs={{0,16},{16,32},{32,48},{48,64},{64,80},{80,96},{96,112},{1,17},{17... | collective-permute-start | bytes 1916936 | tf_op jit(solution)/shard_map/ppermute | solution.py:475
  24.7 11.5 %collective-permute-start.3 = (f32[52,24,128]{2,1,0:T(8,128)S(1)}, f32[52,24,128]{2,1,0:T(8,128)S(1)}, u32[]{:S(2)}, u32[]{:S(2)}) collective-permute-start(f32[52,24,128]{2,1,0:T(8,128)S(1)} %get-tuple-element.22), channel_id=1, source_target_pairs={{16,0},{32,16},{48,32},{64,48},{80,64},{96,80},{112,96},{17,1},{33... | collective-permute-start | bytes 1916936 | tf_op jit(solution)/shard_map/ppermute | solution.py:475
  72.9 7.3 %collective-permute-start.5 = (f32[16,8,128]{2,1,0:T(8,128)S(1)}, f32[16,8,128]{2,1,0:T(8,128)S(1)}, u32[]{:S(2)}, u32[]{:S(2)}) collective-permute-start(f32[16,8,128]{2,1,0:T(8,128)S(1)} %solve.1.mid), channel_id=1, source_target_pairs={{16,0},{32,16},{48,32},{64,48},{80,64},{96,80},{112,96},{17,1},{33... | collective-permute-start | bytes 196616 | tf_op jit(solution)/shard_map/ppermute | solution.py:475
  78.2 6.2 %collective-permute-start.4 = (f32[16,8,128]{2,1,0:T(8,128)S(1)}, f32[16,8,128]{2,1,0:T(8,128)S(1)}, u32[]{:S(2)}, u32[]{:S(2)}) collective-permute-start(f32[16,8,128]{2,1,0:T(8,128)S(1)} %solve.1.mid), channel_id=1, source_target_pairs={{0,16},{16,32},{32,48},{48,64},{64,80},{80,96},{96,112},{1,17},{17... | collective-permute-start | bytes 196616 | tf_op jit(solution)/shard_map/ppermute | solution.py:475

commit v4 on v3

--- a/solution.py
+++ b/solution.py
@@ -10,9 +10,10 @@
 CX, CY, CZ = 8, 16, 128
 ANISO = 200.0
 OMEGA = 0.8
-HY = 12
+HY = 10
+Y0 = 12
 HZ = 18
-YE = CY + 2 * HY
+YE = CY + 2 * Y0
 ZE = 2 * CZ
 YM = 24
 ZM = CZ
@@ -108,67 +109,161 @@
     up[...] = jnp.where(lane >= far, s, jnp.where(lane == 31, t, coef))
 
 
-def pack_y_kernel(g, state, up, down):
-    row = iota((24, CZ), 0)
-
-    def put(at, one, two):
-        zero = jnp.zeros((8, CZ), jnp.float32)
-        one = jnp.concatenate([one, zero], 0)
-        two = jnp.concatenate([two, zero], 0)
-        up[at] = jnp.where(row < HY, pltpu.roll(one, 20, 0), pltpu.roll(two, 8, 0))
-        down[at] = jnp.where(row < HY, one, pltpu.roll(two, 12, 0))
+def pack_y_kernel(g, state, c_up, c_down, s_up, s_down):
+    def put(up, down, n, plane):
+        at = pl.ds(HY * (n % 4), HY)
+        up[n // 4, at] = plane[CY - HY :]
+        down[n // 4, at] = plane[:HY]
 
     for s in range(4):
-        for k in range(12):
-            put(12 * s + k, g[s, 2 * k], g[s, 2 * k + 1])
-    for k in range(4):
-        put(48 + k, state[2 * k], state[2 * k + 1])
-
-
-def rows_of(yp, own, yn, odd):
-    row = iota((YE, CZ), 0)
-    zero16 = jnp.zeros((16, CZ), jnp.float32)
-    zero24 = jnp.zeros((24, CZ), jnp.float32)
-    low = jnp.concatenate([yp, zero16], 0)
-    high = jnp.concatenate([yn, zero16], 0)
-    mid = pltpu.roll(jnp.concatenate([own, zero24], 0), HY, 0)
-    if odd:
-        low = pltpu.roll(low, YE - HY, 0)
-        high = pltpu.roll(high, HY + CY - HY, 0)
-    else:
-        high = pltpu.roll(high, HY + CY, 0)
-    return jnp.where(row < HY, low, jnp.where(row < HY + CY, mid, high))
-
-
-def first_kernel(
-    g, yp, yn, state,
-    src_w, pre_w, c_w, se, mid_pre_o, mid_rhs_o, mid_c_o, low_o, block_o,
-    c, wx, wy, wz, inv, b, va, vb, t, mc, mwx, mwy, mwz, minv, mb, mva, mvb,
+        for i in range(2 * CX):
+            put(c_up, c_down, 2 * CX * s + i, g[s, CX + i])
+        for i in range(CX):
+            put(s_up, s_down, CX * s + i, g[s, i])
+    for i in range(CX):
+        put(s_up, s_down, 4 * CX + i, state[i])
+
+
+def place(out, lanes, n, low, own, high, change):
+    at = pl.ds(HY * (n % 4), HY)
+    out[Y0 - HY : Y0, lanes] = change(low[n // 4, at])
+    out[Y0 : Y0 + CY, lanes] = change(own)
+    out[Y0 + CY : Y0 + CY + HY, lanes] = change(high[n // 4, at])
+
+
+def edge_lanes(v):
+    lane = iota(v.shape, 1)
+    return jnp.where((lane < HZ) | (lane >= CZ - HZ), v, 0.0)
+
+
+LOW, HIGH = slice(0, CZ), slice(CZ, ZE)
+
+
+def window(gx, pairs, planes):
+    nx = 4 * CX
+
+    def keep(w, carry):
+        for out, ref, shift, first in pairs:
+            x = CX * gx - 4 + w - first
+            inside = (x >= -first) & (x < nx)
+            at = jnp.clip(x, -first, nx - 1) + shift
+            out[w] = jnp.where(inside, ref[at, 8:32], 0.0)
+        return carry
+
+    lax.fori_loop(0, planes, keep, 0, unroll=4)
+
+
+def fold_y():
+    return (iota((YM, YE), 1) // 2 + 2 == iota((YM, YE), 0)).astype(jnp.float32)
+
+
+def fold_z():
+    return (iota((ZE, ZM), 0) // 2 == iota((ZE, ZM), 1)).astype(jnp.float32) * 0.125
+
+
+def fold_low(first, count):
+    shape = (8 * count, 16 * YM)
+    to, frm = iota(shape, 0), iota(shape, 1)
+    m, r = frm // YM, frm % YM
+    return ((m // 2 == to % 8) & (r // 2 - 4 == to // 8 + first)).astype(jnp.float32) * 0.125
+
+
+def squeeze():
+    m, l = iota((ZM, CZ), 0), iota((ZM, CZ), 1)
+    m = jnp.where(m < 96, m, m - 128)
+    return ((m + 8) // 2 == l).astype(jnp.float32)
+
+
+def gather(v):
+    lane = iota((8, CZ), 1)
+    out = pltpu.roll(v[0], CZ - 4, 1)
+    for y in range(1, 4):
+        out = jnp.where(lane >= 32 * y, pltpu.roll(v[y], 32 * y - 4, 1), out)
+    return out
+
+
+def coef_kernel(
+    g, yp, yn,
+    wx, wy, wz, inv, c_w, wx_w, wy_w, wz_w, inv_w, mwx, mwy, mwz, minv, low_o,
+    c, t, mc,
 ):
     gx, gz = lax.axis_index("gx"), lax.axis_index("gz")
     zero = jnp.zeros((YE, ZE), jnp.float32)
     nx = 4 * CX
-    for ref in (c, va, vb):
+    c[0] = zero
+    c[nx + 1] = zero
+    none = jnp.zeros((8, ZE), jnp.float32)
+    for s in range(4):
+        for i in range(CX):
+            out = c.at[CX * s + i + 1]
+            out[0:8] = none
+            out[YE - 8 :] = none
+            n = 2 * CX * s + i
+            place(out, LOW, n, yp, g[s, CX + i], yn, lambda v: v)
+            place(
+                out, HIGH, n + CX, yp, g[s, 2 * CX + i], yn,
+                lambda v: edge_lanes(pltpu.roll(v, 64, 1)),
+            )
+    make_weights(c, wx, wy, wz, inv, nx, 1.0)
+    rows = fold_y()
+
+    def coarse(m, carry):
+        t[m] = mm(rows, c[2 * m + 1] + c[2 * m + 2])
+        return carry
+
+    lax.fori_loop(0, 16, coarse, 0, unroll=8)
+    mid_zero = jnp.zeros((YM, ZM), jnp.float32)
+    mc[0] = mid_zero
+    mc[17] = mid_zero
+    mc[1:17] = mm(t[...].reshape(16 * YM, ZE), fold_z()).reshape(16, YM, ZM)
+    make_weights(mc, mwx, mwy, mwz, minv, 16, 0.25)
+    window(gx, [(c_w, c, 1, 0), (wy_w, wy, 0, 0), (wz_w, wz, 0, 0), (inv_w, inv, 0, 0)], XW)
+    window(gx, [(wx_w, wx, 1, 1)], XW + 1)
+
+    low_c = mm(mm(fold_low(-1, 6), mc[1:17].reshape(16 * YM, ZM)), squeeze())
+    low_c = low_c.reshape(6, 8, CZ)
+    here = low_c[1:5]
+    row = iota((4, 8, CZ), 1)
+    scale = 0.0625
+    fx1 = scale * face(here, jnp.where(row < 7, nxt(here, 1), 0.0))
+    fx0 = scale * face(here, jnp.where(row > 0, prv(here, 1), 0.0))
+    fy1 = scale * face(here, low_c[2:6])
+    fy0 = scale * face(here, low_c[0:4])
+    fz = (scale * ANISO) * face(here, nxt(here, 2))
+    lower = prv(fz, 2)
+    total = fx1 + fx0 + fy1 + fy0 + fz + lower
+
+    flag = pltpu.roll(g[3, 16, 0:8], CZ - 20, 1)
+    row = iota((8, CZ), 0)
+    for s in range(2, -1, -1):
+        flag = jnp.where(row < 2 * s + 2, pltpu.roll(g[s, 16, 0:8], CZ - 20, 1), flag)
+    flag = jnp.broadcast_to(flag[:, 0:1], (8, CZ))
+    e = gather(lower)
+    top = iota((8, CZ), 1) % 32 == 0
+    low_o[0] = gather(total)
+    low_o[1] = jnp.where(top, 0.0, e)
+    low_o[2] = jnp.where(top & (flag == 0.0) & (gz > 0), e, 0.0)
+
+
+def first_kernel(
+    g, cp, cn, yp, yn, state, wx, wy, wz, inv, mwx, mwy, mwz, minv, low,
+    src_w, pre_w, se, mid_pre_o, mb, low_o, block_o,
+    b, va, vb, t, mva, mvb,
+):
+    gx = lax.axis_index("gx")
+    zero = jnp.zeros((YE, ZE), jnp.float32)
+    nx = 4 * CX
+    for ref in (va, vb):
         ref[0] = zero
         ref[nx + 1] = zero
-    lane = iota((YE, CZ), 1)
-    edge = (lane < HZ) | (lane >= CZ - HZ)
-
+    none = jnp.zeros((8, ZE), jnp.float32)
     for s in range(4):
-        for i in range(0, CX, 2):
-            for odd in (0, 1):
-                x = CX * s + i + odd
-                near = [
-                    rows_of(yp[12 * s + (a * CX + i) // 2], g[s, a * CX + i + odd],
-                            yn[12 * s + (a * CX + i) // 2], odd)
-                    for a in range(3)
-                ]
-                halo = near[2]
-                b[x] = jnp.concatenate([near[0], jnp.where(edge, halo, 0.0)], 1)
-                other = pltpu.roll(halo, 64, 1)
-                c[x + 1] = jnp.concatenate([near[1], jnp.where(edge, other, 0.0)], 1)
-
-    make_weights(c, wx, wy, wz, inv, nx, 1.0)
+        for i in range(CX):
+            out = b.at[CX * s + i]
+            out[0:8] = none
+            out[YE - 8 :] = none
+            place(out, LOW, CX * s + i, yp, g[s, i], yn, lambda v: v)
+            place(out, HIGH, 2 * CX * s + CX + i, cp, g[s, 2 * CX + i], cn, edge_lanes)
 
     def start(x, carry):
         va[x + 1] = inv[x] * b[x]
@@ -178,38 +273,23 @@
     sweep(va, vb, b, wx, wy, wz, inv, nx)
     sweep(vb, va, b, wx, wy, wz, inv, nx)
 
-    fold_y = (iota((YM, YE), 1) // 2 + 2 == iota((YM, YE), 0)).astype(jnp.float32)
-    fold_z = (iota((ZE, ZM), 0) // 2 == iota((ZE, ZM), 1)).astype(jnp.float32) * 0.125
+    rows = fold_y()
 
     def coarse(m, before):
         x = 2 * m
         _, one, fx = residual(va, b, wx, wy, wz, x, before)
         _, two, fx = residual(va, b, wx, wy, wz, x + 1, fx)
-        t[m] = mm(fold_y, one + two)
-        t[m + 16] = mm(fold_y, c[x + 1] + c[x + 2])
+        t[m] = mm(rows, one + two)
         return fx
 
     lax.fori_loop(0, 16, coarse, wx[0] * (0.0 - va[1]), unroll=8)
-    both = mm(t[...].reshape(32 * YM, ZE), fold_z).reshape(32, YM, ZM)
-    mb[...] = both[:16]
-    mid_rhs_o[...] = both[:16]
+    mb[...] = mm(t[...].reshape(16 * YM, ZE), fold_z()).reshape(16, YM, ZM)
     mid_zero = jnp.zeros((YM, ZM), jnp.float32)
-    for ref in (mc, mva, mvb):
+    for ref in (mva, mvb):
         ref[0] = mid_zero
         ref[17] = mid_zero
-    mc[1:17] = both[16:]
-    mid_c_o[...] = both[16:]
-
-    def keep(w, carry):
-        x = CX * gx - 4 + w
-        inside = (x >= 0) & (x < nx)
-        x = jnp.clip(x, 0, nx - 1)
-        src_w[w] = jnp.where(inside, b[x, 8:32], 0.0)
-        pre_w[w] = jnp.where(inside, va[x + 1, 8:32], 0.0)
-        c_w[w] = jnp.where(inside, c[x + 1, 8:32], 0.0)
-        return carry
-
-    lax.fori_loop(0, XW, keep, 0, unroll=4)
+
+    window(gx, [(src_w, b, 0, 0), (pre_w, va, 1, 0)], XW)
 
     zero8 = jnp.zeros((8, CZ), jnp.float32)
     wide = jnp.zeros((YW, CZ), jnp.float32)
@@ -224,16 +304,15 @@
         se[at] = jnp.concatenate([mid, wide], 1)
     for i in range(CX):
         mid = pltpu.roll(jnp.concatenate([state[i], zero8], 0), 4, 0)
-        low, high = yp[48 + i // 2], yn[48 + i // 2]
-        low = pltpu.roll(low, (3 - 11 - 12 * (i % 2)) % 24, 0)
-        high = pltpu.roll(high, (20 - 12 * (i % 2)) % 24, 0)
-        mid = jnp.where(row == 3, low, jnp.where(row == 20, high, mid))
+        n = 4 * CX + i
+        at = HY * (n % 4)
+        under, over = yp[n // 4, at + HY - 1 : at + HY], yn[n // 4, at : at + 1]
+        mid = jnp.where(row == 3, under, jnp.where(row == 20, over, mid))
         halo = pltpu.roll(jnp.concatenate([g[gx, 16 + i], zero8], 0), 4, 0)
         halo = pltpu.roll(halo, CZ - 32, 1)
         halo = jnp.where((lane == 0) | (lane == CZ - 1), halo, 0.0)
         se[i + 1] = jnp.concatenate([mid, halo], 1)
 
-    make_weights(mc, mwx, mwy, mwz, minv, 16, 0.25)
     mva[1:17] = minv[...] * mb[...]
     sweep(mva, mvb, mb, mwx, mwy, mwz, minv, 16)
     sweep(mvb, mva, mb, mwx, mwy, mwz, minv, 16)
@@ -246,44 +325,10 @@
 
     lax.fori_loop(0, 16, rest, mwx[0] * (0.0 - mva[1]), unroll=16)
 
-    shape = (48, 16 * YM)
-    to, frm = iota(shape, 0), iota(shape, 1)
-    m, r = frm // YM, frm % YM
-    fold = ((m // 2 == to % 8) & (r // 2 - 3 == to // 8)).astype(jnp.float32) * 0.125
-    m, l = iota((ZM, CZ), 0), iota((ZM, CZ), 1)
-    m = jnp.where(m < 96, m, m - 128)
-    squeeze = ((m + 8) // 2 == l).astype(jnp.float32)
-    rhs = mm(mm(fold[8:40], mvb[1:17].reshape(16 * YM, ZM)), squeeze).reshape(4, 8, CZ)
-    low_c = mm(mm(fold, mc[1:17].reshape(16 * YM, ZM)), squeeze).reshape(6, 8, CZ)
-    here = low_c[1:5]
-    row = iota((4, 8, CZ), 1)
-    scale = 0.0625
-    fx1 = scale * face(here, jnp.where(row < 7, nxt(here, 1), 0.0))
-    fx0 = scale * face(here, jnp.where(row > 0, prv(here, 1), 0.0))
-    fy1 = scale * face(here, low_c[2:6])
-    fy0 = scale * face(here, low_c[0:4])
-    fz = (scale * ANISO) * face(here, nxt(here, 2))
-    lower = prv(fz, 2)
-    total = fx1 + fx0 + fy1 + fy0 + fz + lower
-
-    lane = iota((8, CZ), 1)
-    depth = lane % 32
-
-    def gather(v):
-        out = pltpu.roll(v[0], CZ - 4, 1)
-        for y in range(1, 4):
-            out = jnp.where(lane >= 32 * y, pltpu.roll(v[y], 32 * y - 4, 1), out)
-        return out
-
-    flag = pltpu.roll(g[3, 16, 0:8], CZ - 20, 1)
-    row = iota((8, CZ), 0)
-    for s in range(2, -1, -1):
-        flag = jnp.where(row < 2 * s + 2, pltpu.roll(g[s, 16, 0:8], CZ - 20, 1), flag)
-    flag = jnp.broadcast_to(flag[:, 0:1], (8, CZ))
-    r, d, e = gather(rhs), gather(total), gather(lower)
+    rhs = mm(mm(fold_low(0, 4), mvb[1:17].reshape(16 * YM, ZM)), squeeze()).reshape(4, 8, CZ)
+    depth = iota((8, CZ), 1) % 32
     top = depth == 0
-    edge = jnp.where(top & (flag == 0.0) & (gz > 0), e, 0.0)
-    e = jnp.where(top, 0.0, e)
+    r, d, e, edge = gather(rhs), low[0], low[1], low[2]
     v = jnp.where(top, 1.0, 0.0)
     w = jnp.where(depth == 31, 1.0, 0.0)
     for k in range(5):
@@ -312,7 +357,7 @@
         low_o[p] = packed
 
 
-def solve_kernel(rec, block, mid_pre, out):
+def solve_kernel(rec, block, mid_pre, mid_rhs, out, up, down):
     gz = lax.axis_index("gz")
     lane = iota((8, CZ), 1)
     depth = lane % 32
@@ -387,36 +432,39 @@
     spread_z = (k == jnp.where(m < 96, m // 2, m // 2 + 64)).astype(jnp.float32)
     to, frm = iota((128, 32), 0), iota((128, 32), 1)
     spread = ((to // 16 == frm % 8) & ((to % 8) // 2 == frm // 8)).astype(jnp.float32)
-    out[...] = mid_pre[...] + mm(spread, mm(rows, spread_z)).reshape(16, 8, ZM)
+    mid = mid_pre[...] + mm(spread, mm(rows, spread_z)).reshape(16, 8, ZM)
+    out[...] = mid
+    row = iota((16, 8, ZM), 1)
+    rest = pltpu.roll(mid_rhs[:, 8:16], 4, 1)
+    up[...] = jnp.where(row == 0, rest, mid)
+    down[...] = jnp.where(row == 7, rest, mid)
 
 
 def second_kernel(
-    mid, mid_p, mid_n, mid_rhs, mid_c, src_w, pre_w, c_w, se,
+    mid, mid_p, mid_n, mid_rhs, mwx, mwy, mwz, minv, src_w, pre_w, c, wx, wy, wz, inv, se,
     adj, grad,
-    mc, mwx, mwy, mwz, minv, mva, mvb, sp, c, wx, wy, wz, inv, va, vb,
+    mb, mva, mvb, sp, va, vb,
 ):
     gx = lax.axis_index("gx")
     mid_zero = jnp.zeros((YM, ZM), jnp.float32)
-    mc[0] = mid_zero
-    mc[17] = mid_zero
-    mc[1:17] = mid_c[...]
-    make_weights(mc, mwx, mwy, mwz, minv, 16, 0.25)
+    row = iota((YM, ZM), 0)
+    for x in range(16):
+        out = jnp.concatenate([pltpu.roll(v, 4, 0) for v in (mid_p[x], mid[x], mid_n[x])], 0)
+        mb[x] = jnp.where((row == 4) | (row == 19), out, mid_rhs[x])
     for ref in (mva, mvb):
         for at in (0, 1, 18, 19):
             ref[at] = mid_zero
     for x in range(16):
         mva[x + 2] = jnp.concatenate([mid_p[x], mid[x], mid_n[x]], 0)
     a, o = mva.at[1:19], mvb.at[1:19]
-    sweep(a, o, mid_rhs, mwx, mwy, mwz, minv, 16)
-    sweep(o, a, mid_rhs, mwx, mwy, mwz, minv, 16)
-    sweep(a, o, mid_rhs, mwx, mwy, mwz, minv, 16)
+    sweep(a, o, mb, mwx, mwy, mwz, minv, 16)
+    sweep(o, a, mb, mwx, mwy, mwz, minv, 16)
+    sweep(a, o, mb, mwx, mwy, mwz, minv, 16)
 
     zero = jnp.zeros((YW, ZE), jnp.float32)
-    for ref in (c, va, vb):
+    for ref in (va, vb):
         ref[0] = zero
         ref[XW + 1] = zero
-    c[1 : XW + 1] = c_w[...]
-    make_weights(c, wx, wy, wz, inv, XW, 1.0)
     spread_z = (iota((ZM, ZE), 1) // 2 == iota((ZM, ZE), 0)).astype(jnp.float32)
     spread_y = ((iota((YW, YM), 0) + 12) // 2 == iota((YW, YM), 1)).astype(jnp.float32)
     near = mvb[pl.ds(4 * gx, 8)]
@@ -439,8 +487,8 @@
 
     def terms(i, carry):
         before, acc = carry
-        v, k, s = vb[i + 5], c[i + 5], se[i + 1]
-        px = product(half(k, c[i + 6]), v, vb[i + 6], s, se[i + 2])
+        v, k, s = vb[i + 5], c[i + 4], se[i + 1]
+        px = product(half(k, c[i + 5]), v, vb[i + 6], s, se[i + 2])
         py = product(half(k, nxt(k, 0)), v, nxt(v, 0), s, nxt(s, 0))
         pz = product(half(k, nxt(k, 1)), v, nxt(v, 1), s, nxt(s, 1))
         both = k * (px + before + py + prv(py, 0) + pz + prv(pz, 1))
@@ -449,7 +497,7 @@
         adj[i] = pltpu.roll(v, YW - 4, 0)[:CY, :CZ]
         return px, acc
 
-    first = product(half(c[4], c[5]), vb[4], vb[5], se[0], se[1])
+    first = product(half(c[3], c[4]), vb[4], vb[5], se[0], se[1])
     _, acc = lax.fori_loop(
         0, CX, terms, (first, jnp.zeros((YW, CZ), jnp.float32)), unroll=8
     )
@@ -465,7 +513,7 @@
 
 
 def params():
-    return pltpu.CompilerParams(vmem_limit_bytes=48 << 20)
+    return pltpu.CompilerParams(vmem_limit_bytes=20 << 20)
 
 
 def both_ways(up, down, axis):
@@ -491,48 +539,59 @@
     halo = jnp.where(gz > 0, before, 0.0) + jnp.where(gz < count - 1, after, 0.0)
     mine = lax.dynamic_update_slice(mine, halo, (2 * CX, 0, 0))
     g = lax.all_gather(mine, "gx")
-    pair = f32(52, 24, CZ)
-    up, down = pl.pallas_call(
-        pack_y_kernel, out_shape=(pair, pair), compiler_params=params(), name="pack_y"
-    )(g, state)
-    yp, yn = both_ways(up, down, "gy")
-
     fine, fine1, fine2 = (32, YE, ZE), (33, YE, ZE), (34, YE, ZE)
     mid, mid1, mid2 = (16, YM, ZM), (17, YM, ZM), (18, YM, ZM)
     win, win1, win2 = (XW, YW, ZE), (XW + 1, YW, ZE), (XW + 2, YW, ZE)
-    src_w, pre_w, c_w, se, mid_pre, mid_rhs, mid_c, low, block_s = pl.pallas_call(
+    c_rows, s_rows = f32(16, 4 * HY, CZ), f32(10, 4 * HY, CZ)
+    c_up, c_down, s_up, s_down = pl.pallas_call(
+        pack_y_kernel,
+        out_shape=(c_rows, c_rows, s_rows, s_rows),
+        compiler_params=params(),
+        name="pack_y",
+    )(g, state)
+    cp, cn = both_ways(c_up, c_down, "gy")
+    sp, sn = both_ways(s_up, s_down, "gy")
+    wx, wy, wz, inv, c_w, wx_w, wy_w, wz_w, inv_w, mwx, mwy, mwz, minv, low = pl.pallas_call(
+        coef_kernel,
+        out_shape=(
+            f32(*fine1), f32(*fine), f32(*fine), f32(*fine),
+            f32(*win), f32(*win1), f32(*win), f32(*win), f32(*win),
+            f32(*mid1), f32(*mid), f32(*mid), f32(*mid), f32(3, 8, CZ),
+        ),
+        scratch_shapes=[vm(*fine2), vm(16, YM, ZE), vm(*mid2)],
+        compiler_params=params(),
+        name="coef",
+    )(g, cp, cn)
+    src_w, pre_w, se, mid_pre, mid_rhs, ends, block_s = pl.pallas_call(
         first_kernel,
         out_shape=(
-            f32(*win), f32(*win), f32(*win), f32(CX + 2, YW, ZE),
-            f32(16, 8, ZM), f32(*mid), f32(*mid), f32(16, 8, CZ), f32(3, 8, CZ),
+            f32(*win), f32(*win), f32(CX + 2, YW, ZE),
+            f32(16, 8, ZM), f32(*mid), f32(16, 8, CZ), f32(3, 8, CZ),
         ),
         scratch_shapes=[
-            vm(*fine2), vm(*fine1), vm(*fine), vm(*fine), vm(*fine), vm(*fine),
-            vm(*fine2), vm(*fine2), vm(32, YM, ZE),
-            vm(*mid2), vm(*mid1), vm(*mid), vm(*mid), vm(*mid), vm(*mid),
-            vm(*mid2), vm(*mid2),
+            vm(*fine), vm(*fine2), vm(*fine2), vm(16, YM, ZE), vm(*mid2), vm(*mid2),
         ],
         compiler_params=params(),
         name="first",
-    )(g, yp, yn, state)
-
-    rec = lax.all_to_all(low, "gz", 0, 0, tiled=True)
-    mid_init = pl.pallas_call(
-        solve_kernel, out_shape=f32(16, 8, ZM), compiler_params=params(), name="solve"
-    )(rec, block_s, mid_pre)
-    mid_p, mid_n = both_ways(mid_init, mid_init, "gy")
+    )(g, cp, cn, sp, sn, state, wx, wy, wz, inv, mwx, mwy, mwz, minv, low)
+
+    rec = lax.all_to_all(ends, "gz", 0, 0, tiled=True)
+    tile = f32(16, 8, ZM)
+    mid_init, up, down = pl.pallas_call(
+        solve_kernel, out_shape=(tile, tile, tile), compiler_params=params(), name="solve"
+    )(rec, block_s, mid_pre, mid_rhs)
+    mid_p, mid_n = both_ways(up, down, "gy")
 
     adj, grad = pl.pallas_call(
         second_kernel,
         out_shape=(block, f32(CY, CZ)),
         scratch_shapes=[
-            vm(*mid2), vm(*mid1), vm(*mid), vm(*mid), vm(*mid),
-            vm(20, YM, ZM), vm(20, YM, ZM), vm(8, YM, ZE),
-            vm(*win2), vm(*win1), vm(*win), vm(*win), vm(*win), vm(*win2), vm(*win2),
+            vm(*mid), vm(20, YM, ZM), vm(20, YM, ZM), vm(8, YM, ZE), vm(*win2), vm(*win2),
         ],
         compiler_params=params(),
         name="second",
-    )(mid_init, mid_p, mid_n, mid_rhs, mid_c, src_w, pre_w, c_w, se)
+    )(mid_init, mid_p, mid_n, mid_rhs, mwx, mwy, mwz, minv,
+      src_w, pre_w, c_w, wx_w, wy_w, wz_w, inv_w, se)
     sums = lax.all_to_all(grad, "gz", 0, 0, tiled=True)
     total = jnp.sum(sums[:, :CX], axis=0)[:, None]
     return adj, total * (-1.0 / math.sqrt(source.shape[2] * lax.axis_size("gz")))

time: 99.9 us -> 94.1 us (0.942)
  the two profiles are of different devices: /device:TPU:33 before, /device:TPU:27 now
where the time goes in v4:
time: 94.1 us; the launch traced here: 93.8 us
  blocking collectives  44.4 us (47%)
  starting transfers between devices  20.8 us (22%)
  Pallas kernels  17.4 us (18%)
  waiting for transfers between devices  9.34 us (10%)
  other arithmetic  1.16 us (1%)
    all_to_all x1, blocking collectives, per_device(): rec = lax.all_to_all(ends, 'gz', 0, 0, tiled=True)  21.3 us
    ppermute x6, starting transfers between devices, both_ways(): return (lax.ppermute(up, axis, higher), lax.ppermute(down, axis, lower))  18.1 us
    all_gather x1, blocking collectives, per_device(): g = lax.all_gather(mine, 'gx')  12.1 us
    all_to_all x1, blocking collectives, per_device(): sums = lax.all_to_all(grad, 'gz', 0, 0, tiled=True)  11 us
    pallas_call x1, Pallas kernels, per_device(): pl.pallas_call(first_kernel, out_shape=(f32(*win), f32(*win), f32(CX + 2,...  7.4 us
    ppermute x6, waiting for transfers between devices, both_ways(): return (lax.ppermute(up, axis, higher), lax.ppermute(down, axis, lower))  5.45 us
    pallas_call x1, Pallas kernels, per_device(): pl.pallas_call(coef_kernel, out_shape=(f32(*fine1), f32(*fine), f32(*fine...  4.28 us
    pallas_call x1, Pallas kernels, per_device(): pl.pallas_call(second_kernel, out_shape=(block, f32(CY, CZ)), scratch_sha...  2.81 us
  transfers between devices with their start and end apart: 8, of which 6 were waited for; matrix products, arithmetic and copies ran while one was open for 0% of the time, Pallas kernels for 5%

profile of v4, /device:TPU:27, one launch (start us, length us, event | category | flops | bytes accessed | tf_op | source)
XLA Modules:
  0.0 93.8 jit_solution(1742558056129742663)
XLA Ops:
  0.6 0.0 copy-start
  0.6 1.9 %pack_z.1 = (f32[26,16,128]{2,1,0:T(8,128)}, f32[8,16,128]{2,1,0:T(8,128)}, f32[8,16,128]{2,1,0:T(8,128)}) custom-call(s32[16]{0:T(128)} %bitcast.13, f32[8,16,128]{2,1,0:T(8,128)} %src.1, f32[8,16,128]{2,1,0:T(8,128)} %log_coef.1, f32[8,16]{1,0:T(8,128)} %lateral.1, f32[8,16,128]{2,1,0:T(8,128)} %state.5), custom_call_target="tpu_custom_call" | custom-call | tf_op jit(solution)/shard_map/pack_z/pallas_call | solution.py:530
  2.6 2.7 %collective-permute-start = (f32[8,16,128]{2,1,0:T(8,128)}, f32[8,16,128]{2,1,0:T(8,128)S(1)}, u32[]{:S(2)}, u32[]{:S(2)}) collective-permute-start(f32[8,16,128]{2,1,0:T(8,128)} %get-tuple-element.36), channel_id=1, source_target_pairs={{0,1},{1,2},{2,3},{3,4},{4,5},{5,6},{6,7},{7,8},{8,9},{9,10},{10,1... | collective-permute-start | bytes 196616 | tf_op jit(solution)/shard_map/ppermute | solution.py:537
  5.2 0.0 collective-permute-start.1
  5.2 1.6 %collective-permute-done = f32[8,16,128]{2,1,0:T(8,128)S(1)} collective-permute-done((f32[8,16,128]{2,1,0:T(8,128)}, f32[8,16,128]{2,1,0:T(8,128)S(1)}, u32[]{:S(2)}, u32[]{:S(2)}) %collective-permute-start) | collective-permute-done | bytes 65568 | tf_op jit(solution)/shard_map/ppermute | solution.py:537
  6.9 2.3 %collective-permute-done.1 = f32[8,16,128]{2,1,0:T(8,128)S(1)} collective-permute-done((f32[8,16,128]{2,1,0:T(8,128)}, f32[8,16,128]{2,1,0:T(8,128)S(1)}, u32[]{:S(2)}, u32[]{:S(2)}) %collective-permute-start.1) | collective-permute-done | bytes 65568 | tf_op jit(solution)/shard_map/ppermute | solution.py:538
  9.1 0.6 bitcast_dynamic-update-slice_fusion
  9.8 12.1 %all_gather.10.g = f32[4,26,16,128]{3,2,1,0:T(8,128)S(1)} all-gather(f32[1,26,16,128]{3,2,1,0:T(8,128)} %bitcast_dynamic-update-slice_fusion), channel_id=1, replica_groups=mesh['gx'=4,'gy'=8,'gz'=16] {'gx'}, dimensions={0}, use_global_device_ids=true | all-gather | bytes 1064960 | tf_op jit(solution)/shard_map/all_gather | solution.py:541
  21.9 0.0 copy-done
  21.9 0.1 pack_y.1
  22.0 4.4 %collective-permute-start.2 = (f32[16,40,128]{2,1,0:T(8,128)S(1)}, f32[16,40,128]{2,1,0:T(8,128)S(1)}, u32[]{:S(2)}, u32[]{:S(2)}) collective-permute-start(f32[16,40,128]{2,1,0:T(8,128)S(1)} %get-tuple-element.38), channel_id=1, source_target_pairs={{0,16},{16,32},{32,48},{48,64},{64,80},{80,96},{96,112},{1,17},{17... | collective-permute-start | bytes 983048 | tf_op jit(solution)/shard_map/ppermute | solution.py:523
  26.4 1.9 %collective-permute-start.3 = (f32[16,40,128]{2,1,0:T(8,128)S(1)}, f32[16,40,128]{2,1,0:T(8,128)S(1)}, u32[]{:S(2)}, u32[]{:S(2)}) collective-permute-start(f32[16,40,128]{2,1,0:T(8,128)S(1)} %get-tuple-element.39), channel_id=1, source_target_pairs={{16,0},{32,16},{48,32},{64,48},{80,64},{96,80},{112,96},{17,1},{33... | collective-permute-start | bytes 983048 | tf_op jit(solution)/shard_map/ppermute | solution.py:523
  28.3 4.6 %collective-permute-start.4 = (f32[10,40,128]{2,1,0:T(8,128)S(1)}, f32[10,40,128]{2,1,0:T(8,128)S(1)}, u32[]{:S(2)}, u32[]{:S(2)}) collective-permute-start(f32[10,40,128]{2,1,0:T(8,128)S(1)} %get-tuple-element.40), channel_id=1, source_target_pairs={{0,16},{16,32},{32,48},{48,64},{64,80},{80,96},{96,112},{1,17},{17... | collective-permute-start | bytes 614408 | tf_op jit(solution)/shard_map/ppermute | solution.py:523
  32.9 1.9 %collective-permute-start.5 = (f32[10,40,128]{2,1,0:T(8,128)S(1)}, f32[10,40,128]{2,1,0:T(8,128)S(1)}, u32[]{:S(2)}, u32[]{:S(2)}) collective-permute-start(f32[10,40,128]{2,1,0:T(8,128)S(1)} %get-tuple-element.41), channel_id=1, source_target_pairs={{16,0},{32,16},{48,32},{64,48},{80,64},{96,80},{112,96},{17,1},{33... | collective-permute-start | bytes 614408 | tf_op jit(solution)/shard_map/ppermute | solution.py:523
  34.8 0.0 collective-permute-done.2.yp.cp
  34.9 0.6 collective-permute-done.3.yn.cn
  35.4 4.3 %coef.1 = (f32[33,40,256]{2,1,0:T(8,128)S(1)}, f32[32,40,256]{2,1,0:T(8,128)S(1)}, f32[32,40,256]{2,1,0:T(8,128)S(1)}, f32[32,40,256]{2,1,0:T(8,128)S(1)}, f32[1...) custom-call(f32[4,26,16,128]{3,2,1,0:T(8,128)S(1)} %all_gather.10.g,, ...), custom_call_target="tpu_custom_call" | custom-call | tf_op jit(solution)/shard_map/coef/pallas_call | solution.py:554
  39.7 0.0 collective-permute-done.4.yp
  39.7 1.7 %collective-permute-done.5.yn = f32[10,40,128]{2,1,0:T(8,128)S(1)} collective-permute-done((f32[10,40,128]{2,1,0:T(8,128)S(1)}, f32[10,40,128]{2,1,0:T(8,128)S(1)}, u32[]{:S(2)}, u32[]{:S(2)}) %collective-permute-start.5) | collective-permute-done | bytes 204832 | tf_op jit(solution)/shard_map/ppermute | solution.py:523
  41.4 7.4 %first.1 = (f32[16,24,256]{2,1,0:T(8,128)S(1)}, f32[16,24,256]{2,1,0:T(8,128)S(1)}, f32[10,24,256]{2,1,0:T(8,128)S(1)}, f32[16,8,128]{2,1,0:T(8,128)S(1)}, f32[1...) custom-call(f32[4,26,16,128]{3,2,1,0:T(8,128)S(1)} %all_gather.10.g, ...), custom_call_target="tpu_custom_call" | custom-call | tf_op jit(solution)/shard_map/first/pallas_call | solution.py:565
  48.8 21.3 %all_to_all.17.rec = f32[16,8,128]{2,1,0:T(8,128)S(1)} all-to-all(f32[16,8,128]{2,1,0:T(8,128)S(1)} %get-tuple-element.51), channel_id=1, replica_groups=mesh['gx'=4,'gy'=8,'gz'=16] {'gz'}, dimensions={0} | all-to-all | bytes 131072 | tf_op jit(solution)/shard_map/all_to_all | solution.py:578
  70.1 0.8 solve.1
  70.9 2.3 %collective-permute-start.6 = (f32[16,8,128]{2,1,0:T(8,128)S(1)}, f32[16,8,128]{2,1,0:T(8,128)S(1)}, u32[]{:S(2)}, u32[]{:S(2)}) collective-permute-start(f32[16,8,128]{2,1,0:T(8,128)S(1)} %get-tuple-element.56), channel_id=1, source_target_pairs={{0,16},{16,32},{32,48},{48,64},{64,80},{80,96},{96,112},{1,17},{17... | collective-permute-start | bytes 196616 | tf_op jit(solution)/shard_map/ppermute | solution.py:523
  73.2 3.0 %collective-permute-start.7 = (f32[16,8,128]{2,1,0:T(8,128)S(1)}, f32[16,8,128]{2,1,0:T(8,128)S(1)}, u32[]{:S(2)}, u32[]{:S(2)}) collective-permute-start(f32[16,8,128]{2,1,0:T(8,128)S(1)} %get-tuple-element.57), channel_id=1, source_target_pairs={{16,0},{32,16},{48,32},{64,48},{80,64},{96,80},{112,96},{17,1},{33... | collective-permute-start | bytes 196616 | tf_op jit(solution)/shard_map/ppermute | solution.py:523
  76.2 0.1 collective-permute-done.6.mid_p
  76.3 3.1 %collective-permute-done.7.mid_n = f32[16,8,128]{2,1,0:T(8,128)S(1)} collective-permute-done((f32[16,8,128]{2,1,0:T(8,128)S(1)}, f32[16,8,128]{2,1,0:T(8,128)S(1)}, u32[]{:S(2)}, u32[]{:S(2)}) %collective-permute-start.7) | collective-permute-done | bytes 65568 | tf_op jit(solution)/shard_map/ppermute | solution.py:523
  79.4 2.8 %second.1 = (f32[8,16,128]{2,1,0:T(8,128)}, f32[16,128]{1,0:T(8,128)S(1)}) custom-call(f32[16,8,128]{2,1,0:T(8,128)S(1)} %get-tuple-element.55.mid, f32[16,8,128]{2,1,0:T(8,128)S(1)} %collective-permute-done.6.mid_p, f32[16,8,128]{2,1,0:T(8,128)S(1)} %collective-permute-done.7.mid_n, f32[16,24,128]{2,1,0:T(8,128)S(1)} %get-tuple-element.54.mid_rhs, ...), custom_call_target="tpu_custom_call" | custom-call | tf_op jit(solution)/shard_map/second/pallas_call | solution.py:585
  82.2 11.0 %all_to_all.18 = f32[16,1,128]{2,1,0:T(1,128)S(1)} all-to-all(f32[16,1,128]{2,1,0:T(1,128)S(1)} %bitcast.10), channel_id=1, replica_groups=mesh['gx'=4,'gy'=8,'gz'=16] {'gz'}, dimensions={0} | all-to-all | bytes 16384 | tf_op jit(solution)/shard_map/all_to_all | solution.py:595
  93.2 0.5 multiply_bitcast_fusion
  (1 shorter events, 0.0 us)
Async XLA Ops:
  0.6 21.2 %copy-start = (f32[8,16,128]{2,1,0:T(8,128)S(1)}, f32[8,16,128]{2,1,0:T(8,128)}, u32[]{:S(2)}) copy-start(f32[8,16,128]{2,1,0:T(8,128)} %state.5) | copy-start | bytes 196612
  2.6 4.3 %collective-permute-start = (f32[8,16,128]{2,1,0:T(8,128)}, f32[8,16,128]{2,1,0:T(8,128)S(1)}, u32[]{:S(2)}, u32[]{:S(2)}) collective-permute-start(f32[8,16,128]{2,1,0:T(8,128)} %get-tuple-element.36), channel_id=1, source_target_pairs={{0,1},{1,2},{2,3},{3,4},{4,5},{5,6},{6,7},{7,8},{8,9},{9,10},{10,1... | collective-permute-start | bytes 196616 | tf_op jit(solution)/shard_map/ppermute | solution.py:537
  5.2 3.9 %collective-permute-start.1 = (f32[8,16,128]{2,1,0:T(8,128)}, f32[8,16,128]{2,1,0:T(8,128)S(1)}, u32[]{:S(2)}, u32[]{:S(2)}) collective-permute-start(f32[8,16,128]{2,1,0:T(8,128)} %get-tuple-element.37), channel_id=1, source_target_pairs={{0,15},{1,0},{2,1},{3,2},{4,3},{5,4},{6,5},{7,6},{8,7},{9,8},{10,9... | collective-permute-start | bytes 196616 | tf_op jit(solution)/shard_map/ppermute | solution.py:538
  22.0 12.9 %collective-permute-start.2 = (f32[16,40,128]{2,1,0:T(8,128)S(1)}, f32[16,40,128]{2,1,0:T(8,128)S(1)}, u32[]{:S(2)}, u32[]{:S(2)}) collective-permute-start(f32[16,40,128]{2,1,0:T(8,128)S(1)} %get-tuple-element.38), channel_id=1, source_target_pairs={{0,16},{16,32},{32,48},{48,64},{64,80},{80,96},{96,112},{1,17},{17... | collective-permute-start | bytes 983048 | tf_op jit(solution)/shard_map/ppermute | solution.py:523
  26.4 9.0 %collective-permute-start.3 = (f32[16,40,128]{2,1,0:T(8,128)S(1)}, f32[16,40,128]{2,1,0:T(8,128)S(1)}, u32[]{:S(2)}, u32[]{:S(2)}) collective-permute-start(f32[16,40,128]{2,1,0:T(8,128)S(1)} %get-tuple-element.39), channel_id=1, source_target_pairs={{16,0},{32,16},{48,32},{64,48},{80,64},{96,80},{112,96},{17,1},{33... | collective-permute-start | bytes 983048 | tf_op jit(solution)/shard_map/ppermute | solution.py:523
  28.3 11.4 %collective-permute-start.4 = (f32[10,40,128]{2,1,0:T(8,128)S(1)}, f32[10,40,128]{2,1,0:T(8,128)S(1)}, u32[]{:S(2)}, u32[]{:S(2)}) collective-permute-start(f32[10,40,128]{2,1,0:T(8,128)S(1)} %get-tuple-element.40), channel_id=1, source_target_pairs={{0,16},{16,32},{32,48},{48,64},{64,80},{80,96},{96,112},{1,17},{17... | collective-permute-start | bytes 614408 | tf_op jit(solution)/shard_map/ppermute | solution.py:523
  32.9 8.5 %collective-permute-start.5 = (f32[10,40,128]{2,1,0:T(8,128)S(1)}, f32[10,40,128]{2,1,0:T(8,128)S(1)}, u32[]{:S(2)}, u32[]{:S(2)}) collective-permute-start(f32[10,40,128]{2,1,0:T(8,128)S(1)} %get-tuple-element.41), channel_id=1, source_target_pairs={{16,0},{32,16},{48,32},{64,48},{80,64},{96,80},{112,96},{17,1},{33... | collective-permute-start | bytes 614408 | tf_op jit(solution)/shard_map/ppermute | solution.py:523
  70.9 5.4 %collective-permute-start.6 = (f32[16,8,128]{2,1,0:T(8,128)S(1)}, f32[16,8,128]{2,1,0:T(8,128)S(1)}, u32[]{:S(2)}, u32[]{:S(2)}) collective-permute-start(f32[16,8,128]{2,1,0:T(8,128)S(1)} %get-tuple-element.56), channel_id=1, source_target_pairs={{0,16},{16,32},{32,48},{48,64},{64,80},{80,96},{96,112},{1,17},{17... | collective-permute-start | bytes 196616 | tf_op jit(solution)/shard_map/ppermute | solution.py:523
  73.2 6.2 %collective-permute-start.7 = (f32[16,8,128]{2,1,0:T(8,128)S(1)}, f32[16,8,128]{2,1,0:T(8,128)S(1)}, u32[]{:S(2)}, u32[]{:S(2)}) collective-permute-start(f32[16,8,128]{2,1,0:T(8,128)S(1)} %get-tuple-element.57), channel_id=1, source_target_pairs={{16,0},{32,16},{48,32},{64,48},{80,64},{96,80},{112,96},{17,1},{33... | collective-permute-start | bytes 196616 | tf_op jit(solution)/shard_map/ppermute | solution.py:523

commit v5 on v4

--- a/solution.py
+++ b/solution.py
@@ -15,6 +15,7 @@
 HZ = 18
 YE = CY + 2 * Y0
 ZE = 2 * CZ
+TILES = 11
 YM = 24
 ZM = CZ
 XW = CX + 8
@@ -28,6 +29,26 @@
 
 def mm(a, b):
     return jnp.dot(a, b, precision=HIGHEST, preferred_element_type=jnp.float32)
+
+
+def split(v, axis):
+    high = v.astype(jnp.bfloat16)
+    v = v - high.astype(jnp.float32)
+    mid = v.astype(jnp.bfloat16)
+    low = (v - mid.astype(jnp.float32)).astype(jnp.bfloat16)
+    return jnp.concatenate([high, mid, low], axis)
+
+
+def pick_rows(sel, v):
+    out = jnp.dot(sel.astype(jnp.bfloat16), split(v, 1), preferred_element_type=jnp.float32)
+    n = v.shape[1]
+    return out[:, :n] + (out[:, n : 2 * n] + out[:, 2 * n :])
+
+
+def pick_lanes(v, sel):
+    out = jnp.dot(split(v, 0), sel.astype(jnp.bfloat16), preferred_element_type=jnp.float32)
+    n = v.shape[0]
+    return out[:n] + (out[n : 2 * n] + out[2 * n :])
 
 
 def nxt(v, axis):
@@ -81,6 +102,21 @@
         return fx
 
     lax.fori_loop(0, planes, step, wx[0] * (0.0 - v[1]), unroll=unroll(planes))
+
+
+def first_sweeps(out, b, wx, wy, wz, inv, planes):
+    def step(x, carry):
+        before, here = carry
+        after = inv[jnp.minimum(x + 1, planes - 1)] * b[x + 1]
+        fx = wx[x + 1] * (here - after)
+        fy = wy[x] * (here - nxt(here, 0))
+        fz = wz[x] * (here - nxt(here, 1))
+        flow = (fx - before) + (fy - prv(fy, 0)) + (fz - prv(fz, 1))
+        out[x + 1] = here + inv[x] * (b[x] - flow)
+        return fx, after
+
+    here = inv[0] * b[0]
+    lax.fori_loop(0, planes, step, (wx[0] * (0.0 - here), here), unroll=unroll(planes))
 
 
 def pack_z_kernel(line, src, log_coef, lateral, state, mine, down, up):
@@ -110,30 +146,60 @@
 
 
 def pack_y_kernel(g, state, c_up, c_down, s_up, s_down):
-    def put(up, down, n, plane):
+    lane = iota((CY, CZ), 1)
+    none = jnp.zeros((HY, CZ), jnp.float32)
+
+    def put(refs, n, low, high):
         at = pl.ds(HY * (n % 4), HY)
-        up[n // 4, at] = plane[CY - HY :]
-        down[n // 4, at] = plane[:HY]
-
-    for s in range(4):
-        for i in range(2 * CX):
-            put(c_up, c_down, 2 * CX * s + i, g[s, CX + i])
-        for i in range(CX):
-            put(s_up, s_down, CX * s + i, g[s, i])
+        refs[0][n // 4, at] = high
+        refs[1][n // 4, at] = low
+
+    for coef, refs in ((1, (c_up, c_down)), (0, (s_up, s_down))):
+        for s in range(4):
+            for i in range(CX):
+                plane = g[s, CX * coef + i]
+                put(refs, CX * s + i, plane[:HY], plane[CY - HY :])
+        for t in range(TILES):
+            plane = jnp.zeros((CY, CZ), jnp.float32)
+            for x in range(3 * t, min(3 * t + 3, 4 * CX)):
+                off = 2 * HZ * (x % 3)
+                move = off - 46 if coef else off + HZ
+                halo = pltpu.roll(g[x // CX, 2 * CX + x % CX], move % CZ, 1)
+                plane = jnp.where(lane >= off, halo, plane)
+            put(refs, 4 * CX + t, plane[:HY], plane[CY - HY :])
     for i in range(CX):
-        put(s_up, s_down, 4 * CX + i, state[i])
-
-
-def place(out, lanes, n, low, own, high, change):
-    at = pl.ds(HY * (n % 4), HY)
-    out[Y0 - HY : Y0, lanes] = change(low[n // 4, at])
-    out[Y0 : Y0 + CY, lanes] = change(own)
-    out[Y0 + CY : Y0 + CY + HY, lanes] = change(high[n // 4, at])
-
-
-def edge_lanes(v):
+        put((c_up, c_down), 4 * CX + TILES + i, state[i, :HY], state[i, CY - HY :])
+    put((s_up, s_down), 4 * CX + TILES, none, none)
+    put((c_up, c_down), 5 * CX + TILES, none, none)
+
+
+def rows_at(ref, n):
+    return ref[n // 4, HY * (n % 4) : HY * (n % 4) + HY]
+
+
+def place(out, lanes, low, own, high):
+    out[Y0 - HY : Y0, lanes] = low
+    out[Y0 : Y0 + CY, lanes] = own
+    out[Y0 + CY : Y0 + CY + HY, lanes] = high
+
+
+def edge_lanes(v, move):
+    v = pltpu.roll(v, move % CZ, 1) if move % CZ else v
     lane = iota(v.shape, 1)
     return jnp.where((lane < HZ) | (lane >= CZ - HZ), v, 0.0)
+
+
+def fill(out, g, yp, yn, x, coef):
+    s, i = x // CX, x % CX
+    none = jnp.zeros((8, ZE), jnp.float32)
+    out[0:8] = none
+    out[YE - 8 :] = none
+    place(out, LOW, rows_at(yp, x), g[s, CX * coef + i], rows_at(yn, x))
+    n, move = 4 * CX + x // 3, CZ - HZ - 2 * HZ * (x % 3)
+    place(
+        out, HIGH, edge_lanes(rows_at(yp, n), move),
+        edge_lanes(g[s, 2 * CX + i], 64 * coef), edge_lanes(rows_at(yn, n), move),
+    )
 
 
 LOW, HIGH = slice(0, CZ), slice(CZ, ZE)
@@ -192,35 +258,25 @@
     nx = 4 * CX
     c[0] = zero
     c[nx + 1] = zero
-    none = jnp.zeros((8, ZE), jnp.float32)
-    for s in range(4):
-        for i in range(CX):
-            out = c.at[CX * s + i + 1]
-            out[0:8] = none
-            out[YE - 8 :] = none
-            n = 2 * CX * s + i
-            place(out, LOW, n, yp, g[s, CX + i], yn, lambda v: v)
-            place(
-                out, HIGH, n + CX, yp, g[s, 2 * CX + i], yn,
-                lambda v: edge_lanes(pltpu.roll(v, 64, 1)),
-            )
+    for x in range(nx):
+        fill(c.at[x + 1], g, yp, yn, x, 1)
     make_weights(c, wx, wy, wz, inv, nx, 1.0)
     rows = fold_y()
 
     def coarse(m, carry):
-        t[m] = mm(rows, c[2 * m + 1] + c[2 * m + 2])
+        t[m] = pick_rows(rows, c[2 * m + 1] + c[2 * m + 2])
         return carry
 
     lax.fori_loop(0, 16, coarse, 0, unroll=8)
     mid_zero = jnp.zeros((YM, ZM), jnp.float32)
     mc[0] = mid_zero
     mc[17] = mid_zero
-    mc[1:17] = mm(t[...].reshape(16 * YM, ZE), fold_z()).reshape(16, YM, ZM)
+    mc[1:17] = pick_lanes(t[...].reshape(16 * YM, ZE), fold_z()).reshape(16, YM, ZM)
     make_weights(mc, mwx, mwy, mwz, minv, 16, 0.25)
     window(gx, [(c_w, c, 1, 0), (wy_w, wy, 0, 0), (wz_w, wz, 0, 0), (inv_w, inv, 0, 0)], XW)
     window(gx, [(wx_w, wx, 1, 1)], XW + 1)
 
-    low_c = mm(mm(fold_low(-1, 6), mc[1:17].reshape(16 * YM, ZM)), squeeze())
+    low_c = pick_lanes(pick_rows(fold_low(-1, 6), mc[1:17].reshape(16 * YM, ZM)), squeeze())
     low_c = low_c.reshape(6, 8, CZ)
     here = low_c[1:5]
     row = iota((4, 8, CZ), 1)
@@ -256,40 +312,29 @@
     for ref in (va, vb):
         ref[0] = zero
         ref[nx + 1] = zero
-    none = jnp.zeros((8, ZE), jnp.float32)
-    for s in range(4):
-        for i in range(CX):
-            out = b.at[CX * s + i]
-            out[0:8] = none
-            out[YE - 8 :] = none
-            place(out, LOW, CX * s + i, yp, g[s, i], yn, lambda v: v)
-            place(out, HIGH, 2 * CX * s + CX + i, cp, g[s, 2 * CX + i], cn, edge_lanes)
-
-    def start(x, carry):
-        va[x + 1] = inv[x] * b[x]
-        return carry
-
-    lax.fori_loop(0, nx, start, 0, unroll=4)
+    for x in range(nx):
+        fill(b.at[x], g, yp, yn, x, 0)
+    b[nx] = zero
+    first_sweeps(va, b, wx, wy, wz, inv, nx)
     sweep(va, vb, b, wx, wy, wz, inv, nx)
-    sweep(vb, va, b, wx, wy, wz, inv, nx)
 
     rows = fold_y()
 
     def coarse(m, before):
         x = 2 * m
-        _, one, fx = residual(va, b, wx, wy, wz, x, before)
-        _, two, fx = residual(va, b, wx, wy, wz, x + 1, fx)
-        t[m] = mm(rows, one + two)
+        _, one, fx = residual(vb, b, wx, wy, wz, x, before)
+        _, two, fx = residual(vb, b, wx, wy, wz, x + 1, fx)
+        t[m] = pick_rows(rows, one + two)
         return fx
 
-    lax.fori_loop(0, 16, coarse, wx[0] * (0.0 - va[1]), unroll=8)
-    mb[...] = mm(t[...].reshape(16 * YM, ZE), fold_z()).reshape(16, YM, ZM)
+    lax.fori_loop(0, 16, coarse, wx[0] * (0.0 - vb[1]), unroll=8)
+    mb[...] = pick_lanes(t[...].reshape(16 * YM, ZE), fold_z()).reshape(16, YM, ZM)
     mid_zero = jnp.zeros((YM, ZM), jnp.float32)
     for ref in (mva, mvb):
         ref[0] = mid_zero
         ref[17] = mid_zero
 
-    window(gx, [(src_w, b, 0, 0), (pre_w, va, 1, 0)], XW)
+    window(gx, [(src_w, b, 0, 0), (pre_w, vb, 1, 0)], XW)
 
     zero8 = jnp.zeros((8, CZ), jnp.float32)
     wide = jnp.zeros((YW, CZ), jnp.float32)
@@ -304,9 +349,9 @@
         se[at] = jnp.concatenate([mid, wide], 1)
     for i in range(CX):
         mid = pltpu.roll(jnp.concatenate([state[i], zero8], 0), 4, 0)
-        n = 4 * CX + i
+        n = 4 * CX + TILES + i
         at = HY * (n % 4)
-        under, over = yp[n // 4, at + HY - 1 : at + HY], yn[n // 4, at : at + 1]
+        under, over = cp[n // 4, at + HY - 1 : at + HY], cn[n // 4, at : at + 1]
         mid = jnp.where(row == 3, under, jnp.where(row == 20, over, mid))
         halo = pltpu.roll(jnp.concatenate([g[gx, 16 + i], zero8], 0), 4, 0)
         halo = pltpu.roll(halo, CZ - 32, 1)
@@ -325,7 +370,7 @@
 
     lax.fori_loop(0, 16, rest, mwx[0] * (0.0 - mva[1]), unroll=16)
 
-    rhs = mm(mm(fold_low(0, 4), mvb[1:17].reshape(16 * YM, ZM)), squeeze()).reshape(4, 8, CZ)
+    rhs = pick_lanes(pick_rows(fold_low(0, 4), mvb[1:17].reshape(16 * YM, ZM)), squeeze()).reshape(4, 8, CZ)
     depth = iota((8, CZ), 1) % 32
     top = depth == 0
     r, d, e, edge = gather(rhs), low[0], low[1], low[2]
@@ -412,7 +457,7 @@
     ends = jnp.concatenate([left, right, left_m, right_m, left_p, right_p], 0)
     ends = jnp.where(iota((48, CZ), 1) % 32 == 0, ends, 0.0)
     copy = (iota((CZ, CZ), 1) // 32 * 32 == iota((CZ, CZ), 0)).astype(jnp.float32)
-    ends = mm(ends, copy).reshape(6, 8, CZ)
+    ends = pick_lanes(ends, copy).reshape(6, 8, CZ)
     own = block[0] + block[1] * ends[0] + block[2] * ends[1]
     v = every[-1][0]
     low = v + pltpu.roll(v, 3, 1) * ends[2] + pltpu.roll(v, 6, 1) * ends[3]
@@ -432,7 +477,7 @@
     spread_z = (k == jnp.where(m < 96, m // 2, m // 2 + 64)).astype(jnp.float32)
     to, frm = iota((128, 32), 0), iota((128, 32), 1)
     spread = ((to // 16 == frm % 8) & ((to % 8) // 2 == frm // 8)).astype(jnp.float32)
-    mid = mid_pre[...] + mm(spread, mm(rows, spread_z)).reshape(16, 8, ZM)
+    mid = mid_pre[...] + pick_rows(spread, pick_lanes(rows, spread_z)).reshape(16, 8, ZM)
     out[...] = mid
     row = iota((16, 8, ZM), 1)
     rest = pltpu.roll(mid_rhs[:, 8:16], 4, 1)
@@ -468,9 +513,9 @@
     spread_z = (iota((ZM, ZE), 1) // 2 == iota((ZM, ZE), 0)).astype(jnp.float32)
     spread_y = ((iota((YW, YM), 0) + 12) // 2 == iota((YW, YM), 1)).astype(jnp.float32)
     near = mvb[pl.ds(4 * gx, 8)]
-    sp[...] = mm(near.reshape(8 * YM, ZM), spread_z).reshape(8, YM, ZE)
+    sp[...] = pick_lanes(near.reshape(8 * YM, ZM), spread_z).reshape(8, YM, ZE)
     for m in range(8):
-        more = mm(spread_y, sp[m])
+        more = pick_rows(spread_y, sp[m])
         for x in (2 * m, 2 * m + 1):
             va[x + 1] = pre_w[x] + more
     sweep(va, vb, src_w, wx, wy, wz, inv, XW)
@@ -542,7 +587,7 @@
     fine, fine1, fine2 = (32, YE, ZE), (33, YE, ZE), (34, YE, ZE)
     mid, mid1, mid2 = (16, YM, ZM), (17, YM, ZM), (18, YM, ZM)
     win, win1, win2 = (XW, YW, ZE), (XW + 1, YW, ZE), (XW + 2, YW, ZE)
-    c_rows, s_rows = f32(16, 4 * HY, CZ), f32(10, 4 * HY, CZ)
+    c_rows, s_rows = f32(13, 4 * HY, CZ), f32(11, 4 * HY, CZ)
     c_up, c_down, s_up, s_down = pl.pallas_call(
         pack_y_kernel,
         out_shape=(c_rows, c_rows, s_rows, s_rows),
@@ -550,7 +595,7 @@
         name="pack_y",
     )(g, state)
     cp, cn = both_ways(c_up, c_down, "gy")
-    sp, sn = both_ways(s_up, s_down, "gy")
+    yp, yn = both_ways(s_up, s_down, "gy")
     wx, wy, wz, inv, c_w, wx_w, wy_w, wz_w, inv_w, mwx, mwy, mwz, minv, low = pl.pallas_call(
         coef_kernel,
         out_shape=(
@@ -569,11 +614,11 @@
             f32(16, 8, ZM), f32(*mid), f32(16, 8, CZ), f32(3, 8, CZ),
         ),
         scratch_shapes=[
-            vm(*fine), vm(*fine2), vm(*fine2), vm(16, YM, ZE), vm(*mid2), vm(*mid2),
+            vm(*fine1), vm(*fine2), vm(*fine2), vm(16, YM, ZE), vm(*mid2), vm(*mid2),
         ],
         compiler_params=params(),
         name="first",
-    )(g, cp, cn, sp, sn, state, wx, wy, wz, inv, mwx, mwy, mwz, minv, low)
+    )(g, cp, cn, yp, yn, state, wx, wy, wz, inv, mwx, mwy, mwz, minv, low)
 
     rec = lax.all_to_all(ends, "gz", 0, 0, tiled=True)
     tile = f32(16, 8, ZM)

time: 94.1 us -> 93.1 us (0.989)
  the two profiles are of different devices: /device:TPU:27 before, /device:TPU:19 now
where the time goes in v5:
time: 93.1 us; the launch traced here: 92.8 us
  blocking collectives  43.6 us (47%)
  starting transfers between devices  20.9 us (22%)
  Pallas kernels  15.9 us (17%)
  waiting for transfers between devices  10.5 us (11%)
  other arithmetic  1.16 us (1%)
    all_to_all x1, blocking collectives, per_device(): rec = lax.all_to_all(ends, 'gz', 0, 0, tiled=True)  20.5 us
    ppermute x6, starting transfers between devices, both_ways(): return (lax.ppermute(up, axis, higher), lax.ppermute(down, axis, lower))  18.2 us
    all_gather x1, blocking collectives, per_device(): g = lax.all_gather(mine, 'gx')  12.1 us
    all_to_all x1, blocking collectives, per_device(): sums = lax.all_to_all(grad, 'gz', 0, 0, tiled=True)  11 us
    pallas_call x1, Pallas kernels, per_device(): pl.pallas_call(first_kernel, out_shape=(f32(*win), f32(*win), f32(CX + 2,...  6.77 us
    ppermute x6, waiting for transfers between devices, both_ways(): return (lax.ppermute(up, axis, higher), lax.ppermute(down, axis, lower))  6.61 us
    pallas_call x1, Pallas kernels, per_device(): pl.pallas_call(coef_kernel, out_shape=(f32(*fine1), f32(*fine), f32(*fine...  3.73 us
    ppermute x1, starting transfers between devices, per_device(): lax.ppermute(up, 'gz', [(i, (i + 1) % count) for i in range(count)])  2.65 us
  transfers between devices with their start and end apart: 8, of which 4 were waited for; matrix products, arithmetic and copies ran while one was open for 0% of the time, Pallas kernels for 4%

profile of v5, /device:TPU:19, one launch (start us, length us, event | category | flops | bytes accessed | tf_op | source)
XLA Modules:
  0.0 92.8 jit_solution(14176683164915248212)
XLA Ops:
  0.6 0.0 copy-start
  0.6 1.9 %pack_z.1 = (f32[26,16,128]{2,1,0:T(8,128)}, f32[8,16,128]{2,1,0:T(8,128)}, f32[8,16,128]{2,1,0:T(8,128)}) custom-call(s32[16]{0:T(128)} %bitcast.13, f32[8,16,128]{2,1,0:T(8,128)} %src.1, f32[8,16,128]{2,1,0:T(8,128)} %log_coef.1, f32[8,16]{1,0:T(8,128)} %lateral.1, f32[8,16,128]{2,1,0:T(8,128)} %state.5), custom_call_target="tpu_custom_call" | custom-call | tf_op jit(solution)/shard_map/pack_z/pallas_call | solution.py:575
  2.6 2.7 %collective-permute-start = (f32[8,16,128]{2,1,0:T(8,128)}, f32[8,16,128]{2,1,0:T(8,128)S(1)}, u32[]{:S(2)}, u32[]{:S(2)}) collective-permute-start(f32[8,16,128]{2,1,0:T(8,128)} %get-tuple-element.36), channel_id=1, source_target_pairs={{0,1},{1,2},{2,3},{3,4},{4,5},{5,6},{6,7},{7,8},{8,9},{9,10},{10,1... | collective-permute-start | bytes 196616 | tf_op jit(solution)/shard_map/ppermute | solution.py:582
  5.2 0.0 collective-permute-start.1
  5.2 1.6 %collective-permute-done = f32[8,16,128]{2,1,0:T(8,128)S(1)} collective-permute-done((f32[8,16,128]{2,1,0:T(8,128)}, f32[8,16,128]{2,1,0:T(8,128)S(1)}, u32[]{:S(2)}, u32[]{:S(2)}) %collective-permute-start) | collective-permute-done | bytes 65568 | tf_op jit(solution)/shard_map/ppermute | solution.py:582
  6.9 2.3 %collective-permute-done.1 = f32[8,16,128]{2,1,0:T(8,128)S(1)} collective-permute-done((f32[8,16,128]{2,1,0:T(8,128)}, f32[8,16,128]{2,1,0:T(8,128)S(1)}, u32[]{:S(2)}, u32[]{:S(2)}) %collective-permute-start.1) | collective-permute-done | bytes 65568 | tf_op jit(solution)/shard_map/ppermute | solution.py:583
  9.1 0.6 bitcast_dynamic-update-slice_fusion
  9.8 12.1 %all_gather.10.g = f32[4,26,16,128]{3,2,1,0:T(8,128)S(1)} all-gather(f32[1,26,16,128]{3,2,1,0:T(8,128)} %bitcast_dynamic-update-slice_fusion), channel_id=1, replica_groups=mesh['gx'=4,'gy'=8,'gz'=16] {'gx'}, dimensions={0}, use_global_device_ids=true | all-gather | bytes 1064960 | tf_op jit(solution)/shard_map/all_gather | solution.py:586
  21.9 0.0 copy-done
  21.9 0.2 pack_y.1
  22.1 3.2 %collective-permute-start.2 = (f32[13,40,128]{2,1,0:T(8,128)S(1)}, f32[13,40,128]{2,1,0:T(8,128)S(1)}, u32[]{:S(2)}, u32[]{:S(2)}) collective-permute-start(f32[13,40,128]{2,1,0:T(8,128)S(1)} %get-tuple-element.38), channel_id=1, source_target_pairs={{0,16},{16,32},{32,48},{48,64},{64,80},{80,96},{96,112},{1,17},{17... | collective-permute-start | bytes 798728 | tf_op jit(solution)/shard_map/ppermute | solution.py:568
  25.3 2.1 %collective-permute-start.3 = (f32[13,40,128]{2,1,0:T(8,128)S(1)}, f32[13,40,128]{2,1,0:T(8,128)S(1)}, u32[]{:S(2)}, u32[]{:S(2)}) collective-permute-start(f32[13,40,128]{2,1,0:T(8,128)S(1)} %get-tuple-element.39), channel_id=1, source_target_pairs={{16,0},{32,16},{48,32},{64,48},{80,64},{96,80},{112,96},{17,1},{33... | collective-permute-start | bytes 798728 | tf_op jit(solution)/shard_map/ppermute | solution.py:568
  27.4 4.3 %collective-permute-start.4 = (f32[11,40,128]{2,1,0:T(8,128)S(1)}, f32[11,40,128]{2,1,0:T(8,128)S(1)}, u32[]{:S(2)}, u32[]{:S(2)}) collective-permute-start(f32[11,40,128]{2,1,0:T(8,128)S(1)} %get-tuple-element.40), channel_id=1, source_target_pairs={{0,16},{16,32},{32,48},{48,64},{64,80},{80,96},{96,112},{1,17},{17... | collective-permute-start | bytes 675848 | tf_op jit(solution)/shard_map/ppermute | solution.py:568
  31.6 1.9 %collective-permute-start.5 = (f32[11,40,128]{2,1,0:T(8,128)S(1)}, f32[11,40,128]{2,1,0:T(8,128)S(1)}, u32[]{:S(2)}, u32[]{:S(2)}) collective-permute-start(f32[11,40,128]{2,1,0:T(8,128)S(1)} %get-tuple-element.41), channel_id=1, source_target_pairs={{16,0},{32,16},{48,32},{64,48},{80,64},{96,80},{112,96},{17,1},{33... | collective-permute-start | bytes 675848 | tf_op jit(solution)/shard_map/ppermute | solution.py:568
  33.6 0.0 collective-permute-done.2.yp.cp
  33.6 0.0 collective-permute-done.3.yn.cn
  33.6 3.7 %coef.1 = (f32[33,40,256]{2,1,0:T(8,128)S(1)}, f32[32,40,256]{2,1,0:T(8,128)S(1)}, f32[32,40,256]{2,1,0:T(8,128)S(1)}, f32[32,40,256]{2,1,0:T(8,128)S(1)}, f32[1...) custom-call(f32[4,26,16,128]{3,2,1,0:T(8,128)S(1)} %all_gather.10.g,, ...), custom_call_target="tpu_custom_call" | custom-call | tf_op jit(solution)/shard_map/coef/pallas_call | solution.py:599
  37.3 0.0 collective-permute-done.4.yp
  37.3 3.5 %collective-permute-done.5.yn = f32[11,40,128]{2,1,0:T(8,128)S(1)} collective-permute-done((f32[11,40,128]{2,1,0:T(8,128)S(1)}, f32[11,40,128]{2,1,0:T(8,128)S(1)}, u32[]{:S(2)}, u32[]{:S(2)}) %collective-permute-start.5) | collective-permute-done | bytes 225312 | tf_op jit(solution)/shard_map/ppermute | solution.py:568
  40.9 6.8 %first.1 = (f32[16,24,256]{2,1,0:T(8,128)S(1)}, f32[16,24,256]{2,1,0:T(8,128)S(1)}, f32[10,24,256]{2,1,0:T(8,128)S(1)}, f32[16,8,128]{2,1,0:T(8,128)S(1)}, f32[1...) custom-call(f32[4,26,16,128]{3,2,1,0:T(8,128)S(1)} %all_gather.10.g, ...), custom_call_target="tpu_custom_call" | custom-call | tf_op jit(solution)/shard_map/first/pallas_call | solution.py:610
  47.6 20.5 %all_to_all.17.rec = f32[16,8,128]{2,1,0:T(8,128)S(1)} all-to-all(f32[16,8,128]{2,1,0:T(8,128)S(1)} %get-tuple-element.51), channel_id=1, replica_groups=mesh['gx'=4,'gy'=8,'gz'=16] {'gz'}, dimensions={0} | all-to-all | bytes 131072 | tf_op jit(solution)/shard_map/all_to_all | solution.py:623
  68.1 0.7 solve.1
  68.8 4.9 %collective-permute-start.6 = (f32[16,8,128]{2,1,0:T(8,128)S(1)}, f32[16,8,128]{2,1,0:T(8,128)S(1)}, u32[]{:S(2)}, u32[]{:S(2)}) collective-permute-start(f32[16,8,128]{2,1,0:T(8,128)S(1)} %get-tuple-element.56), channel_id=1, source_target_pairs={{0,16},{16,32},{32,48},{48,64},{64,80},{80,96},{96,112},{1,17},{17... | collective-permute-start | bytes 196616 | tf_op jit(solution)/shard_map/ppermute | solution.py:568
  73.7 1.9 %collective-permute-start.7 = (f32[16,8,128]{2,1,0:T(8,128)S(1)}, f32[16,8,128]{2,1,0:T(8,128)S(1)}, u32[]{:S(2)}, u32[]{:S(2)}) collective-permute-start(f32[16,8,128]{2,1,0:T(8,128)S(1)} %get-tuple-element.57), channel_id=1, source_target_pairs={{16,0},{32,16},{48,32},{64,48},{80,64},{96,80},{112,96},{17,1},{33... | collective-permute-start | bytes 196616 | tf_op jit(solution)/shard_map/ppermute | solution.py:568
  75.6 0.0 collective-permute-done.6.mid_p
  75.6 3.1 %collective-permute-done.7.mid_n = f32[16,8,128]{2,1,0:T(8,128)S(1)} collective-permute-done((f32[16,8,128]{2,1,0:T(8,128)S(1)}, f32[16,8,128]{2,1,0:T(8,128)S(1)}, u32[]{:S(2)}, u32[]{:S(2)}) %collective-permute-start.7) | collective-permute-done | bytes 65568 | tf_op jit(solution)/shard_map/ppermute | solution.py:568
  78.7 2.5 %second.1 = (f32[8,16,128]{2,1,0:T(8,128)}, f32[16,128]{1,0:T(8,128)S(1)}) custom-call(f32[16,8,128]{2,1,0:T(8,128)S(1)} %get-tuple-element.55.mid, f32[16,8,128]{2,1,0:T(8,128)S(1)} %collective-permute-done.6.mid_p, f32[16,8,128]{2,1,0:T(8,128)S(1)} %collective-permute-done.7.mid_n, f32[16,24,128]{2,1,0:T(8,128)S(1)} %get-tuple-element.54.mid_rhs, ...), custom_call_target="tpu_custom_call" | custom-call | tf_op jit(solution)/shard_map/second/pallas_call | solution.py:630
  81.2 11.0 %all_to_all.18 = f32[16,1,128]{2,1,0:T(1,128)S(1)} all-to-all(f32[16,1,128]{2,1,0:T(1,128)S(1)} %bitcast.10), channel_id=1, replica_groups=mesh['gx'=4,'gy'=8,'gz'=16] {'gz'}, dimensions={0} | all-to-all | bytes 16384 | tf_op jit(solution)/shard_map/all_to_all | solution.py:640
  92.3 0.5 multiply_bitcast_fusion
  (1 shorter events, 0.0 us)
Async XLA Ops:
  0.6 21.2 %copy-start = (f32[8,16,128]{2,1,0:T(8,128)S(1)}, f32[8,16,128]{2,1,0:T(8,128)}, u32[]{:S(2)}) copy-start(f32[8,16,128]{2,1,0:T(8,128)} %state.5) | copy-start | bytes 196612
  2.6 4.3 %collective-permute-start = (f32[8,16,128]{2,1,0:T(8,128)}, f32[8,16,128]{2,1,0:T(8,128)S(1)}, u32[]{:S(2)}, u32[]{:S(2)}) collective-permute-start(f32[8,16,128]{2,1,0:T(8,128)} %get-tuple-element.36), channel_id=1, source_target_pairs={{0,1},{1,2},{2,3},{3,4},{4,5},{5,6},{6,7},{7,8},{8,9},{9,10},{10,1... | collective-permute-start | bytes 196616 | tf_op jit(solution)/shard_map/ppermute | solution.py:582
  5.2 3.9 %collective-permute-start.1 = (f32[8,16,128]{2,1,0:T(8,128)}, f32[8,16,128]{2,1,0:T(8,128)S(1)}, u32[]{:S(2)}, u32[]{:S(2)}) collective-permute-start(f32[8,16,128]{2,1,0:T(8,128)} %get-tuple-element.37), channel_id=1, source_target_pairs={{0,15},{1,0},{2,1},{3,2},{4,3},{5,4},{6,5},{7,6},{8,7},{9,8},{10,9... | collective-permute-start | bytes 196616 | tf_op jit(solution)/shard_map/ppermute | solution.py:583
  22.1 11.5 %collective-permute-start.2 = (f32[13,40,128]{2,1,0:T(8,128)S(1)}, f32[13,40,128]{2,1,0:T(8,128)S(1)}, u32[]{:S(2)}, u32[]{:S(2)}) collective-permute-start(f32[13,40,128]{2,1,0:T(8,128)S(1)} %get-tuple-element.38), channel_id=1, source_target_pairs={{0,16},{16,32},{32,48},{48,64},{64,80},{80,96},{96,112},{1,17},{17... | collective-permute-start | bytes 798728 | tf_op jit(solution)/shard_map/ppermute | solution.py:568
  25.3 8.3 %collective-permute-start.3 = (f32[13,40,128]{2,1,0:T(8,128)S(1)}, f32[13,40,128]{2,1,0:T(8,128)S(1)}, u32[]{:S(2)}, u32[]{:S(2)}) collective-permute-start(f32[13,40,128]{2,1,0:T(8,128)S(1)} %get-tuple-element.39), channel_id=1, source_target_pairs={{16,0},{32,16},{48,32},{64,48},{80,64},{96,80},{112,96},{17,1},{33... | collective-permute-start | bytes 798728 | tf_op jit(solution)/shard_map/ppermute | solution.py:568
  27.4 10.0 %collective-permute-start.4 = (f32[11,40,128]{2,1,0:T(8,128)S(1)}, f32[11,40,128]{2,1,0:T(8,128)S(1)}, u32[]{:S(2)}, u32[]{:S(2)}) collective-permute-start(f32[11,40,128]{2,1,0:T(8,128)S(1)} %get-tuple-element.40), channel_id=1, source_target_pairs={{0,16},{16,32},{32,48},{48,64},{64,80},{80,96},{96,112},{1,17},{17... | collective-permute-start | bytes 675848 | tf_op jit(solution)/shard_map/ppermute | solution.py:568
  31.6 9.2 %collective-permute-start.5 = (f32[11,40,128]{2,1,0:T(8,128)S(1)}, f32[11,40,128]{2,1,0:T(8,128)S(1)}, u32[]{:S(2)}, u32[]{:S(2)}) collective-permute-start(f32[11,40,128]{2,1,0:T(8,128)S(1)} %get-tuple-element.41), channel_id=1, source_target_pairs={{16,0},{32,16},{48,32},{64,48},{80,64},{96,80},{112,96},{17,1},{33... | collective-permute-start | bytes 675848 | tf_op jit(solution)/shard_map/ppermute | solution.py:568
  68.8 6.8 %collective-permute-start.6 = (f32[16,8,128]{2,1,0:T(8,128)S(1)}, f32[16,8,128]{2,1,0:T(8,128)S(1)}, u32[]{:S(2)}, u32[]{:S(2)}) collective-permute-start(f32[16,8,128]{2,1,0:T(8,128)S(1)} %get-tuple-element.56), channel_id=1, source_target_pairs={{0,16},{16,32},{32,48},{48,64},{64,80},{80,96},{96,112},{1,17},{17... | collective-permute-start | bytes 196616 | tf_op jit(solution)/shard_map/ppermute | solution.py:568
  73.7 5.0 %collective-permute-start.7 = (f32[16,8,128]{2,1,0:T(8,128)S(1)}, f32[16,8,128]{2,1,0:T(8,128)S(1)}, u32[]{:S(2)}, u32[]{:S(2)}) collective-permute-start(f32[16,8,128]{2,1,0:T(8,128)S(1)} %get-tuple-element.57), channel_id=1, source_target_pairs={{16,0},{32,16},{48,32},{64,48},{80,64},{96,80},{112,96},{17,1},{33... | collective-permute-start | bytes 196616 | tf_op jit(solution)/shard_map/ppermute | solution.py:568

commit v6 on v5

--- a/solution.py
+++ b/solution.py
@@ -1,3 +1,4 @@
+import functools
 import math
 
 import jax
@@ -10,7 +11,7 @@
 CX, CY, CZ = 8, 16, 128
 ANISO = 200.0
 OMEGA = 0.8
-HY = 10
+HC, HS = 10, 9
 Y0 = 12
 HZ = 18
 YE = CY + 2 * Y0
@@ -119,9 +120,25 @@
     lax.fori_loop(0, planes, step, (wx[0] * (0.0 - here), here), unroll=unroll(planes))
 
 
-def pack_z_kernel(line, src, log_coef, lateral, state, mine, down, up):
+def pack_z_kernel(
+    line_far, src_far, log_coef_far, lateral_far, state_far, mine, down, up,
+    line, src, log_coef, lateral, state, sems,
+):
+    copies = [
+        pltpu.make_async_copy(far, near, sems.at[i])
+        for i, (far, near) in enumerate(
+            (
+                (lateral_far, lateral), (log_coef_far, log_coef), (src_far, src),
+                (state_far, state), (line_far, line),
+            )
+        )
+    ]
+    for copy in copies:
+        copy.start()
+    for copy in copies:
+        copy.wait()
     gz = lax.axis_index("gz")
-    cut = (line[gz] != line[jnp.minimum(gz + 1, 15)]).astype(jnp.float32)
+    cut = (line[0, 0, gz] != line[0, 0, jnp.minimum(gz + 1, 15)]).astype(jnp.float32)
     pick = (iota((CX * CY, CX), 0) // CY == iota((CX * CY, CX), 1)).astype(jnp.float32)
     rows = mm(pick, lateral[...])
     own = iota((CX * CY, CY), 0) % CY == iota((CX * CY, CY), 1)
@@ -147,18 +164,16 @@
 
 def pack_y_kernel(g, state, c_up, c_down, s_up, s_down):
     lane = iota((CY, CZ), 1)
-    none = jnp.zeros((HY, CZ), jnp.float32)
-
-    def put(refs, n, low, high):
-        at = pl.ds(HY * (n % 4), HY)
-        refs[0][n // 4, at] = high
-        refs[1][n // 4, at] = low
-
-    for coef, refs in ((1, (c_up, c_down)), (0, (s_up, s_down))):
+    planes = 4 * CX + TILES
+    for coef, h, up, down in ((1, HC, c_up, c_down), (0, HS, s_up, s_down)):
+
+        def put(n, plane):
+            up[h * n : h * n + h] = plane[CY - h :]
+            down[h * n : h * n + h] = plane[:h]
+
         for s in range(4):
             for i in range(CX):
-                plane = g[s, CX * coef + i]
-                put(refs, CX * s + i, plane[:HY], plane[CY - HY :])
+                put(CX * s + i, g[s, CX * coef + i])
         for t in range(TILES):
             plane = jnp.zeros((CY, CZ), jnp.float32)
             for x in range(3 * t, min(3 * t + 3, 4 * CX)):
@@ -166,21 +181,23 @@
                 move = off - 46 if coef else off + HZ
                 halo = pltpu.roll(g[x // CX, 2 * CX + x % CX], move % CZ, 1)
                 plane = jnp.where(lane >= off, halo, plane)
-            put(refs, 4 * CX + t, plane[:HY], plane[CY - HY :])
-    for i in range(CX):
-        put((c_up, c_down), 4 * CX + TILES + i, state[i, :HY], state[i, CY - HY :])
-    put((s_up, s_down), 4 * CX + TILES, none, none)
-    put((c_up, c_down), 5 * CX + TILES, none, none)
-
-
-def rows_at(ref, n):
-    return ref[n // 4, HY * (n % 4) : HY * (n % 4) + HY]
+            put(4 * CX + t, plane)
+        end = h * planes
+        if coef:
+            for i in range(CX):
+                up[end + i : end + i + 1] = state[i, CY - 1 :]
+                down[end + i : end + i + 1] = state[i, :1]
+            end += CX
+        none = jnp.zeros((up.shape[0] - end, CZ), jnp.float32)
+        up[end:] = none
+        down[end:] = none
 
 
 def place(out, lanes, low, own, high):
-    out[Y0 - HY : Y0, lanes] = low
+    h = low.shape[0]
+    out[Y0 - h : Y0, lanes] = low
     out[Y0 : Y0 + CY, lanes] = own
-    out[Y0 + CY : Y0 + CY + HY, lanes] = high
+    out[Y0 + CY : Y0 + CY + h, lanes] = high
 
 
 def edge_lanes(v, move):
@@ -194,11 +211,14 @@
     none = jnp.zeros((8, ZE), jnp.float32)
     out[0:8] = none
     out[YE - 8 :] = none
-    place(out, LOW, rows_at(yp, x), g[s, CX * coef + i], rows_at(yn, x))
+    h = HC if coef else HS
+    at = slice(h * x, h * x + h)
+    place(out, LOW, yp[at], g[s, CX * coef + i], yn[at])
     n, move = 4 * CX + x // 3, CZ - HZ - 2 * HZ * (x % 3)
+    at = slice(h * n, h * n + h)
     place(
-        out, HIGH, edge_lanes(rows_at(yp, n), move),
-        edge_lanes(g[s, 2 * CX + i], 64 * coef), edge_lanes(rows_at(yn, n), move),
+        out, HIGH, edge_lanes(yp[at], move),
+        edge_lanes(g[s, 2 * CX + i], 64 * coef), edge_lanes(yn[at], move),
     )
 
 
@@ -349,9 +369,8 @@
         se[at] = jnp.concatenate([mid, wide], 1)
     for i in range(CX):
         mid = pltpu.roll(jnp.concatenate([state[i], zero8], 0), 4, 0)
-        n = 4 * CX + TILES + i
-        at = HY * (n % 4)
-        under, over = cp[n // 4, at + HY - 1 : at + HY], cn[n // 4, at : at + 1]
+        n = HC * (4 * CX + TILES) + i
+        under, over = cp[n : n + 1], cn[n : n + 1]
         mid = jnp.where(row == 3, under, jnp.where(row == 20, over, mid))
         halo = pltpu.roll(jnp.concatenate([g[gx, 16 + i], zero8], 0), 4, 0)
         halo = pltpu.roll(halo, CZ - 32, 1)
@@ -479,28 +498,34 @@
     spread = ((to // 16 == frm % 8) & ((to % 8) // 2 == frm // 8)).astype(jnp.float32)
     mid = mid_pre[...] + pick_rows(spread, pick_lanes(rows, spread_z)).reshape(16, 8, ZM)
     out[...] = mid
-    row = iota((16, 8, ZM), 1)
-    rest = pltpu.roll(mid_rhs[:, 8:16], 4, 1)
-    up[...] = jnp.where(row == 0, rest, mid)
-    down[...] = jnp.where(row == 7, rest, mid)
+    for x in range(16):
+        up[6 * x : 6 * x + 5] = mid[x, 3:]
+        up[6 * x + 5 : 6 * x + 6] = mid_rhs[x, 12:13]
+        down[6 * x : 6 * x + 5] = mid[x, :5]
+        down[6 * x + 5 : 6 * x + 6] = mid_rhs[x, 11:12]
 
 
 def second_kernel(
-    mid, mid_p, mid_n, mid_rhs, mwx, mwy, mwz, minv, src_w, pre_w, c, wx, wy, wz, inv, se,
+    scale, mid, mid_p, mid_n, mid_rhs, mwx, mwy, mwz, minv, src_w, pre_w, c, wx, wy, wz, inv, se,
     adj, grad,
     mb, mva, mvb, sp, va, vb,
 ):
     gx = lax.axis_index("gx")
     mid_zero = jnp.zeros((YM, ZM), jnp.float32)
-    row = iota((YM, ZM), 0)
+    none = jnp.zeros((8, ZM), jnp.float32)
+    mb[...] = mid_rhs[...]
     for x in range(16):
-        out = jnp.concatenate([pltpu.roll(v, 4, 0) for v in (mid_p[x], mid[x], mid_n[x])], 0)
-        mb[x] = jnp.where((row == 4) | (row == 19), out, mid_rhs[x])
+        mb[x, 4:5] = mid_p[6 * x + 5 : 6 * x + 6]
+        mb[x, 19:20] = mid_n[6 * x + 5 : 6 * x + 6]
     for ref in (mva, mvb):
         for at in (0, 1, 18, 19):
             ref[at] = mid_zero
     for x in range(16):
-        mva[x + 2] = jnp.concatenate([mid_p[x], mid[x], mid_n[x]], 0)
+        mva[x + 2, 0:8] = none
+        mva[x + 2, 16:24] = none
+        mva[x + 2, 3:8] = mid_p[6 * x : 6 * x + 5]
+        mva[x + 2, 8:16] = mid[x]
+        mva[x + 2, 16:21] = mid_n[6 * x : 6 * x + 5]
     a, o = mva.at[1:19], mvb.at[1:19]
     sweep(a, o, mb, mwx, mwy, mwz, minv, 16)
     sweep(o, a, mb, mwx, mwy, mwz, minv, 16)
@@ -546,7 +571,7 @@
     _, acc = lax.fori_loop(
         0, CX, terms, (first, jnp.zeros((YW, CZ), jnp.float32)), unroll=8
     )
-    grad[...] = pltpu.roll(acc, YW - 4, 0)[:CY]
+    grad[...] = pltpu.roll(acc, YW - 4, 0)[:CY] * scale
 
 
 def f32(*shape):
@@ -558,7 +583,7 @@
 
 
 def params():
-    return pltpu.CompilerParams(vmem_limit_bytes=20 << 20)
+    return pltpu.CompilerParams(vmem_limit_bytes=16 << 20)
 
 
 def both_ways(up, down, axis):
@@ -570,14 +595,22 @@
 
 def per_device(source, state, log_coef, lateral, owners):
     block = f32(CX, CY, CZ)
-    smem = pl.BlockSpec(memory_space=pltpu.SMEM)
-    vmem = pl.BlockSpec(memory_space=pltpu.VMEM)
+    far = pl.BlockSpec(memory_space=pltpu.HBM)
     mine, down, up = pl.pallas_call(
         pack_z_kernel,
         out_shape=(f32(3 * CX + 2, CY, CZ), block, block),
-        in_specs=[smem, vmem, vmem, vmem, vmem],
+        in_specs=[far] * 5,
+        scratch_shapes=[
+            pltpu.SMEM((1, 1, 16), jnp.int32),
+            vm(CX, CY, CZ), vm(CX, CY, CZ), vm(CX, CY), vm(CX, CY, CZ),
+            pltpu.SemaphoreType.DMA((5,)),
+        ],
+        compiler_params=params(),
         name="pack_z",
-    )(owners[0, 0], source, log_coef, lateral, state)
+    )(*[
+        pltpu.with_memory_space_constraint(v, pltpu.HBM)
+        for v in (owners, source, log_coef, lateral, state)
+    ])
     gz, count = lax.axis_index("gz"), lax.axis_size("gz")
     before = lax.ppermute(up, "gz", [(i, (i + 1) % count) for i in range(count)])
     after = lax.ppermute(down, "gz", [(i, (i - 1) % count) for i in range(count)])
@@ -587,7 +620,7 @@
     fine, fine1, fine2 = (32, YE, ZE), (33, YE, ZE), (34, YE, ZE)
     mid, mid1, mid2 = (16, YM, ZM), (17, YM, ZM), (18, YM, ZM)
     win, win1, win2 = (XW, YW, ZE), (XW + 1, YW, ZE), (XW + 2, YW, ZE)
-    c_rows, s_rows = f32(13, 4 * HY, CZ), f32(11, 4 * HY, CZ)
+    c_rows, s_rows = f32(440, CZ), f32(392, CZ)
     c_up, c_down, s_up, s_down = pl.pallas_call(
         pack_y_kernel,
         out_shape=(c_rows, c_rows, s_rows, s_rows),
@@ -623,13 +656,14 @@
     rec = lax.all_to_all(ends, "gz", 0, 0, tiled=True)
     tile = f32(16, 8, ZM)
     mid_init, up, down = pl.pallas_call(
-        solve_kernel, out_shape=(tile, tile, tile), compiler_params=params(), name="solve"
+        solve_kernel, out_shape=(tile, f32(96, ZM), f32(96, ZM)), compiler_params=params(), name="solve"
     )(rec, block_s, mid_pre, mid_rhs)
     mid_p, mid_n = both_ways(up, down, "gy")
 
+    scale = -1.0 / math.sqrt(source.shape[2] * count)
     adj, grad = pl.pallas_call(
-        second_kernel,
-        out_shape=(block, f32(CY, CZ)),
+        functools.partial(second_kernel, scale),
+        out_shape=(f32(CX, CY, CZ), f32(CY, CZ)),
         scratch_shapes=[
             vm(*mid), vm(20, YM, ZM), vm(20, YM, ZM), vm(8, YM, ZE), vm(*win2), vm(*win2),
         ],
@@ -638,8 +672,7 @@
     )(mid_init, mid_p, mid_n, mid_rhs, mwx, mwy, mwz, minv,
       src_w, pre_w, c_w, wx_w, wy_w, wz_w, inv_w, se)
     sums = lax.all_to_all(grad, "gz", 0, 0, tiled=True)
-    total = jnp.sum(sums[:, :CX], axis=0)[:, None]
-    return adj, total * (-1.0 / math.sqrt(source.shape[2] * lax.axis_size("gz")))
+    return adj, jnp.sum(sums[:, :CX], axis=0)[:, None]
 
 
 def solution(mesh):

time: 93.1 us -> 90.9 us (0.976)
  no operation moved by 1% of the time
where the time goes in v6:
time: 90.9 us; the launch traced here: 90.6 us
  blocking collectives  43.6 us (48%)
  starting transfers between devices  20.9 us (23%)
  Pallas kernels  15.1 us (17%)
  waiting for transfers between devices  9.66 us (11%)
    all_to_all x1, blocking collectives, per_device(): rec = lax.all_to_all(ends, 'gz', 0, 0, tiled=True)  20.6 us
    ppermute x6, starting transfers between devices, both_ways(): return (lax.ppermute(up, axis, higher), lax.ppermute(down, axis, lower))  18.2 us
    all_gather x1, blocking collectives, per_device(): g = lax.all_gather(mine, 'gx')  12 us
    all_to_all x1, blocking collectives, per_device(): sums = lax.all_to_all(grad, 'gz', 0, 0, tiled=True)  11 us
    pallas_call x1, Pallas kernels, per_device(): pl.pallas_call(first_kernel, out_shape=(f32(*win), f32(*win), f32(CX + 2,...  6.59 us
    ppermute x6, waiting for transfers between devices, both_ways(): return (lax.ppermute(up, axis, higher), lax.ppermute(down, axis, lower))  5.97 us
    pallas_call x1, Pallas kernels, per_device(): pl.pallas_call(coef_kernel, out_shape=(f32(*fine1), f32(*fine), f32(*fine...  3.73 us
    ppermute x1, starting transfers between devices, per_device(): lax.ppermute(up, 'gz', [(i, (i + 1) % count) for i in range(count)])  2.67 us
  transfers between devices with their start and end apart: 8, of which 4 were waited for; matrix products, arithmetic and copies ran while one was open for 0% of the time, Pallas kernels for 4%

profile of v6, /device:TPU:19, one launch (start us, length us, event | category | flops | bytes accessed | tf_op | source)
XLA Modules:
  0.0 90.6 jit_solution(3468998979850781078)
XLA Ops:
  0.6 0.0 copy-start
  0.6 1.3 %pack_z.1 = (f32[26,16,128]{2,1,0:T(8,128)S(1)}, f32[8,16,128]{2,1,0:T(8,128)S(1)}, f32[8,16,128]{2,1,0:T(8,128)S(1)}) custom-call(s32[1,1,16]{2,1,0:T(1,128)} %line_far.1, f32[8,16,128]{2,1,0:T(8,128)} %src_far.1, f32[8,16,128]{2,1,0:T(8,128)} %log_coef_far.1, f32[8,16]{1,0:T(8,128)} %lateral_far.1, f32[8,16,128]{2,1,0:T(8,128)} %state.3), custom_call_target="tpu_custom_call" | custom-call | tf_op jit(solution)/shard_map/pack_z/pallas_call | solution.py:599
  2.0 2.7 %collective-permute-start = (f32[8,16,128]{2,1,0:T(8,128)S(1)}, f32[8,16,128]{2,1,0:T(8,128)S(1)}, u32[]{:S(2)}, u32[]{:S(2)}) collective-permute-start(f32[8,16,128]{2,1,0:T(8,128)S(1)} %get-tuple-element.36), channel_id=1, source_target_pairs={{0,1},{1,2},{2,3},{3,4},{4,5},{5,6},{6,7},{7,8},{8,9},{9,10},{10,1... | collective-permute-start | bytes 196616 | tf_op jit(solution)/shard_map/ppermute | solution.py:615
  4.7 0.0 collective-permute-start.1
  4.7 1.3 %collective-permute-done = f32[8,16,128]{2,1,0:T(8,128)S(1)} collective-permute-done((f32[8,16,128]{2,1,0:T(8,128)S(1)}, f32[8,16,128]{2,1,0:T(8,128)S(1)}, u32[]{:S(2)}, u32[]{:S(2)}) %collective-permute-start) | collective-permute-done | bytes 65568 | tf_op jit(solution)/shard_map/ppermute | solution.py:615
  6.0 2.4 %collective-permute-done.1 = f32[8,16,128]{2,1,0:T(8,128)S(1)} collective-permute-done((f32[8,16,128]{2,1,0:T(8,128)S(1)}, f32[8,16,128]{2,1,0:T(8,128)S(1)}, u32[]{:S(2)}, u32[]{:S(2)}) %collective-permute-start.1) | collective-permute-done | bytes 65568 | tf_op jit(solution)/shard_map/ppermute | solution.py:616
  8.4 12.0 %all_gather.10.g = f32[4,26,16,128]{3,2,1,0:T(8,128)S(1)} all-gather(f32[1,26,16,128]{3,2,1,0:T(8,128)S(1)} %bitcast_dynamic-update-slice_fusion), channel_id=1, replica_groups=mesh['gx'=4,'gy'=8,'gz'=16] {'gx'}, dimensions={0}, use_global_device_ids=true | all-gather | bytes 1064960 | tf_op jit(solution)/shard_map/all_gather | solution.py:619
  20.3 0.0 copy-done
  20.3 0.2 pack_y.1
  20.6 3.2 %collective-permute-start.2 = (f32[440,128]{1,0:T(8,128)S(1)}, f32[440,128]{1,0:T(8,128)S(1)}, u32[]{:S(2)}, u32[]{:S(2)}) collective-permute-start(f32[440,128]{1,0:T(8,128)S(1)} %get-tuple-element.38), channel_id=1, source_target_pairs={{0,16},{16,32},{32,48},{48,64},{64,80},{80,96},{96,112},{1,17},{17... | collective-permute-start | bytes 675848 | tf_op jit(solution)/shard_map/ppermute | solution.py:593
  23.8 2.1 %collective-permute-start.3 = (f32[440,128]{1,0:T(8,128)S(1)}, f32[440,128]{1,0:T(8,128)S(1)}, u32[]{:S(2)}, u32[]{:S(2)}) collective-permute-start(f32[440,128]{1,0:T(8,128)S(1)} %get-tuple-element.39), channel_id=1, source_target_pairs={{16,0},{32,16},{48,32},{64,48},{80,64},{96,80},{112,96},{17,1},{33... | collective-permute-start | bytes 675848 | tf_op jit(solution)/shard_map/ppermute | solution.py:593
  25.9 4.3 %collective-permute-start.4 = (f32[392,128]{1,0:T(8,128)S(1)}, f32[392,128]{1,0:T(8,128)S(1)}, u32[]{:S(2)}, u32[]{:S(2)}) collective-permute-start(f32[392,128]{1,0:T(8,128)S(1)} %get-tuple-element.40), channel_id=1, source_target_pairs={{0,16},{16,32},{32,48},{48,64},{64,80},{80,96},{96,112},{1,17},{17... | collective-permute-start | bytes 602120 | tf_op jit(solution)/shard_map/ppermute | solution.py:593
  30.1 1.9 %collective-permute-start.5 = (f32[392,128]{1,0:T(8,128)S(1)}, f32[392,128]{1,0:T(8,128)S(1)}, u32[]{:S(2)}, u32[]{:S(2)}) collective-permute-start(f32[392,128]{1,0:T(8,128)S(1)} %get-tuple-element.41), channel_id=1, source_target_pairs={{16,0},{32,16},{48,32},{64,48},{80,64},{96,80},{112,96},{17,1},{33... | collective-permute-start | bytes 602120 | tf_op jit(solution)/shard_map/ppermute | solution.py:593
  32.1 0.0 collective-permute-done.2.yp.cp
  32.1 0.0 collective-permute-done.3.yn.cn
  32.1 3.7 %coef.1 = (f32[33,40,256]{2,1,0:T(8,128)S(1)}, f32[32,40,256]{2,1,0:T(8,128)S(1)}, f32[32,40,256]{2,1,0:T(8,128)S(1)}, f32[32,40,256]{2,1,0:T(8,128)S(1)}, f32[1...) custom-call(f32[4,26,16,128]{3,2,1,0:T(8,128)S(1)} %all_gather.10.g,, ...), custom_call_target="tpu_custom_call" | custom-call | tf_op jit(solution)/shard_map/coef/pallas_call | solution.py:632
  35.8 0.0 collective-permute-done.4.yp
  35.8 3.1 %collective-permute-done.5.yn = f32[392,128]{1,0:T(8,128)S(1)} collective-permute-done((f32[392,128]{1,0:T(8,128)S(1)}, f32[392,128]{1,0:T(8,128)S(1)}, u32[]{:S(2)}, u32[]{:S(2)}) %collective-permute-start.5) | collective-permute-done | bytes 200736 | tf_op jit(solution)/shard_map/ppermute | solution.py:593
  38.9 6.6 %first.1 = (f32[16,24,256]{2,1,0:T(8,128)S(1)}, f32[16,24,256]{2,1,0:T(8,128)S(1)}, f32[10,24,256]{2,1,0:T(8,128)S(1)}, f32[16,8,128]{2,1,0:T(8,128)S(1)}, f32[1...) custom-call(f32[4,26,16,128]{3,2,1,0:T(8,128)S(1)} %all_gather.10.g, ...), custom_call_target="tpu_custom_call" | custom-call | tf_op jit(solution)/shard_map/first/pallas_call | solution.py:643
  45.5 20.6 %all_to_all.17.rec = f32[16,8,128]{2,1,0:T(8,128)S(1)} all-to-all(f32[16,8,128]{2,1,0:T(8,128)S(1)} %get-tuple-element.51), channel_id=1, replica_groups=mesh['gx'=4,'gy'=8,'gz'=16] {'gz'}, dimensions={0} | all-to-all | bytes 131072 | tf_op jit(solution)/shard_map/all_to_all | solution.py:656
  66.1 0.7 solve.1
  66.8 4.9 %collective-permute-start.6 = (f32[96,128]{1,0:T(8,128)S(1)}, f32[96,128]{1,0:T(8,128)S(1)}, u32[]{:S(2)}, u32[]{:S(2)}) collective-permute-start(f32[96,128]{1,0:T(8,128)S(1)} %get-tuple-element.56), channel_id=1, source_target_pairs={{0,16},{16,32},{32,48},{48,64},{64,80},{80,96},{96,112},{1,17},{17... | collective-permute-start | bytes 147464 | tf_op jit(solution)/shard_map/ppermute | solution.py:593
  71.6 1.9 %collective-permute-start.7 = (f32[96,128]{1,0:T(8,128)S(1)}, f32[96,128]{1,0:T(8,128)S(1)}, u32[]{:S(2)}, u32[]{:S(2)}) collective-permute-start(f32[96,128]{1,0:T(8,128)S(1)} %get-tuple-element.57), channel_id=1, source_target_pairs={{16,0},{32,16},{48,32},{64,48},{80,64},{96,80},{112,96},{17,1},{33... | collective-permute-start | bytes 147464 | tf_op jit(solution)/shard_map/ppermute | solution.py:593
  73.5 0.0 collective-permute-done.6.mid_p
  73.6 2.9 %collective-permute-done.7.mid_n = f32[96,128]{1,0:T(8,128)S(1)} collective-permute-done((f32[96,128]{1,0:T(8,128)S(1)}, f32[96,128]{1,0:T(8,128)S(1)}, u32[]{:S(2)}, u32[]{:S(2)}) %collective-permute-start.7) | collective-permute-done | bytes 49184 | tf_op jit(solution)/shard_map/ppermute | solution.py:593
  76.5 2.5 %second.1 = (f32[8,16,128]{2,1,0:T(8,128)}, f32[16,128]{1,0:T(8,128)S(1)}) custom-call(f32[16,8,128]{2,1,0:T(8,128)S(1)} %get-tuple-element.55.mid, f32[96,128]{1,0:T(8,128)S(1)} %collective-permute-done.6.mid_p, f32[96,128]{1,0:T(8,128)S(1)} %collective-permute-done.7.mid_n, f32[16,24,128]{2,1,0:T(8,128)S(1)} %get-tuple-element.54.mid_rhs, ...), custom_call_target="tpu_custom_call" | custom-call | tf_op jit(solution)/shard_map/second/pallas_call | solution.py:664
  79.0 11.0 %all_to_all.18 = f32[16,1,128]{2,1,0:T(1,128)S(1)} all-to-all(f32[16,1,128]{2,1,0:T(1,128)S(1)} %bitcast.9), channel_id=1, replica_groups=mesh['gx'=4,'gy'=8,'gz'=16] {'gz'}, dimensions={0} | all-to-all | bytes 16384 | tf_op jit(solution)/shard_map/all_to_all | solution.py:674
  90.0 0.5 slice_reduce_fusion
  (1 shorter events, 0.0 us)
Async XLA Ops:
  0.6 19.7 %copy-start = (f32[8,16,128]{2,1,0:T(8,128)S(1)}, f32[8,16,128]{2,1,0:T(8,128)}, u32[]{:S(2)}) copy-start(f32[8,16,128]{2,1,0:T(8,128)} %state.3) | copy-start | bytes 196612
  2.0 4.0 %collective-permute-start = (f32[8,16,128]{2,1,0:T(8,128)S(1)}, f32[8,16,128]{2,1,0:T(8,128)S(1)}, u32[]{:S(2)}, u32[]{:S(2)}) collective-permute-start(f32[8,16,128]{2,1,0:T(8,128)S(1)} %get-tuple-element.36), channel_id=1, source_target_pairs={{0,1},{1,2},{2,3},{3,4},{4,5},{5,6},{6,7},{7,8},{8,9},{9,10},{10,1... | collective-permute-start | bytes 196616 | tf_op jit(solution)/shard_map/ppermute | solution.py:615
  4.7 3.7 %collective-permute-start.1 = (f32[8,16,128]{2,1,0:T(8,128)S(1)}, f32[8,16,128]{2,1,0:T(8,128)S(1)}, u32[]{:S(2)}, u32[]{:S(2)}) collective-permute-start(f32[8,16,128]{2,1,0:T(8,128)S(1)} %get-tuple-element.37), channel_id=1, source_target_pairs={{0,15},{1,0},{2,1},{3,2},{4,3},{5,4},{6,5},{7,6},{8,7},{9,8},{10,9... | collective-permute-start | bytes 196616 | tf_op jit(solution)/shard_map/ppermute | solution.py:616
  20.6 11.5 %collective-permute-start.2 = (f32[440,128]{1,0:T(8,128)S(1)}, f32[440,128]{1,0:T(8,128)S(1)}, u32[]{:S(2)}, u32[]{:S(2)}) collective-permute-start(f32[440,128]{1,0:T(8,128)S(1)} %get-tuple-element.38), channel_id=1, source_target_pairs={{0,16},{16,32},{32,48},{48,64},{64,80},{80,96},{96,112},{1,17},{17... | collective-permute-start | bytes 675848 | tf_op jit(solution)/shard_map/ppermute | solution.py:593
  23.8 8.3 %collective-permute-start.3 = (f32[440,128]{1,0:T(8,128)S(1)}, f32[440,128]{1,0:T(8,128)S(1)}, u32[]{:S(2)}, u32[]{:S(2)}) collective-permute-start(f32[440,128]{1,0:T(8,128)S(1)} %get-tuple-element.39), channel_id=1, source_target_pairs={{16,0},{32,16},{48,32},{64,48},{80,64},{96,80},{112,96},{17,1},{33... | collective-permute-start | bytes 675848 | tf_op jit(solution)/shard_map/ppermute | solution.py:593
  25.9 10.0 %collective-permute-start.4 = (f32[392,128]{1,0:T(8,128)S(1)}, f32[392,128]{1,0:T(8,128)S(1)}, u32[]{:S(2)}, u32[]{:S(2)}) collective-permute-start(f32[392,128]{1,0:T(8,128)S(1)} %get-tuple-element.40), channel_id=1, source_target_pairs={{0,16},{16,32},{32,48},{48,64},{64,80},{80,96},{96,112},{1,17},{17... | collective-permute-start | bytes 602120 | tf_op jit(solution)/shard_map/ppermute | solution.py:593
  30.1 8.8 %collective-permute-start.5 = (f32[392,128]{1,0:T(8,128)S(1)}, f32[392,128]{1,0:T(8,128)S(1)}, u32[]{:S(2)}, u32[]{:S(2)}) collective-permute-start(f32[392,128]{1,0:T(8,128)S(1)} %get-tuple-element.41), channel_id=1, source_target_pairs={{16,0},{32,16},{48,32},{64,48},{80,64},{96,80},{112,96},{17,1},{33... | collective-permute-start | bytes 602120 | tf_op jit(solution)/shard_map/ppermute | solution.py:593
  66.8 6.8 %collective-permute-start.6 = (f32[96,128]{1,0:T(8,128)S(1)}, f32[96,128]{1,0:T(8,128)S(1)}, u32[]{:S(2)}, u32[]{:S(2)}) collective-permute-start(f32[96,128]{1,0:T(8,128)S(1)} %get-tuple-element.56), channel_id=1, source_target_pairs={{0,16},{16,32},{32,48},{48,64},{64,80},{80,96},{96,112},{1,17},{17... | collective-permute-start | bytes 147464 | tf_op jit(solution)/shard_map/ppermute | solution.py:593
  71.6 4.8 %collective-permute-start.7 = (f32[96,128]{1,0:T(8,128)S(1)}, f32[96,128]{1,0:T(8,128)S(1)}, u32[]{:S(2)}, u32[]{:S(2)}) collective-permute-start(f32[96,128]{1,0:T(8,128)S(1)} %get-tuple-element.57), channel_id=1, source_target_pairs={{16,0},{32,16},{48,32},{64,48},{80,64},{96,80},{112,96},{17,1},{33... | collective-permute-start | bytes 147464 | tf_op jit(solution)/shard_map/ppermute | solution.py:593

commit v7 on v6

--- a/solution.py
+++ b/solution.py
@@ -135,15 +135,16 @@
     ]
     for copy in copies:
         copy.start()
-    for copy in copies:
-        copy.wait()
+    copies[0].wait()
     gz = lax.axis_index("gz")
-    cut = (line[0, 0, gz] != line[0, 0, jnp.minimum(gz + 1, 15)]).astype(jnp.float32)
     pick = (iota((CX * CY, CX), 0) // CY == iota((CX * CY, CX), 1)).astype(jnp.float32)
-    rows = mm(pick, lateral[...])
+    rows = pick_rows(pick, lateral[...])
     own = iota((CX * CY, CY), 0) % CY == iota((CX * CY, CY), 1)
     rows = jnp.sum(jnp.where(own, rows, 0.0), axis=1, keepdims=True)
     rows = jnp.broadcast_to(rows, (CX * CY, CZ)).reshape(CX, CY, CZ)
+    for copy in copies[1:]:
+        copy.wait()
+    cut = (line[0, 0, gz] != line[0, 0, jnp.minimum(gz + 1, 15)]).astype(jnp.float32)
     c = jnp.exp(log_coef[...] + rows)
     s = src[...]
     mine[0:CX] = s
@@ -287,7 +288,7 @@
         t[m] = pick_rows(rows, c[2 * m + 1] + c[2 * m + 2])
         return carry
 
-    lax.fori_loop(0, 16, coarse, 0, unroll=8)
+    lax.fori_loop(0, 16, coarse, 0, unroll=16)
     mid_zero = jnp.zeros((YM, ZM), jnp.float32)
     mc[0] = mid_zero
     mc[17] = mid_zero
@@ -347,7 +348,7 @@
         t[m] = pick_rows(rows, one + two)
         return fx
 
-    lax.fori_loop(0, 16, coarse, wx[0] * (0.0 - vb[1]), unroll=8)
+    lax.fori_loop(0, 16, coarse, wx[0] * (0.0 - vb[1]), unroll=16)
     mb[...] = pick_lanes(t[...].reshape(16 * YM, ZE), fold_z()).reshape(16, YM, ZM)
     mid_zero = jnp.zeros((YM, ZM), jnp.float32)
     for ref in (mva, mvb):

time: 90.9 us -> 90.5 us (level)
  no operation moved by 1% of the time
where the time goes in v7:
time: 90.5 us; the launch traced here: 90.2 us
  blocking collectives  43.6 us (48%)
  starting transfers between devices  20.9 us (23%)
  Pallas kernels  14.4 us (16%)
  waiting for transfers between devices  9.94 us (11%)
    all_to_all x1, blocking collectives, per_device(): rec = lax.all_to_all(ends, 'gz', 0, 0, tiled=True)  20.6 us
    ppermute x6, starting transfers between devices, both_ways(): return (lax.ppermute(up, axis, higher), lax.ppermute(down, axis, lower))  18.2 us
    all_gather x1, blocking collectives, per_device(): g = lax.all_gather(mine, 'gx')  12 us
    all_to_all x1, blocking collectives, per_device(): sums = lax.all_to_all(grad, 'gz', 0, 0, tiled=True)  11 us
    ppermute x6, waiting for transfers between devices, both_ways(): return (lax.ppermute(up, axis, higher), lax.ppermute(down, axis, lower))  6.25 us
    pallas_call x1, Pallas kernels, per_device(): pl.pallas_call(first_kernel, out_shape=(f32(*win), f32(*win), f32(CX + 2,...  6.23 us
    pallas_call x1, Pallas kernels, per_device(): pl.pallas_call(coef_kernel, out_shape=(f32(*fine1), f32(*fine), f32(*fine...  3.45 us
    ppermute x1, starting transfers between devices, per_device(): lax.ppermute(up, 'gz', [(i, (i + 1) % count) for i in range(count)])  2.67 us
  transfers between devices with their start and end apart: 8, of which 4 were waited for; matrix products, arithmetic and copies ran while one was open for 0% of the time, Pallas kernels for 4%

profile of v7, /device:TPU:19, one launch (start us, length us, event | category | flops | bytes accessed | tf_op | source)
XLA Modules:
  0.0 90.2 jit_solution(7353012177506135845)
XLA Ops:
  0.6 0.0 copy-start
  0.6 1.3 %pack_z.1 = (f32[26,16,128]{2,1,0:T(8,128)S(1)}, f32[8,16,128]{2,1,0:T(8,128)S(1)}, f32[8,16,128]{2,1,0:T(8,128)S(1)}) custom-call(s32[1,1,16]{2,1,0:T(1,128)} %line_far.1, f32[8,16,128]{2,1,0:T(8,128)} %src_far.1, f32[8,16,128]{2,1,0:T(8,128)} %log_coef_far.1, f32[8,16]{1,0:T(8,128)} %lateral_far.1, f32[8,16,128]{2,1,0:T(8,128)} %state.3), custom_call_target="tpu_custom_call" | custom-call | tf_op jit(solution)/shard_map/pack_z/pallas_call | solution.py:600
  2.0 2.7 %collective-permute-start = (f32[8,16,128]{2,1,0:T(8,128)S(1)}, f32[8,16,128]{2,1,0:T(8,128)S(1)}, u32[]{:S(2)}, u32[]{:S(2)}) collective-permute-start(f32[8,16,128]{2,1,0:T(8,128)S(1)} %get-tuple-element.36), channel_id=1, source_target_pairs={{0,1},{1,2},{2,3},{3,4},{4,5},{5,6},{6,7},{7,8},{8,9},{9,10},{10,1... | collective-permute-start | bytes 196616 | tf_op jit(solution)/shard_map/ppermute | solution.py:616
  4.6 0.0 collective-permute-start.1
  4.6 1.3 %collective-permute-done = f32[8,16,128]{2,1,0:T(8,128)S(1)} collective-permute-done((f32[8,16,128]{2,1,0:T(8,128)S(1)}, f32[8,16,128]{2,1,0:T(8,128)S(1)}, u32[]{:S(2)}, u32[]{:S(2)}) %collective-permute-start) | collective-permute-done | bytes 65568 | tf_op jit(solution)/shard_map/ppermute | solution.py:616
  6.0 2.4 %collective-permute-done.1 = f32[8,16,128]{2,1,0:T(8,128)S(1)} collective-permute-done((f32[8,16,128]{2,1,0:T(8,128)S(1)}, f32[8,16,128]{2,1,0:T(8,128)S(1)}, u32[]{:S(2)}, u32[]{:S(2)}) %collective-permute-start.1) | collective-permute-done | bytes 65568 | tf_op jit(solution)/shard_map/ppermute | solution.py:617
  8.3 12.0 %all_gather.10.g = f32[4,26,16,128]{3,2,1,0:T(8,128)S(1)} all-gather(f32[1,26,16,128]{3,2,1,0:T(8,128)S(1)} %bitcast_dynamic-update-slice_fusion), channel_id=1, replica_groups=mesh['gx'=4,'gy'=8,'gz'=16] {'gx'}, dimensions={0}, use_global_device_ids=true | all-gather | bytes 1064960 | tf_op jit(solution)/shard_map/all_gather | solution.py:620
  20.3 0.0 copy-done
  20.3 0.2 pack_y.1
  20.5 3.2 %collective-permute-start.2 = (f32[440,128]{1,0:T(8,128)S(1)}, f32[440,128]{1,0:T(8,128)S(1)}, u32[]{:S(2)}, u32[]{:S(2)}) collective-permute-start(f32[440,128]{1,0:T(8,128)S(1)} %get-tuple-element.38), channel_id=1, source_target_pairs={{0,16},{16,32},{32,48},{48,64},{64,80},{80,96},{96,112},{1,17},{17... | collective-permute-start | bytes 675848 | tf_op jit(solution)/shard_map/ppermute | solution.py:594
  23.7 2.1 %collective-permute-start.3 = (f32[440,128]{1,0:T(8,128)S(1)}, f32[440,128]{1,0:T(8,128)S(1)}, u32[]{:S(2)}, u32[]{:S(2)}) collective-permute-start(f32[440,128]{1,0:T(8,128)S(1)} %get-tuple-element.39), channel_id=1, source_target_pairs={{16,0},{32,16},{48,32},{64,48},{80,64},{96,80},{112,96},{17,1},{33... | collective-permute-start | bytes 675848 | tf_op jit(solution)/shard_map/ppermute | solution.py:594
  25.8 4.3 %collective-permute-start.4 = (f32[392,128]{1,0:T(8,128)S(1)}, f32[392,128]{1,0:T(8,128)S(1)}, u32[]{:S(2)}, u32[]{:S(2)}) collective-permute-start(f32[392,128]{1,0:T(8,128)S(1)} %get-tuple-element.40), channel_id=1, source_target_pairs={{0,16},{16,32},{32,48},{48,64},{64,80},{80,96},{96,112},{1,17},{17... | collective-permute-start | bytes 602120 | tf_op jit(solution)/shard_map/ppermute | solution.py:594
  30.1 1.9 %collective-permute-start.5 = (f32[392,128]{1,0:T(8,128)S(1)}, f32[392,128]{1,0:T(8,128)S(1)}, u32[]{:S(2)}, u32[]{:S(2)}) collective-permute-start(f32[392,128]{1,0:T(8,128)S(1)} %get-tuple-element.41), channel_id=1, source_target_pairs={{16,0},{32,16},{48,32},{64,48},{80,64},{96,80},{112,96},{17,1},{33... | collective-permute-start | bytes 602120 | tf_op jit(solution)/shard_map/ppermute | solution.py:594
  32.0 0.0 collective-permute-done.2.yp.cp
  32.0 0.0 collective-permute-done.3.yn.cn
  32.0 3.4 %coef.1 = (f32[33,40,256]{2,1,0:T(8,128)S(1)}, f32[32,40,256]{2,1,0:T(8,128)S(1)}, f32[32,40,256]{2,1,0:T(8,128)S(1)}, f32[32,40,256]{2,1,0:T(8,128)S(1)}, f32[1...) custom-call(f32[4,26,16,128]{3,2,1,0:T(8,128)S(1)} %all_gather.10.g,, ...), custom_call_target="tpu_custom_call" | custom-call | tf_op jit(solution)/shard_map/coef/pallas_call | solution.py:633
  35.5 0.0 collective-permute-done.4.yp
  35.5 3.3 %collective-permute-done.5.yn = f32[392,128]{1,0:T(8,128)S(1)} collective-permute-done((f32[392,128]{1,0:T(8,128)S(1)}, f32[392,128]{1,0:T(8,128)S(1)}, u32[]{:S(2)}, u32[]{:S(2)}) %collective-permute-start.5) | collective-permute-done | bytes 200736 | tf_op jit(solution)/shard_map/ppermute | solution.py:594
  38.8 6.2 %first.1 = (f32[16,24,256]{2,1,0:T(8,128)S(1)}, f32[16,24,256]{2,1,0:T(8,128)S(1)}, f32[10,24,256]{2,1,0:T(8,128)S(1)}, f32[16,8,128]{2,1,0:T(8,128)S(1)}, f32[1...) custom-call(f32[4,26,16,128]{3,2,1,0:T(8,128)S(1)} %all_gather.10.g, ...), custom_call_target="tpu_custom_call" | custom-call | tf_op jit(solution)/shard_map/first/pallas_call | solution.py:644
  45.1 20.6 %all_to_all.17.rec = f32[16,8,128]{2,1,0:T(8,128)S(1)} all-to-all(f32[16,8,128]{2,1,0:T(8,128)S(1)} %get-tuple-element.51), channel_id=1, replica_groups=mesh['gx'=4,'gy'=8,'gz'=16] {'gz'}, dimensions={0} | all-to-all | bytes 131072 | tf_op jit(solution)/shard_map/all_to_all | solution.py:657
  65.7 0.7 solve.1
  66.4 4.9 %collective-permute-start.6 = (f32[96,128]{1,0:T(8,128)S(1)}, f32[96,128]{1,0:T(8,128)S(1)}, u32[]{:S(2)}, u32[]{:S(2)}) collective-permute-start(f32[96,128]{1,0:T(8,128)S(1)} %get-tuple-element.56), channel_id=1, source_target_pairs={{0,16},{16,32},{32,48},{48,64},{64,80},{80,96},{96,112},{1,17},{17... | collective-permute-start | bytes 147464 | tf_op jit(solution)/shard_map/ppermute | solution.py:594
  71.2 1.9 %collective-permute-start.7 = (f32[96,128]{1,0:T(8,128)S(1)}, f32[96,128]{1,0:T(8,128)S(1)}, u32[]{:S(2)}, u32[]{:S(2)}) collective-permute-start(f32[96,128]{1,0:T(8,128)S(1)} %get-tuple-element.57), channel_id=1, source_target_pairs={{16,0},{32,16},{48,32},{64,48},{80,64},{96,80},{112,96},{17,1},{33... | collective-permute-start | bytes 147464 | tf_op jit(solution)/shard_map/ppermute | solution.py:594
  73.1 0.0 collective-permute-done.6.mid_p
  73.2 2.9 %collective-permute-done.7.mid_n = f32[96,128]{1,0:T(8,128)S(1)} collective-permute-done((f32[96,128]{1,0:T(8,128)S(1)}, f32[96,128]{1,0:T(8,128)S(1)}, u32[]{:S(2)}, u32[]{:S(2)}) %collective-permute-start.7) | collective-permute-done | bytes 49184 | tf_op jit(solution)/shard_map/ppermute | solution.py:594
  76.0 2.5 %second.1 = (f32[8,16,128]{2,1,0:T(8,128)}, f32[16,128]{1,0:T(8,128)S(1)}) custom-call(f32[16,8,128]{2,1,0:T(8,128)S(1)} %get-tuple-element.55.mid, f32[96,128]{1,0:T(8,128)S(1)} %collective-permute-done.6.mid_p, f32[96,128]{1,0:T(8,128)S(1)} %collective-permute-done.7.mid_n, f32[16,24,128]{2,1,0:T(8,128)S(1)} %get-tuple-element.54.mid_rhs, ...), custom_call_target="tpu_custom_call" | custom-call | tf_op jit(solution)/shard_map/second/pallas_call | solution.py:665
  78.6 11.0 %all_to_all.18 = f32[16,1,128]{2,1,0:T(1,128)S(1)} all-to-all(f32[16,1,128]{2,1,0:T(1,128)S(1)} %bitcast.9), channel_id=1, replica_groups=mesh['gx'=4,'gy'=8,'gz'=16] {'gz'}, dimensions={0} | all-to-all | bytes 16384 | tf_op jit(solution)/shard_map/all_to_all | solution.py:675
  89.6 0.5 slice_reduce_fusion
  (1 shorter events, 0.0 us)
Async XLA Ops:
  0.6 19.7 %copy-start = (f32[8,16,128]{2,1,0:T(8,128)S(1)}, f32[8,16,128]{2,1,0:T(8,128)}, u32[]{:S(2)}) copy-start(f32[8,16,128]{2,1,0:T(8,128)} %state.3) | copy-start | bytes 196612
  2.0 4.0 %collective-permute-start = (f32[8,16,128]{2,1,0:T(8,128)S(1)}, f32[8,16,128]{2,1,0:T(8,128)S(1)}, u32[]{:S(2)}, u32[]{:S(2)}) collective-permute-start(f32[8,16,128]{2,1,0:T(8,128)S(1)} %get-tuple-element.36), channel_id=1, source_target_pairs={{0,1},{1,2},{2,3},{3,4},{4,5},{5,6},{6,7},{7,8},{8,9},{9,10},{10,1... | collective-permute-start | bytes 196616 | tf_op jit(solution)/shard_map/ppermute | solution.py:616
  4.6 3.7 %collective-permute-start.1 = (f32[8,16,128]{2,1,0:T(8,128)S(1)}, f32[8,16,128]{2,1,0:T(8,128)S(1)}, u32[]{:S(2)}, u32[]{:S(2)}) collective-permute-start(f32[8,16,128]{2,1,0:T(8,128)S(1)} %get-tuple-element.37), channel_id=1, source_target_pairs={{0,15},{1,0},{2,1},{3,2},{4,3},{5,4},{6,5},{7,6},{8,7},{9,8},{10,9... | collective-permute-start | bytes 196616 | tf_op jit(solution)/shard_map/ppermute | solution.py:617
  20.5 11.5 %collective-permute-start.2 = (f32[440,128]{1,0:T(8,128)S(1)}, f32[440,128]{1,0:T(8,128)S(1)}, u32[]{:S(2)}, u32[]{:S(2)}) collective-permute-start(f32[440,128]{1,0:T(8,128)S(1)} %get-tuple-element.38), channel_id=1, source_target_pairs={{0,16},{16,32},{32,48},{48,64},{64,80},{80,96},{96,112},{1,17},{17... | collective-permute-start | bytes 675848 | tf_op jit(solution)/shard_map/ppermute | solution.py:594
  23.7 8.3 %collective-permute-start.3 = (f32[440,128]{1,0:T(8,128)S(1)}, f32[440,128]{1,0:T(8,128)S(1)}, u32[]{:S(2)}, u32[]{:S(2)}) collective-permute-start(f32[440,128]{1,0:T(8,128)S(1)} %get-tuple-element.39), channel_id=1, source_target_pairs={{16,0},{32,16},{48,32},{64,48},{80,64},{96,80},{112,96},{17,1},{33... | collective-permute-start | bytes 675848 | tf_op jit(solution)/shard_map/ppermute | solution.py:594
  25.8 9.7 %collective-permute-start.4 = (f32[392,128]{1,0:T(8,128)S(1)}, f32[392,128]{1,0:T(8,128)S(1)}, u32[]{:S(2)}, u32[]{:S(2)}) collective-permute-start(f32[392,128]{1,0:T(8,128)S(1)} %get-tuple-element.40), channel_id=1, source_target_pairs={{0,16},{16,32},{32,48},{48,64},{64,80},{80,96},{96,112},{1,17},{17... | collective-permute-start | bytes 602120 | tf_op jit(solution)/shard_map/ppermute | solution.py:594
  30.1 8.8 %collective-permute-start.5 = (f32[392,128]{1,0:T(8,128)S(1)}, f32[392,128]{1,0:T(8,128)S(1)}, u32[]{:S(2)}, u32[]{:S(2)}) collective-permute-start(f32[392,128]{1,0:T(8,128)S(1)} %get-tuple-element.41), channel_id=1, source_target_pairs={{16,0},{32,16},{48,32},{64,48},{80,64},{96,80},{112,96},{17,1},{33... | collective-permute-start | bytes 602120 | tf_op jit(solution)/shard_map/ppermute | solution.py:594
  66.4 6.8 %collective-permute-start.6 = (f32[96,128]{1,0:T(8,128)S(1)}, f32[96,128]{1,0:T(8,128)S(1)}, u32[]{:S(2)}, u32[]{:S(2)}) collective-permute-start(f32[96,128]{1,0:T(8,128)S(1)} %get-tuple-element.56), channel_id=1, source_target_pairs={{0,16},{16,32},{32,48},{48,64},{64,80},{80,96},{96,112},{1,17},{17... | collective-permute-start | bytes 147464 | tf_op jit(solution)/shard_map/ppermute | solution.py:594
  71.2 4.8 %collective-permute-start.7 = (f32[96,128]{1,0:T(8,128)S(1)}, f32[96,128]{1,0:T(8,128)S(1)}, u32[]{:S(2)}, u32[]{:S(2)}) collective-permute-start(f32[96,128]{1,0:T(8,128)S(1)} %get-tuple-element.57), channel_id=1, source_target_pairs={{16,0},{32,16},{48,32},{64,48},{80,64},{96,80},{112,96},{17,1},{33... | collective-permute-start | bytes 147464 | tf_op jit(solution)/shard_map/ppermute | solution.py:594

commit v8 on v7

--- a/solution.py
+++ b/solution.py
@@ -237,7 +237,7 @@
             out[w] = jnp.where(inside, ref[at, 8:32], 0.0)
         return carry
 
-    lax.fori_loop(0, planes, keep, 0, unroll=4)
+    lax.fori_loop(0, planes, keep, 0, unroll=8)
 
 
 def fold_y():

time: 90.5 us -> 90.5 us (level)
  no operation moved by 1% of the time
where the time goes in v8:
time: 90.5 us; the launch traced here: 90.1 us
  blocking collectives  43.6 us (48%)
  starting transfers between devices  20.9 us (23%)
  Pallas kernels  14.4 us (16%)
  waiting for transfers between devices  9.96 us (11%)
    all_to_all x1, blocking collectives, per_device(): rec = lax.all_to_all(ends, 'gz', 0, 0, tiled=True)  20.6 us
    ppermute x6, starting transfers between devices, both_ways(): return (lax.ppermute(up, axis, higher), lax.ppermute(down, axis, lower))  18.2 us
    all_gather x1, blocking collectives, per_device(): g = lax.all_gather(mine, 'gx')  12 us
    all_to_all x1, blocking collectives, per_device(): sums = lax.all_to_all(grad, 'gz', 0, 0, tiled=True)  11 us
    ppermute x6, waiting for transfers between devices, both_ways(): return (lax.ppermute(up, axis, higher), lax.ppermute(down, axis, lower))  6.27 us
    pallas_call x1, Pallas kernels, per_device(): pl.pallas_call(first_kernel, out_shape=(f32(*win), f32(*win), f32(CX + 2,...  6.21 us
    pallas_call x1, Pallas kernels, per_device(): pl.pallas_call(coef_kernel, out_shape=(f32(*fine1), f32(*fine), f32(*fine...  3.43 us
    ppermute x1, starting transfers between devices, per_device(): lax.ppermute(up, 'gz', [(i, (i + 1) % count) for i in range(count)])  2.67 us
  transfers between devices with their start and end apart: 8, of which 4 were waited for; matrix products, arithmetic and copies ran while one was open for 0% of the time, Pallas kernels for 4%

profile of v8, /device:TPU:19, one launch (start us, length us, event | category | flops | bytes accessed | tf_op | source)
XLA Modules:
  0.0 90.1 jit_solution(3359557343643111452)
XLA Ops:
  0.6 0.0 copy-start
  0.6 1.3 %pack_z.1 = (f32[26,16,128]{2,1,0:T(8,128)S(1)}, f32[8,16,128]{2,1,0:T(8,128)S(1)}, f32[8,16,128]{2,1,0:T(8,128)S(1)}) custom-call(s32[1,1,16]{2,1,0:T(1,128)} %line_far.1, f32[8,16,128]{2,1,0:T(8,128)} %src_far.1, f32[8,16,128]{2,1,0:T(8,128)} %log_coef_far.1, f32[8,16]{1,0:T(8,128)} %lateral_far.1, f32[8,16,128]{2,1,0:T(8,128)} %state.3), custom_call_target="tpu_custom_call" | custom-call | tf_op jit(solution)/shard_map/pack_z/pallas_call | solution.py:600
  2.0 2.7 %collective-permute-start = (f32[8,16,128]{2,1,0:T(8,128)S(1)}, f32[8,16,128]{2,1,0:T(8,128)S(1)}, u32[]{:S(2)}, u32[]{:S(2)}) collective-permute-start(f32[8,16,128]{2,1,0:T(8,128)S(1)} %get-tuple-element.36), channel_id=1, source_target_pairs={{0,1},{1,2},{2,3},{3,4},{4,5},{5,6},{6,7},{7,8},{8,9},{9,10},{10,1... | collective-permute-start | bytes 196616 | tf_op jit(solution)/shard_map/ppermute | solution.py:616
  4.6 0.0 collective-permute-start.1
  4.6 1.3 %collective-permute-done = f32[8,16,128]{2,1,0:T(8,128)S(1)} collective-permute-done((f32[8,16,128]{2,1,0:T(8,128)S(1)}, f32[8,16,128]{2,1,0:T(8,128)S(1)}, u32[]{:S(2)}, u32[]{:S(2)}) %collective-permute-start) | collective-permute-done | bytes 65568 | tf_op jit(solution)/shard_map/ppermute | solution.py:616
  6.0 2.4 %collective-permute-done.1 = f32[8,16,128]{2,1,0:T(8,128)S(1)} collective-permute-done((f32[8,16,128]{2,1,0:T(8,128)S(1)}, f32[8,16,128]{2,1,0:T(8,128)S(1)}, u32[]{:S(2)}, u32[]{:S(2)}) %collective-permute-start.1) | collective-permute-done | bytes 65568 | tf_op jit(solution)/shard_map/ppermute | solution.py:617
  8.3 12.0 %all_gather.10.g = f32[4,26,16,128]{3,2,1,0:T(8,128)S(1)} all-gather(f32[1,26,16,128]{3,2,1,0:T(8,128)S(1)} %bitcast_dynamic-update-slice_fusion), channel_id=1, replica_groups=mesh['gx'=4,'gy'=8,'gz'=16] {'gx'}, dimensions={0}, use_global_device_ids=true | all-gather | bytes 1064960 | tf_op jit(solution)/shard_map/all_gather | solution.py:620
  20.3 0.0 copy-done
  20.3 0.2 pack_y.1
  20.5 3.2 %collective-permute-start.2 = (f32[440,128]{1,0:T(8,128)S(1)}, f32[440,128]{1,0:T(8,128)S(1)}, u32[]{:S(2)}, u32[]{:S(2)}) collective-permute-start(f32[440,128]{1,0:T(8,128)S(1)} %get-tuple-element.38), channel_id=1, source_target_pairs={{0,16},{16,32},{32,48},{48,64},{64,80},{80,96},{96,112},{1,17},{17... | collective-permute-start | bytes 675848 | tf_op jit(solution)/shard_map/ppermute | solution.py:594
  23.7 2.1 %collective-permute-start.3 = (f32[440,128]{1,0:T(8,128)S(1)}, f32[440,128]{1,0:T(8,128)S(1)}, u32[]{:S(2)}, u32[]{:S(2)}) collective-permute-start(f32[440,128]{1,0:T(8,128)S(1)} %get-tuple-element.39), channel_id=1, source_target_pairs={{16,0},{32,16},{48,32},{64,48},{80,64},{96,80},{112,96},{17,1},{33... | collective-permute-start | bytes 675848 | tf_op jit(solution)/shard_map/ppermute | solution.py:594
  25.8 4.3 %collective-permute-start.4 = (f32[392,128]{1,0:T(8,128)S(1)}, f32[392,128]{1,0:T(8,128)S(1)}, u32[]{:S(2)}, u32[]{:S(2)}) collective-permute-start(f32[392,128]{1,0:T(8,128)S(1)} %get-tuple-element.40), channel_id=1, source_target_pairs={{0,16},{16,32},{32,48},{48,64},{64,80},{80,96},{96,112},{1,17},{17... | collective-permute-start | bytes 602120 | tf_op jit(solution)/shard_map/ppermute | solution.py:594
  30.1 1.9 %collective-permute-start.5 = (f32[392,128]{1,0:T(8,128)S(1)}, f32[392,128]{1,0:T(8,128)S(1)}, u32[]{:S(2)}, u32[]{:S(2)}) collective-permute-start(f32[392,128]{1,0:T(8,128)S(1)} %get-tuple-element.41), channel_id=1, source_target_pairs={{16,0},{32,16},{48,32},{64,48},{80,64},{96,80},{112,96},{17,1},{33... | collective-permute-start | bytes 602120 | tf_op jit(solution)/shard_map/ppermute | solution.py:594
  32.0 0.0 collective-permute-done.2.yp.cp
  32.0 0.0 collective-permute-done.3.yn.cn
  32.0 3.4 %coef.1 = (f32[33,40,256]{2,1,0:T(8,128)S(1)}, f32[32,40,256]{2,1,0:T(8,128)S(1)}, f32[32,40,256]{2,1,0:T(8,128)S(1)}, f32[32,40,256]{2,1,0:T(8,128)S(1)}, f32[1...) custom-call(f32[4,26,16,128]{3,2,1,0:T(8,128)S(1)} %all_gather.10.g,, ...), custom_call_target="tpu_custom_call" | custom-call | tf_op jit(solution)/shard_map/coef/pallas_call | solution.py:633
  35.5 0.0 collective-permute-done.4.yp
  35.5 3.4 %collective-permute-done.5.yn = f32[392,128]{1,0:T(8,128)S(1)} collective-permute-done((f32[392,128]{1,0:T(8,128)S(1)}, f32[392,128]{1,0:T(8,128)S(1)}, u32[]{:S(2)}, u32[]{:S(2)}) %collective-permute-start.5) | collective-permute-done | bytes 200736 | tf_op jit(solution)/shard_map/ppermute | solution.py:594
  38.8 6.2 %first.1 = (f32[16,24,256]{2,1,0:T(8,128)S(1)}, f32[16,24,256]{2,1,0:T(8,128)S(1)}, f32[10,24,256]{2,1,0:T(8,128)S(1)}, f32[16,8,128]{2,1,0:T(8,128)S(1)}, f32[1...) custom-call(f32[4,26,16,128]{3,2,1,0:T(8,128)S(1)} %all_gather.10.g, ...), custom_call_target="tpu_custom_call" | custom-call | tf_op jit(solution)/shard_map/first/pallas_call | solution.py:644
  45.1 20.6 %all_to_all.17.rec = f32[16,8,128]{2,1,0:T(8,128)S(1)} all-to-all(f32[16,8,128]{2,1,0:T(8,128)S(1)} %get-tuple-element.51), channel_id=1, replica_groups=mesh['gx'=4,'gy'=8,'gz'=16] {'gz'}, dimensions={0} | all-to-all | bytes 131072 | tf_op jit(solution)/shard_map/all_to_all | solution.py:657
  65.7 0.7 solve.1
  66.3 4.9 %collective-permute-start.6 = (f32[96,128]{1,0:T(8,128)S(1)}, f32[96,128]{1,0:T(8,128)S(1)}, u32[]{:S(2)}, u32[]{:S(2)}) collective-permute-start(f32[96,128]{1,0:T(8,128)S(1)} %get-tuple-element.56), channel_id=1, source_target_pairs={{0,16},{16,32},{32,48},{48,64},{64,80},{80,96},{96,112},{1,17},{17... | collective-permute-start | bytes 147464 | tf_op jit(solution)/shard_map/ppermute | solution.py:594
  71.2 1.9 %collective-permute-start.7 = (f32[96,128]{1,0:T(8,128)S(1)}, f32[96,128]{1,0:T(8,128)S(1)}, u32[]{:S(2)}, u32[]{:S(2)}) collective-permute-start(f32[96,128]{1,0:T(8,128)S(1)} %get-tuple-element.57), channel_id=1, source_target_pairs={{16,0},{32,16},{48,32},{64,48},{80,64},{96,80},{112,96},{17,1},{33... | collective-permute-start | bytes 147464 | tf_op jit(solution)/shard_map/ppermute | solution.py:594
  73.1 0.0 collective-permute-done.6.mid_p
  73.1 2.9 %collective-permute-done.7.mid_n = f32[96,128]{1,0:T(8,128)S(1)} collective-permute-done((f32[96,128]{1,0:T(8,128)S(1)}, f32[96,128]{1,0:T(8,128)S(1)}, u32[]{:S(2)}, u32[]{:S(2)}) %collective-permute-start.7) | collective-permute-done | bytes 49184 | tf_op jit(solution)/shard_map/ppermute | solution.py:594
  76.0 2.5 %second.1 = (f32[8,16,128]{2,1,0:T(8,128)}, f32[16,128]{1,0:T(8,128)S(1)}) custom-call(f32[16,8,128]{2,1,0:T(8,128)S(1)} %get-tuple-element.55.mid, f32[96,128]{1,0:T(8,128)S(1)} %collective-permute-done.6.mid_p, f32[96,128]{1,0:T(8,128)S(1)} %collective-permute-done.7.mid_n, f32[16,24,128]{2,1,0:T(8,128)S(1)} %get-tuple-element.54.mid_rhs, ...), custom_call_target="tpu_custom_call" | custom-call | tf_op jit(solution)/shard_map/second/pallas_call | solution.py:665
  78.6 11.0 %all_to_all.18 = f32[16,1,128]{2,1,0:T(1,128)S(1)} all-to-all(f32[16,1,128]{2,1,0:T(1,128)S(1)} %bitcast.9), channel_id=1, replica_groups=mesh['gx'=4,'gy'=8,'gz'=16] {'gz'}, dimensions={0} | all-to-all | bytes 16384 | tf_op jit(solution)/shard_map/all_to_all | solution.py:675
  89.6 0.5 slice_reduce_fusion
  (1 shorter events, 0.0 us)
Async XLA Ops:
  0.6 19.7 %copy-start = (f32[8,16,128]{2,1,0:T(8,128)S(1)}, f32[8,16,128]{2,1,0:T(8,128)}, u32[]{:S(2)}) copy-start(f32[8,16,128]{2,1,0:T(8,128)} %state.3) | copy-start | bytes 196612
  2.0 4.0 %collective-permute-start = (f32[8,16,128]{2,1,0:T(8,128)S(1)}, f32[8,16,128]{2,1,0:T(8,128)S(1)}, u32[]{:S(2)}, u32[]{:S(2)}) collective-permute-start(f32[8,16,128]{2,1,0:T(8,128)S(1)} %get-tuple-element.36), channel_id=1, source_target_pairs={{0,1},{1,2},{2,3},{3,4},{4,5},{5,6},{6,7},{7,8},{8,9},{9,10},{10,1... | collective-permute-start | bytes 196616 | tf_op jit(solution)/shard_map/ppermute | solution.py:616
  4.6 3.7 %collective-permute-start.1 = (f32[8,16,128]{2,1,0:T(8,128)S(1)}, f32[8,16,128]{2,1,0:T(8,128)S(1)}, u32[]{:S(2)}, u32[]{:S(2)}) collective-permute-start(f32[8,16,128]{2,1,0:T(8,128)S(1)} %get-tuple-element.37), channel_id=1, source_target_pairs={{0,15},{1,0},{2,1},{3,2},{4,3},{5,4},{6,5},{7,6},{8,7},{9,8},{10,9... | collective-permute-start | bytes 196616 | tf_op jit(solution)/shard_map/ppermute | solution.py:617
  20.5 11.5 %collective-permute-start.2 = (f32[440,128]{1,0:T(8,128)S(1)}, f32[440,128]{1,0:T(8,128)S(1)}, u32[]{:S(2)}, u32[]{:S(2)}) collective-permute-start(f32[440,128]{1,0:T(8,128)S(1)} %get-tuple-element.38), channel_id=1, source_target_pairs={{0,16},{16,32},{32,48},{48,64},{64,80},{80,96},{96,112},{1,17},{17... | collective-permute-start | bytes 675848 | tf_op jit(solution)/shard_map/ppermute | solution.py:594
  23.7 8.3 %collective-permute-start.3 = (f32[440,128]{1,0:T(8,128)S(1)}, f32[440,128]{1,0:T(8,128)S(1)}, u32[]{:S(2)}, u32[]{:S(2)}) collective-permute-start(f32[440,128]{1,0:T(8,128)S(1)} %get-tuple-element.39), channel_id=1, source_target_pairs={{16,0},{32,16},{48,32},{64,48},{80,64},{96,80},{112,96},{17,1},{33... | collective-permute-start | bytes 675848 | tf_op jit(solution)/shard_map/ppermute | solution.py:594
  25.8 9.7 %collective-permute-start.4 = (f32[392,128]{1,0:T(8,128)S(1)}, f32[392,128]{1,0:T(8,128)S(1)}, u32[]{:S(2)}, u32[]{:S(2)}) collective-permute-start(f32[392,128]{1,0:T(8,128)S(1)} %get-tuple-element.40), channel_id=1, source_target_pairs={{0,16},{16,32},{32,48},{48,64},{64,80},{80,96},{96,112},{1,17},{17... | collective-permute-start | bytes 602120 | tf_op jit(solution)/shard_map/ppermute | solution.py:594
  30.1 8.8 %collective-permute-start.5 = (f32[392,128]{1,0:T(8,128)S(1)}, f32[392,128]{1,0:T(8,128)S(1)}, u32[]{:S(2)}, u32[]{:S(2)}) collective-permute-start(f32[392,128]{1,0:T(8,128)S(1)} %get-tuple-element.41), channel_id=1, source_target_pairs={{16,0},{32,16},{48,32},{64,48},{80,64},{96,80},{112,96},{17,1},{33... | collective-permute-start | bytes 602120 | tf_op jit(solution)/shard_map/ppermute | solution.py:594
  66.3 6.8 %collective-permute-start.6 = (f32[96,128]{1,0:T(8,128)S(1)}, f32[96,128]{1,0:T(8,128)S(1)}, u32[]{:S(2)}, u32[]{:S(2)}) collective-permute-start(f32[96,128]{1,0:T(8,128)S(1)} %get-tuple-element.56), channel_id=1, source_target_pairs={{0,16},{16,32},{32,48},{48,64},{64,80},{80,96},{96,112},{1,17},{17... | collective-permute-start | bytes 147464 | tf_op jit(solution)/shard_map/ppermute | solution.py:594
  71.2 4.8 %collective-permute-start.7 = (f32[96,128]{1,0:T(8,128)S(1)}, f32[96,128]{1,0:T(8,128)S(1)}, u32[]{:S(2)}, u32[]{:S(2)}) collective-permute-start(f32[96,128]{1,0:T(8,128)S(1)} %get-tuple-element.57), channel_id=1, source_target_pairs={{16,0},{32,16},{48,32},{64,48},{80,64},{96,80},{112,96},{17,1},{33... | collective-permute-start | bytes 147464 | tf_op jit(solution)/shard_map/ppermute | solution.py:594
